TPU v7x, 128 devices: a whole 4x4x4 slice. The times are simulated.
128 devices in a mesh: seq: 64 (over z, y_hi, x, core), branch: 2 (over y_lo).
Axes of the slice: x: 4, y: 4 (y_hi: 2, y_lo: 2; y = y_hi * 2 + y_lo), z: 4, core: 2. Of those that a mesh axis runs over, the one named last changes fastest.
Arguments:
- queries: bfloat16 [2, 3584, 2560], P('branch', 'seq'), may hold values from -100 to 100
- keys_values: bfloat16 [2, 3584, 2560], P(None, 'seq', 'branch'), may hold values from -10 to 10
- residual_in: bfloat16 [2, 3584, 2560], P('branch', 'seq'), may hold values from -90 to 90
- cross_gain: bfloat16 [2560], replicated, may hold values from 0.099609375 to 1.8984375
- text_kv: bfloat16 [2, 2, 512, 2560], replicated, may hold values from -90 to 90
- prompt_ids: int32 [2, 512], replicated, may hold values from 0 to 256383
- word_align: int32 [512], replicated, may hold values from 0 to 511, as said below
Outputs:
- attended: bfloat16 [2, 3584, 2560], P('branch', 'seq')
- result: bfloat16 [2, 3584, 2560], P('branch', 'seq')
Inputs may be any that keep to these rules, and one draw needn't show every extreme that they name: `word_align`: a permutation of the 512 source positions.
All inputs are finite; a program needn't handle non-finite values.
Results may differ from a plain program's by a relative error of at most 0.019.
Values may be sent and summed in bfloat16 or wider, within the bound.
No kernel may reach another device: no remote copies, remote signals or barrier semaphores. Data moves between devices by JAX's collectives and lax.ppermute only.
A program may use at most 128 MiB of HBM per device.

v0:
```python
import functools
import math

import jax
import jax.numpy as jnp
from jax import lax
from jax.experimental import pallas as pl
from jax.experimental.pallas import tpu as pltpu
from jax.sharding import Mesh, PartitionSpec as P


HD = 128
NQ = 5
TOK = 56
ROWS = 4 * TOK
KEYS = 2 * TOK
TXT = 512
GROUPS = ((0, 3, "x", "z"), (3, 2, "z", "x"))
STAT = 32
SCALE = 1.0 / math.sqrt(HD)
LOG2E = 1.4426950408889634
PLANE = ("yh", "yl")
BF = jnp.bfloat16
F32 = jnp.float32


def shift(value, axis, distance, size):
    return lax.ppermute(value, axis, [(i, (i + distance) % size) for i in range(size)])


def dot_t(left, right):
    return lax.dot_general(left, right, (((1,), (1,)), ((), ())), preferred_element_type=F32)


def first_head(plane):
    return 10 * (plane % 2) + 5 * (plane // 2)


def vmem(count):
    return [pl.BlockSpec(memory_space=pltpu.VMEM) for _ in range(count)]


def call(kernel, out_shapes, scalars, operands, kept=(), scratch=(), flops=0, exps=0, limit=40):
    in_specs = [pl.BlockSpec(memory_space=pltpu.SMEM)] * len(scalars) + vmem(len(operands))
    in_specs += [pl.BlockSpec(memory_space=space) for _, space in kept]
    moved = sum(math.prod(o.shape) * o.dtype.itemsize for o in operands)
    moved += sum(math.prod(o.shape) * o.dtype.itemsize for o in out_shapes)
    return pl.pallas_call(
        kernel,
        out_shape=out_shapes,
        in_specs=in_specs,
        out_specs=vmem(len(out_shapes)),
        scratch_shapes=list(scratch),
        cost_estimate=pl.CostEstimate(flops=flops, bytes_accessed=moved, transcendentals=exps),
        compiler_params=pltpu.CompilerParams(vmem_limit_bytes=limit << 20),
    )(*scalars, *operands, *(array for array, _ in kept))


def shaped(shape, dtype=BF):
    return jax.ShapeDtypeStruct(shape, dtype)


def stacked(parts):
    return jnp.concatenate([part.astype(F32) for part in parts], axis=0).astype(BF)


def split_kernel(plane_ref, rows_ref, kv_ref, kept, first, last, across, own):
    high = plane_ref[0] // 2
    outs = (own, first, across, last)
    for distance in range(4):
        plane = lax.rem(plane_ref[0] + distance, 4)
        for head in range(NQ):
            lane = pl.multiple_of((first_head(plane) + head) * HD, HD)
            outs[distance][head] = rows_ref[:, pl.ds(lane, HD)]
    for head in range(NQ):
        here = pl.multiple_of((high * NQ + head) * HD, HD)
        there = pl.multiple_of(((1 - high) * NQ + head) * HD, HD)
        for which in range(2):
            kept[2 * head + which] = kv_ref[which, :, pl.ds(here, HD)]
            across[NQ + 2 * head + which] = kv_ref[which, :, pl.ds(there, HD)]


def split_rows_kernel(plane_ref, rows_ref, *outs):
    for distance in range(4):
        plane = lax.rem(plane_ref[0] + distance, 4)
        for head in range(NQ):
            lane = pl.multiple_of((first_head(plane) + head) * HD, HD)
            outs[distance][head] = rows_ref[:, pl.ds(lane, HD)]


def pack_kernel(kept, own, first, across, last, *outs):
    queries = (own, first, across, last)
    for group, (low, count, _, _) in enumerate(GROUPS):
        rows, keys = outs[2 * group], outs[2 * group + 1]
        for index in range(count):
            head = low + index
            rows[index * ROWS : (index + 1) * ROWS, :] = stacked([query[head] for query in queries])
            keys[index * ROWS : (index + 1) * ROWS, :] = stacked(
                [kept[2 * head], across[NQ + 2 * head], kept[2 * head + 1], across[NQ + 2 * head + 1]]
            )


def repack_kernel(*refs):
    out = refs[4]
    size = refs[0].shape[0]
    for index in range(4):
        out[index * size : (index + 1) * size, :] = refs[index][...]


def join_rows_kernel(plane_ref, *refs):
    pieces, out = refs[:-1], refs[-1]
    for distance in range(4):
        plane = lax.rem(plane_ref[0] + distance, 4)
        for head in range(NQ):
            lane = pl.multiple_of((first_head(plane) + head) * HD, HD)
            out[:, pl.ds(lane, HD)] = pieces[distance][head]


def attend_kernel(count, *refs):
    rows_of, keys_of, swapped = refs[:4], refs[4:8], refs[8]
    outs, (keys, values, stats) = refs[9:13], refs[13:]
    size = count * ROWS
    pieces = [(ref, 0) for ref in keys_of] + [(swapped, index * size) for index in range(4)]
    lanes = lax.broadcasted_iota(jnp.int32, (ROWS, HD), 1)
    stats[...] = jnp.zeros_like(stats)

    def one_head(head, _):
        for index, (piece, base) in enumerate(pieces):
            start = pl.multiple_of(base + head * ROWS, 16)
            keys[pl.ds(index * KEYS, KEYS), :] = piece[pl.ds(start, KEYS), :]
            values[pl.ds(index * KEYS, KEYS), :] = piece[
                pl.ds(pl.multiple_of(start + KEYS, 16), KEYS), :
            ]
        for index in range(4):
            start = pl.multiple_of(head * ROWS, 16)
            scores = dot_t(rows_of[index][pl.ds(start, ROWS), :], keys[...])
            peak = jnp.max(scores, axis=1, keepdims=True)
            weights = jnp.exp2(scores * (SCALE * LOG2E) - peak * (SCALE * LOG2E))
            total = jnp.sum(weights, axis=1, keepdims=True)
            summed = jnp.dot(weights.astype(BF), values[...], preferred_element_type=F32)
            outs[index][pl.ds(pl.multiple_of(head * ROWS, 16), ROWS), :] = (summed / total).astype(BF)
            level = peak * SCALE + jnp.log(total)
            coarse = level.astype(BF).astype(F32)
            middle = (level - coarse).astype(BF).astype(F32)
            fine = level - coarse - middle
            old = stats[index, 0:ROWS, :]
            old = jnp.where(lanes == 3 * head, coarse, old)
            old = jnp.where(lanes == 3 * head + 1, middle, old)
            stats[index, 0:ROWS, :] = jnp.where(lanes == 3 * head + 2, fine, old)
        return 0

    lax.fori_loop(0, count, one_head, 0)
    for index in range(4):
        turned = stats[index].T
        outs[index][size : size + 16, :] = turned[0:16, 0:HD].astype(BF)
        outs[index][size + 16 : size + STAT, :] = turned[0:16, HD : 2 * HD].astype(BF)


def attend(group, rows, keys, swapped):
    _, count, _, _ = GROUPS[group]
    return call(
        functools.partial(attend_kernel, count),
        [shaped((count * ROWS + STAT, HD))] * 4,
        [],
        [*rows, *keys, swapped],
        scratch=[
            pltpu.VMEM((8 * KEYS, HD), BF),
            pltpu.VMEM((8 * KEYS, HD), BF),
            pltpu.VMEM((4, 2 * HD, HD), F32),
        ],
        flops=4 * count * 4 * ROWS * 8 * KEYS * HD,
        exps=count * 4 * ROWS * 8 * KEYS,
    )


def combine_kernel(*refs):
    partials = (refs[:4], refs[4:8])
    residuals, attended = refs[8:12], refs[13:17]
    middle_ref, turn_ref = refs[17:]
    turn_ref[...] = jnp.zeros_like(turn_ref)
    squares = jnp.zeros((ROWS, HD), F32)
    for group, (low, count, _, _) in enumerate(GROUPS):
        size = count * ROWS
        levels = []
        for partial in partials[group]:
            turn_ref[0:16, 0:HD] = partial[size : size + 16, :].astype(F32)
            turn_ref[0:16, HD : 2 * HD] = partial[size + 16 : size + STAT, :].astype(F32)
            stat = turn_ref[...].T[0:ROWS, :]
            levels.append(stat + pltpu.roll(stat, HD - 1, 1) + pltpu.roll(stat, HD - 2, 1))
        peak = functools.reduce(jnp.maximum, levels)
        shares = [jnp.exp(level - peak) for level in levels]
        inverse = 1.0 / sum(shares)
        shares = [share * inverse for share in shares]
        for index in range(count):
            head = low + index
            total = sum(
                partial[index * ROWS : (index + 1) * ROWS, :].astype(F32)
                * share[:, 3 * index : 3 * index + 1]
                for partial, share in zip(partials[group], shares)
            )
            middles = []
            for block in range(4):
                part = total[block * TOK : (block + 1) * TOK].astype(BF)
                attended[block][head] = part
                middle = residuals[block][head].astype(F32) + part.astype(F32)
                middle_ref[head, block] = middle
                middles.append(middle)
            rows = jnp.concatenate(middles, axis=0)
            squares = squares + rows * rows
    sums = jnp.sum(squares, axis=1, keepdims=True)
    lanes = lax.broadcasted_iota(jnp.int32, (TOK, HD), 1)
    packed = jnp.zeros((TOK, HD), F32)
    for block in range(4):
        column = sums[block * TOK : (block + 1) * TOK]
        coarse = column.astype(BF).astype(F32)
        middle = (column - coarse).astype(BF).astype(F32)
        packed = jnp.where(lanes == block, coarse, packed)
        packed = jnp.where(lanes == block + 32, middle, packed)
        packed = jnp.where(lanes == block + 64, column - coarse - middle, packed)
    for block in range(4):
        attended[block][NQ] = packed.astype(BF)


def digits(ids):
    row = lax.broadcasted_iota(jnp.int32, (16, TXT), 0)
    shifts = jnp.where(row == 0, 0, jnp.where(row == 1, 8, 16))
    value = jnp.bitwise_and(lax.shift_right_logical(jnp.broadcast_to(ids, (16, TXT)), shifts), 255)
    return jnp.where(row < 3, value, 0).astype(F32)


def prompt_kernel(
    info_ref, ids_ref, align_ref, gain_ref, text_ref, after_ref, mixed_ref, own_ref, copy_ref, scale_ref, sem
):
    start = pl.multiple_of(info_ref[0] * (NQ * HD), HD)
    copy = pltpu.make_async_copy(text_ref.at[:, :, :, pl.ds(start, NQ * HD)], copy_ref, sem)
    copy.start()
    pairs = lax.broadcasted_iota(jnp.int32, (TXT, TXT), 0) == align_ref[0:1, :]
    chosen = jnp.where(pairs, 1.0, 0.0)
    aligned = jnp.dot(digits(ids_ref[0:1, :]).astype(BF), chosen.astype(BF), preferred_element_type=F32)
    apart = jnp.sum(jnp.abs(aligned - digits(ids_ref[1:2, :])), axis=0, keepdims=True)
    own = jnp.where(apart == 0.0, 0.0, 1.0)
    own_ref[...] = jnp.broadcast_to(own, (8, TXT))
    selection = (chosen * (1.0 - own)).astype(BF)
    scale_ref[...] = jnp.broadcast_to(gain_ref[0:1, pl.ds(start, NQ * HD)].astype(F32), (8, NQ * HD))
    copy.wait()
    mixed_ref[...] = jnp.dot(selection, copy_ref[1, 1], preferred_element_type=F32).astype(BF)


def prompts(info, prompt_ids, word_align, gain, text_kv, after):
    return call(
        prompt_kernel,
        [
            shaped((TXT, NQ * HD)),
            shaped((8, TXT), F32),
            shaped((2, 2, TXT, NQ * HD)),
            shaped((8, NQ * HD), F32),
        ],
        [info],
        [prompt_ids, word_align.reshape(1, TXT), gain.reshape(1, -1)],
        kept=[(text_kv, pltpu.HBM), (after, pl.ANY)],
        scratch=[pltpu.SemaphoreType.DMA],
        flops=2 * TXT * TXT * NQ * HD,
        limit=47,
    )


def pairs_of(info_ref):
    odd = lax.rem(info_ref[1], 2)
    return ((odd, 3 * (1 - odd)), (2 + odd, 1 + odd))


def scores_kernel(info_ref, middle_ref, gain_ref, text_ref, out_ref):
    pairs = pairs_of(info_ref)
    for head in range(NQ):
        columns = slice(head * HD, (head + 1) * HD)
        gain = gain_ref[0:1, columns]
        for side in range(2):
            rows = jnp.concatenate([middle_ref[head, pair[side]] for pair in pairs], axis=0)
            out_ref[side, head] = dot_t((rows * gain).astype(BF), text_ref[0, side, :, columns])


def cross_kernel(info_ref, s0, s1, s2, s3, middle_ref, scores_ref, text_ref, mixed_ref, own_ref, *refs):
    outs, (scale_ref, done_ref) = refs[:4], refs[4:]
    lanes = lax.broadcasted_iota(jnp.int32, (TOK, HD), 1)

    def sums_of(ref):
        packed = ref[NQ].astype(F32)
        return packed + pltpu.roll(packed, HD - 32, 1) + pltpu.roll(packed, HD - 64, 1)

    squares = sums_of(s0)
    for distance, ref in ((1, s1), (2, s2), (3, s3)):
        other = sums_of(ref)
        turned = pltpu.roll(other, HD - distance, 1)
        wrapped = pltpu.roll(other, 4 - distance, 1)
        squares = squares + jnp.where(lanes < 4 - distance, turned, wrapped)
    norm = lax.rsqrt(squares * (1.0 / (4 * NQ * HD)) + 1e-06) * (SCALE * LOG2E)
    for block in range(4):
        scale_ref[block] = jnp.broadcast_to(norm[:, block : block + 1], (TOK, HD))
    pairs = pairs_of(info_ref)
    own = own_ref[0:1, :]
    norms = [
        jnp.concatenate([scale_ref[pair[side]] for pair in pairs], axis=0)[:, 0:1] for side in range(2)
    ]

    def softmax(side, head):
        scores = scores_ref[side, head] * norms[side]
        weights = jnp.exp2(scores - jnp.max(scores, axis=1, keepdims=True))
        return weights * (1.0 / jnp.sum(weights, axis=1, keepdims=True))

    for head in range(NQ):
        columns = slice(head * HD, (head + 1) * HD)
        source = softmax(0, head).astype(BF)
        edited = (softmax(1, head) * own).astype(BF)
        results = (
            jnp.dot(source, text_ref[1, 0, :, columns], preferred_element_type=F32),
            jnp.dot(source, mixed_ref[:, columns], preferred_element_type=F32)
            + jnp.dot(edited, text_ref[1, 1, :, columns], preferred_element_type=F32),
        )
        for side in range(2):
            for index, pair in enumerate(pairs):
                part = results[side][index * TOK : (index + 1) * TOK]
                done_ref[pair[side]] = middle_ref[head, pair[side]] + part
        for block in range(4):
            outs[block][head] = done_ref[block].astype(BF)


def per_device(queries, keys_values, residual_in, cross_gain, text_kv, prompt_ids, word_align):
    plane = 2 * lax.axis_index("yh") + lax.axis_index("yl")
    quarter = 2 * lax.axis_index("yl") + lax.axis_index("yh")
    where = plane.reshape(1).astype(jnp.int32)
    info = jnp.stack([quarter, plane]).astype(jnp.int32)
    piece = (NQ, TOK, HD)

    kept, first, last, over, mine = call(
        split_kernel,
        [shaped((2 * NQ, TOK, HD)), shaped(piece), shaped(piece), shaped((3 * NQ, TOK, HD)), shaped(piece)],
        [where],
        [queries[0], keys_values],
    )
    over = shift(over, PLANE, 2, 4)
    first = shift(first, PLANE, 1, 4)
    last = shift(last, PLANE, 3, 4)
    residuals = call(split_rows_kernel, [shaped(piece)] * 4, [where], [residual_in[0]])
    residuals = [p if d == 0 else shift(p, PLANE, d, 4) for d, p in enumerate(residuals)]
    buffers = [shaped((count * ROWS, HD)) for _, count, _, _ in GROUPS for _ in range(2)]
    packed = call(pack_kernel, buffers, [], [kept, mine, first, over, last])
    partials, groups = [], []
    for group, (_, count, row_axis, key_axis) in enumerate(GROUPS):
        rows, keys = packed[2 * group], packed[2 * group + 1]
        keys = [keys] + [shift(keys, key_axis, d, 4) for d in (2, 1, 3)]
        rows = [rows] + [shift(rows, row_axis, d, 4) for d in (2, 1, 3)]
        held = call(repack_kernel, [shaped((4 * count * ROWS, HD))], [], keys)[0]
        groups.append((rows, keys, shift(held, "c", 1, 2)))
    for group, (_, _, row_axis, _) in enumerate(GROUPS):
        outs = attend(group, *groups[group])
        partials += [outs[0]] + [shift(outs[i], row_axis, -d, 4) for i, d in ((1, 2), (2, 1), (3, 3))]
    mixed, own, text, gain = prompts(info, prompt_ids, word_align, cross_gain, text_kv, outs[0])
    combined = call(
        combine_kernel,
        [shaped((NQ + 1, TOK, HD))] * 4 + [shaped((NQ, 4, TOK, HD), F32)],
        [],
        [*partials, *residuals],
        kept=[(own, pl.ANY)],
        scratch=[pltpu.VMEM((HD, 2 * HD), F32)],
    )
    middle = combined[4]

    def home(pieces):
        return [p if d == 0 else shift(p, PLANE, -d, 4) for d, p in enumerate(pieces)]

    def join(pieces):
        return call(join_rows_kernel, [shaped((TOK, 4 * NQ * HD))], [where], pieces)[0]

    attended = home(combined[:4])
    scores = call(
        scores_kernel,
        [shaped((2, NQ, KEYS, TXT), F32)],
        [info],
        [middle, gain, text],
        flops=2 * 2 * KEYS * TXT * NQ * HD,
    )[0]
    results = call(
        cross_kernel,
        [shaped(piece)] * 4,
        [info],
        [*attended, middle, scores, text, mixed, own],
        scratch=[pltpu.VMEM((4, TOK, HD), F32), pltpu.VMEM((4, TOK, HD), F32)],
        flops=2 * 3 * KEYS * TXT * NQ * HD,
        exps=2 * KEYS * NQ * TXT,
    )
    results = home(results)
    return (join(attended)[None], join(results)[None])


def solution(mesh):
    grid = Mesh(mesh.devices.reshape(4, 2, 4, 2, 2), ("z", "yh", "x", "c", "yl"))
    seq = ("z", "yh", "x", "c")
    in_specs = (
        P("yl", seq, None),
        P(None, seq, "yl"),
        P("yl", seq, None),
        P(),
        P(),
        P(),
        P(),
    )
    out_specs = (P("yl", seq, None), P("yl", seq, None))
    return jax.shard_map(per_device, mesh=grid, in_specs=in_specs, out_specs=out_specs, check_vma=False)
```

profile of v0, /device:TPU:24, one launch (start us, length us, event | category | flops | bytes accessed | tf_op | source)
XLA Modules:
  0.0 97.4 jit_solution(2263527608357113814)
XLA Ops:
  0.7 1.0 %copy-done.1 = bf16[1,56,2560]{2,1,0:T(8,128)(2,1)S(1)} copy-done((bf16[1,56,2560]{2,1,0:T(8,128)(2,1)S(1)}, bf16[1,56,2560]{2,1,0:T(8,128)(2,1)}, u32[]{:S(2)}) %copy-start.1) | copy-done | bytes 286744
  1.7 1.0 copy-done.2
  2.7 1.3 %collective-permute-start.1 = (bf16[15,56,128]{2,1,0:T(8,128)(2,1)S(1)}, bf16[15,56,128]{2,1,0:T(8,128)(2,1)S(1)}, u32[]{:S(2)}, u32[]{:S(2)}) collective-permute-start(bf16[15,56,128]{2,1,0:T(8,128)(2,1)S(1)} %get-tuple-element.39), channel_id=1, source_target_pairs={{0,16},{1,17},{16,0},{17,1},{2,18},{3,19},{18,2},{19,3},{4,20},{5,... | collective-permute-start | bytes 645128 | tf_op jit(solution)/shard_map/ppermute | solution.py:28
  4.1 2.2 %collective-permute-start = (bf16[5,56,128]{2,1,0:T(8,128)(2,1)S(1)}, bf16[5,56,128]{2,1,0:T(8,128)(2,1)S(1)}, u32[]{:S(2)}, u32[]{:S(2)}) collective-permute-start(bf16[5,56,128]{2,1,0:T(8,128)(2,1)S(1)} %get-tuple-element.38), channel_id=1, source_target_pairs={{0,1},{1,16},{16,17},{17,0},{2,3},{3,18},{18,19},{19,2},{4,5},{5,2... | collective-permute-start | bytes 215048 | tf_op jit(solution)/shard_map/ppermute | solution.py:28
  6.2 4.2 %collective-permute-done.first = bf16[5,56,128]{2,1,0:T(8,128)(2,1)S(1)} collective-permute-done((bf16[5,56,128]{2,1,0:T(8,128)(2,1)S(1)}, bf16[5,56,128]{2,1,0:T(8,128)(2,1)S(1)}, u32[]{:S(2)}, u32[]{:S(2)}) %collective-permute-start) | collective-permute-done | bytes 71712 | tf_op jit(solution)/shard_map/ppermute | solution.py:28
  10.4 2.5 %collective-permute-done.2.last = bf16[5,56,128]{2,1,0:T(8,128)(2,1)S(1)} collective-permute-done((bf16[5,56,128]{2,1,0:T(8,128)(2,1)S(1)}, bf16[5,56,128]{2,1,0:T(8,128)(2,1)S(1)}, u32[]{:S(2)}, u32[]{:S(2)}) %collective-permute-start.2) | collective-permute-done | bytes 71712 | tf_op jit(solution)/shard_map/ppermute | solution.py:28
  13.0 4.0 %collective-permute-start.6 = (bf16[672,128]{1,0:T(8,128)(2,1)S(1)}, bf16[672,128]{1,0:T(8,128)(2,1)S(1)}, u32[]{:S(2)}, u32[]{:S(2)}) collective-permute-start(bf16[672,128]{1,0:T(8,128)(2,1)S(1)} %get-tuple-element.42.refs_0_.refs_4_), channel_id=1, source_target_pairs={{0,64},{32,96},{64,0},{96,32},{1,65},{33,97},{65,1},{97,33},{2,66}... | collective-permute-start | bytes 516104 | tf_op jit(solution)/shard_map/ppermute | solution.py:28
  17.0 1.0 %collective-permute-start.7 = (bf16[672,128]{1,0:T(8,128)(2,1)S(1)}, bf16[672,128]{1,0:T(8,128)(2,1)S(1)}, u32[]{:S(2)}, u32[]{:S(2)}) collective-permute-start(bf16[672,128]{1,0:T(8,128)(2,1)S(1)} %get-tuple-element.42.refs_0_.refs_4_), channel_id=1, source_target_pairs={{0,32},{32,64},{64,96},{96,0},{1,33},{33,65},{65,97},{97,1},{2,34}... | collective-permute-start | bytes 516104 | tf_op jit(solution)/shard_map/ppermute | solution.py:28
  18.0 2.2 %collective-permute-start.8 = (bf16[672,128]{1,0:T(8,128)(2,1)S(1)}, bf16[672,128]{1,0:T(8,128)(2,1)S(1)}, u32[]{:S(2)}, u32[]{:S(2)}) collective-permute-start(bf16[672,128]{1,0:T(8,128)(2,1)S(1)} %get-tuple-element.42.refs_0_.refs_4_), channel_id=1, source_target_pairs={{0,96},{32,0},{64,32},{96,64},{1,97},{33,1},{65,33},{97,65},{2,98}... | collective-permute-start | bytes 516104 | tf_op jit(solution)/shard_map/ppermute | solution.py:28
  20.2 2.0 %collective-permute-done.6.refs_1_.refs_5_ = bf16[672,128]{1,0:T(8,128)(2,1)S(1)} collective-permute-done((bf16[672,128]{1,0:T(8,128)(2,1)S(1)}, bf16[672,128]{1,0:T(8,128)(2,1)S(1)}, u32[]{:S(2)}, u32[]{:S(2)}) %collective-permute-start.6) | collective-permute-done | bytes 172064 | tf_op jit(solution)/shard_map/ppermute | solution.py:28
  22.2 2.7 %collective-permute-done.7.refs_2_.refs_6_ = bf16[672,128]{1,0:T(8,128)(2,1)S(1)} collective-permute-done((bf16[672,128]{1,0:T(8,128)(2,1)S(1)}, bf16[672,128]{1,0:T(8,128)(2,1)S(1)}, u32[]{:S(2)}, u32[]{:S(2)}) %collective-permute-start.7) | collective-permute-done | bytes 172064 | tf_op jit(solution)/shard_map/ppermute | solution.py:28
  24.9 0.7 collective-permute-done.8.refs_3_.refs_7_
  25.8 3.1 %collective-permute-start.16 = (bf16[448,128]{1,0:T(8,128)(2,1)S(1)}, bf16[448,128]{1,0:T(8,128)(2,1)S(1)}, u32[]{:S(2)}, u32[]{:S(2)}) collective-permute-start(bf16[448,128]{1,0:T(8,128)(2,1)S(1)} %get-tuple-element.48.refs_0_.refs_4_), channel_id=1, source_target_pairs={{0,8},{4,12},{8,0},{12,4},{1,9},{5,13},{9,1},{13,5},{2,10},{6,14},... | collective-permute-start | bytes 344072 | tf_op jit(solution)/shard_map/ppermute | solution.py:28
  28.9 0.6 collective-permute-start.17
  29.5 2.6 %collective-permute-start.18 = (bf16[448,128]{1,0:T(8,128)(2,1)S(1)}, bf16[448,128]{1,0:T(8,128)(2,1)S(1)}, u32[]{:S(2)}, u32[]{:S(2)}) collective-permute-start(bf16[448,128]{1,0:T(8,128)(2,1)S(1)} %get-tuple-element.48.refs_0_.refs_4_), channel_id=1, source_target_pairs={{0,12},{4,0},{8,4},{12,8},{1,13},{5,1},{9,5},{13,9},{2,14},{6,2},{... | collective-permute-start | bytes 344072 | tf_op jit(solution)/shard_map/ppermute | solution.py:28
  32.1 1.3 %collective-permute-done.16.refs_1_.refs_5_ = bf16[448,128]{1,0:T(8,128)(2,1)S(1)} collective-permute-done((bf16[448,128]{1,0:T(8,128)(2,1)S(1)}, bf16[448,128]{1,0:T(8,128)(2,1)S(1)}, u32[]{:S(2)}, u32[]{:S(2)}) %collective-permute-start.16) | collective-permute-done | bytes 114720 | tf_op jit(solution)/shard_map/ppermute | solution.py:28
  33.4 2.2 %collective-permute-done.17.refs_2_.refs_6_ = bf16[448,128]{1,0:T(8,128)(2,1)S(1)} collective-permute-done((bf16[448,128]{1,0:T(8,128)(2,1)S(1)}, bf16[448,128]{1,0:T(8,128)(2,1)S(1)}, u32[]{:S(2)}, u32[]{:S(2)}) %collective-permute-start.17) | collective-permute-done | bytes 114720 | tf_op jit(solution)/shard_map/ppermute | solution.py:28
  35.7 2.2 %collective-permute-start.13 = (bf16[448,128]{1,0:T(8,128)(2,1)S(1)}, bf16[448,128]{1,0:T(8,128)(2,1)S(1)}, u32[]{:S(2)}, u32[]{:S(2)}) collective-permute-start(bf16[448,128]{1,0:T(8,128)(2,1)S(1)} %get-tuple-element.47.refs_0_), channel_id=1, source_target_pairs={{0,64},{32,96},{64,0},{96,32},{1,65},{33,97},{65,1},{97,33},{2,66}... | collective-permute-start | bytes 344072 | tf_op jit(solution)/shard_map/ppermute | solution.py:28
  37.9 1.5 %collective-permute-start.14 = (bf16[448,128]{1,0:T(8,128)(2,1)S(1)}, bf16[448,128]{1,0:T(8,128)(2,1)S(1)}, u32[]{:S(2)}, u32[]{:S(2)}) collective-permute-start(bf16[448,128]{1,0:T(8,128)(2,1)S(1)} %get-tuple-element.47.refs_0_), channel_id=1, source_target_pairs={{0,32},{32,64},{64,96},{96,0},{1,33},{33,65},{65,97},{97,1},{2,34}... | collective-permute-start | bytes 344072 | tf_op jit(solution)/shard_map/ppermute | solution.py:28
  39.3 1.8 %collective-permute-start.15 = (bf16[448,128]{1,0:T(8,128)(2,1)S(1)}, bf16[448,128]{1,0:T(8,128)(2,1)S(1)}, u32[]{:S(2)}, u32[]{:S(2)}) collective-permute-start(bf16[448,128]{1,0:T(8,128)(2,1)S(1)} %get-tuple-element.47.refs_0_), channel_id=1, source_target_pairs={{0,96},{32,0},{64,32},{96,64},{1,97},{33,1},{65,33},{97,65},{2,98}... | collective-permute-start | bytes 344072 | tf_op jit(solution)/shard_map/ppermute | solution.py:28
  41.1 2.2 %collective-permute-done.13.refs_1_ = bf16[448,128]{1,0:T(8,128)(2,1)S(1)} collective-permute-done((bf16[448,128]{1,0:T(8,128)(2,1)S(1)}, bf16[448,128]{1,0:T(8,128)(2,1)S(1)}, u32[]{:S(2)}, u32[]{:S(2)}) %collective-permute-start.13) | collective-permute-done | bytes 114720 | tf_op jit(solution)/shard_map/ppermute | solution.py:28
  43.3 1.9 %collective-permute-start.3 = (bf16[672,128]{1,0:T(8,128)(2,1)S(1)}, bf16[672,128]{1,0:T(8,128)(2,1)S(1)}, u32[]{:S(2)}, u32[]{:S(2)}) collective-permute-start(bf16[672,128]{1,0:T(8,128)(2,1)S(1)} %get-tuple-element.41.refs_0_), channel_id=1, source_target_pairs={{0,8},{4,12},{8,0},{12,4},{1,9},{5,13},{9,1},{13,5},{2,10},{6,14},... | collective-permute-start | bytes 516104 | tf_op jit(solution)/shard_map/ppermute | solution.py:28
  45.2 1.8 %collective-permute-start.4 = (bf16[672,128]{1,0:T(8,128)(2,1)S(1)}, bf16[672,128]{1,0:T(8,128)(2,1)S(1)}, u32[]{:S(2)}, u32[]{:S(2)}) collective-permute-start(bf16[672,128]{1,0:T(8,128)(2,1)S(1)} %get-tuple-element.41.refs_0_), channel_id=1, source_target_pairs={{0,4},{4,8},{8,12},{12,0},{1,5},{5,9},{9,13},{13,1},{2,6},{6,10},{... | collective-permute-start | bytes 516104 | tf_op jit(solution)/shard_map/ppermute | solution.py:28
  47.0 1.4 %collective-permute-start.5 = (bf16[672,128]{1,0:T(8,128)(2,1)S(1)}, bf16[672,128]{1,0:T(8,128)(2,1)S(1)}, u32[]{:S(2)}, u32[]{:S(2)}) collective-permute-start(bf16[672,128]{1,0:T(8,128)(2,1)S(1)} %get-tuple-element.41.refs_0_), channel_id=1, source_target_pairs={{0,12},{4,0},{8,4},{12,8},{1,13},{5,1},{9,5},{13,9},{2,14},{6,2},{... | collective-permute-start | bytes 516104 | tf_op jit(solution)/shard_map/ppermute | solution.py:28
  49.0 4.2 %shard_map.91 = (bf16[480,128]{1,0:T(8,128)(2,1)S(1)}, bf16[480,128]{1,0:T(8,128)(2,1)S(1)}, bf16[480,128]{1,0:T(8,128)(2,1)S(1)}, bf16[480,128]{1,0:T(8,128)(2,1)S(1)}) custom-call(bf16[448,128]{1,0:T(8,128)(2,1)S(1)} %get-tuple-element.47.refs_0_, bf16[448,128]{1,0:T(8,128)(2,1)S(1)} %collective-permute-done.13.refs_1_, ...), custom_call_target="tpu_custom_call" | custom-call | flops 822083584 | bytes 1867776 | tf_op jit(solution)/shard_map/pallas_call | solution.py:48
  53.2 1.3 %collective-permute-start.24 = (bf16[5,56,128]{2,1,0:T(8,128)(2,1)S(1)}, bf16[5,56,128]{2,1,0:T(8,128)(2,1)S(1)}, u32[]{:S(2)}, u32[]{:S(2)}) collective-permute-start(bf16[5,56,128]{2,1,0:T(8,128)(2,1)S(1)} %get-tuple-element.55), channel_id=1, source_target_pairs={{0,16},{1,17},{16,0},{17,1},{2,18},{3,19},{18,2},{19,3},{4,20},{5,... | collective-permute-start | bytes 215048 | tf_op jit(solution)/shard_map/ppermute | solution.py:28
  54.5 1.4 %collective-permute-start.25 = (bf16[5,56,128]{2,1,0:T(8,128)(2,1)S(1)}, bf16[5,56,128]{2,1,0:T(8,128)(2,1)S(1)}, u32[]{:S(2)}, u32[]{:S(2)}) collective-permute-start(bf16[5,56,128]{2,1,0:T(8,128)(2,1)S(1)} %get-tuple-element.56), channel_id=1, source_target_pairs={{0,17},{1,0},{16,1},{17,16},{2,19},{3,2},{18,3},{19,18},{4,21},{5,... | collective-permute-start | bytes 215048 | tf_op jit(solution)/shard_map/ppermute | solution.py:28
  55.9 2.1 %collective-permute-start.20 = (bf16[480,128]{1,0:T(8,128)(2,1)S(1)}, bf16[480,128]{1,0:T(8,128)(2,1)S(1)}, u32[]{:S(2)}, u32[]{:S(2)}) collective-permute-start(bf16[480,128]{1,0:T(8,128)(2,1)S(1)} %get-tuple-element.50), channel_id=1, source_target_pairs={{0,64},{32,96},{64,0},{96,32},{1,65},{33,97},{65,1},{97,33},{2,66}... | collective-permute-start | bytes 368648 | tf_op jit(solution)/shard_map/ppermute | solution.py:28
  58.0 6.3 %shard_map.89 = (bf16[704,128]{1,0:T(8,128)(2,1)S(1)}, bf16[704,128]{1,0:T(8,128)(2,1)S(1)}, bf16[704,128]{1,0:T(8,128)(2,1)S(1)}, bf16[704,128]{1,0:T(8,128)(2,1)S(1)}) custom-call(bf16[672,128]{1,0:T(8,128)(2,1)S(1)} %get-tuple-element.41.refs_0_, bf16[672,128]{1,0:T(8,128)(2,1)S(1)} %collective-permute-done.3.refs_1_, ...), custom_call_target="tpu_custom_call" | custom-call | flops 1233125376 | bytes 2785280 | tf_op jit(solution)/shard_map/pallas_call | solution.py:48
  64.3 1.2 %collective-permute-start.10 = (bf16[704,128]{1,0:T(8,128)(2,1)S(1)}, bf16[704,128]{1,0:T(8,128)(2,1)S(1)}, u32[]{:S(2)}, u32[]{:S(2)}) collective-permute-start(bf16[704,128]{1,0:T(8,128)(2,1)S(1)} %get-tuple-element.44), channel_id=1, source_target_pairs={{0,8},{4,12},{8,0},{12,4},{1,9},{5,13},{9,1},{13,5},{2,10},{6,14},... | collective-permute-start | bytes 540680 | tf_op jit(solution)/shard_map/ppermute | solution.py:28
  65.4 2.2 %collective-permute-start.11 = (bf16[704,128]{1,0:T(8,128)(2,1)S(1)}, bf16[704,128]{1,0:T(8,128)(2,1)S(1)}, u32[]{:S(2)}, u32[]{:S(2)}) collective-permute-start(bf16[704,128]{1,0:T(8,128)(2,1)S(1)} %get-tuple-element.45), channel_id=1, source_target_pairs={{0,12},{4,0},{8,4},{12,8},{1,13},{5,1},{9,5},{13,9},{2,14},{6,2},{... | collective-permute-start | bytes 540680 | tf_op jit(solution)/shard_map/ppermute | solution.py:28
  67.7 1.7 %collective-permute-start.21 = (bf16[480,128]{1,0:T(8,128)(2,1)S(1)}, bf16[480,128]{1,0:T(8,128)(2,1)S(1)}, u32[]{:S(2)}, u32[]{:S(2)}) collective-permute-start(bf16[480,128]{1,0:T(8,128)(2,1)S(1)} %get-tuple-element.51), channel_id=1, source_target_pairs={{0,96},{32,0},{64,32},{96,64},{1,97},{33,1},{65,33},{97,65},{2,98}... | collective-permute-start | bytes 368648 | tf_op jit(solution)/shard_map/ppermute | solution.py:28
  69.4 0.4 collective-permute-start.22
  69.8 2.9 %shard_map.93 = (bf16[512,640]{1,0:T(8,128)(2,1)S(1)}, f32[8,512]{1,0:T(8,128)S(1)}, bf16[2,2,512,640]{3,2,1,0:T(8,128)(2,1)S(1)}, f32[8,640]{1,0:T(8,128)S(1)}) custom-call(s32[2]{0:T(128)S(1)} %pad_add_fusion.info_ref, s32[2,512]{1,0:T(2,128)S(1)} %copy-done.3, s32[1,512]{1,0:T(1,128)S(1)} %bitcast.9, bf16[1,2560]{1,0:T(2,128)(2,1)S(1)} %reshape.15.gain_ref, ...), custom_call_target="tpu_custom_call" | custom-call | flops 335544320 | bytes 3324928 | tf_op jit(solution)/shard_map/pallas_call | solution.py:48
  72.7 2.7 %collective-permute-done.22.refs_7_ = bf16[480,128]{1,0:T(8,128)(2,1)S(1)} collective-permute-done((bf16[480,128]{1,0:T(8,128)(2,1)S(1)}, bf16[480,128]{1,0:T(8,128)(2,1)S(1)}, u32[]{:S(2)}, u32[]{:S(2)}) %collective-permute-start.22) | collective-permute-done | bytes 122912 | tf_op jit(solution)/shard_map/ppermute | solution.py:28
  75.5 1.6 %shard_map.94 = (bf16[6,56,128]{2,1,0:T(8,128)(2,1)S(1)}, bf16[6,56,128]{2,1,0:T(8,128)(2,1)S(1)}, bf16[6,56,128]{2,1,0:T(8,128)(2,1)S(1)}, bf16[6,56,128]{2,1,0:T(8,128)(2,1)S(1)}, f32[5,4,56,128]{3,2,1,0:T(8,128)S(1)}) custom-call(bf16[704,128]{1,0:T(8,128)(2,1)S(1)} %get-tuple-element.43.refs_0_, bf16[704,128]{1,0:T(8,128)(2,1)S(1)} %collective-permute-done.10.refs_1_, ...), custom_call_target="tpu_custom_call" | custom-call | bytes 2416640 | tf_op jit(solution)/shard_map/pallas_call | solution.py:48
  77.0 0.9 collective-permute-start.26
  78.0 2.4 %collective-permute-start.27 = (bf16[6,56,128]{2,1,0:T(8,128)(2,1)S(1)}, bf16[6,56,128]{2,1,0:T(8,128)(2,1)S(1)}, u32[]{:S(2)}, u32[]{:S(2)}) collective-permute-start(bf16[6,56,128]{2,1,0:T(8,128)(2,1)S(1)} %get-tuple-element.60), channel_id=1, source_target_pairs={{0,16},{1,17},{16,0},{17,1},{2,18},{3,19},{18,2},{19,3},{4,20},{5,... | collective-permute-start | bytes 258056 | tf_op jit(solution)/shard_map/ppermute | solution.py:28
  80.4 2.5 %collective-permute-start.28 = (bf16[6,56,128]{2,1,0:T(8,128)(2,1)S(1)}, bf16[6,56,128]{2,1,0:T(8,128)(2,1)S(1)}, u32[]{:S(2)}, u32[]{:S(2)}) collective-permute-start(bf16[6,56,128]{2,1,0:T(8,128)(2,1)S(1)} %get-tuple-element.61), channel_id=1, source_target_pairs={{0,1},{1,16},{16,17},{17,0},{2,3},{3,18},{18,19},{19,2},{4,5},{5,2... | collective-permute-start | bytes 258056 | tf_op jit(solution)/shard_map/ppermute | solution.py:28
  82.9 1.1 %shard_map.96.scores_ref = f32[2,5,112,512]{3,2,1,0:T(8,128)S(1)} custom-call(s32[2]{0:T(128)S(1)} %pad_add_fusion.info_ref, f32[5,4,56,128]{3,2,1,0:T(8,128)S(1)} %get-tuple-element.62.middle_ref, f32[8,640]{1,0:T(8,128)S(1)} %get-tuple-element.63.gain_ref, bf16[2,2,512,640]{3,2,1,0:T(8,128)(2,1)S(1)} %get-tuple-element.64.text_ref), custom_call_target="tpu_custom_call" | custom-call | flops 146800640 | bytes 5509120 | tf_op jit(solution)/shard_map/pallas_call | solution.py:48
  84.1 1.0 %collective-permute-done.28.refs_3_.s3 = bf16[6,56,128]{2,1,0:T(8,128)(2,1)S(1)} collective-permute-done((bf16[6,56,128]{2,1,0:T(8,128)(2,1)S(1)}, bf16[6,56,128]{2,1,0:T(8,128)(2,1)S(1)}, u32[]{:S(2)}, u32[]{:S(2)}) %collective-permute-start.28) | collective-permute-done | bytes 86048 | tf_op jit(solution)/shard_map/ppermute | solution.py:28
  85.0 2.1 %shard_map.97 = (bf16[5,56,128]{2,1,0:T(8,128)(2,1)S(1)}, bf16[5,56,128]{2,1,0:T(8,128)(2,1)S(1)}, bf16[5,56,128]{2,1,0:T(8,128)(2,1)S(1)}, bf16[5,56,128]{2,1,0:T(8,128)(2,1)S(1)}) custom-call(s32[2]{0:T(128)S(1)} %pad_add_fusion.info_ref, bf16[6,56,128]{2,1,0:T(8,128)(2,1)S(1)} %get-tuple-element.58.refs_0_.s0, ...), custom_call_target="tpu_custom_call" | custom-call | flops 220200960 | bytes 6791168 | tf_op jit(solution)/shard_map/pallas_call | solution.py:48
  87.2 1.6 %collective-permute-start.29 = (bf16[5,56,128]{2,1,0:T(8,128)(2,1)S(1)}, bf16[5,56,128]{2,1,0:T(8,128)(2,1)S(1)}, u32[]{:S(2)}, u32[]{:S(2)}) collective-permute-start(bf16[5,56,128]{2,1,0:T(8,128)(2,1)S(1)} %get-tuple-element.67), channel_id=1, source_target_pairs={{0,17},{1,0},{16,1},{17,16},{2,19},{3,2},{18,3},{19,18},{4,21},{5,... | collective-permute-start | bytes 215048 | tf_op jit(solution)/shard_map/ppermute | solution.py:28
  88.8 3.5 %collective-permute-start.30 = (bf16[5,56,128]{2,1,0:T(8,128)(2,1)S(1)}, bf16[5,56,128]{2,1,0:T(8,128)(2,1)S(1)}, u32[]{:S(2)}, u32[]{:S(2)}) collective-permute-start(bf16[5,56,128]{2,1,0:T(8,128)(2,1)S(1)} %get-tuple-element.68), channel_id=1, source_target_pairs={{0,16},{1,17},{16,0},{17,1},{2,18},{3,19},{18,2},{19,3},{4,20},{5,... | collective-permute-start | bytes 215048 | tf_op jit(solution)/shard_map/ppermute | solution.py:28
  92.6 0.8 shard_map.95
  93.4 2.0 %collective-permute-done.30.refs_2_ = bf16[5,56,128]{2,1,0:T(8,128)(2,1)S(1)} collective-permute-done((bf16[5,56,128]{2,1,0:T(8,128)(2,1)S(1)}, bf16[5,56,128]{2,1,0:T(8,128)(2,1)S(1)}, u32[]{:S(2)}, u32[]{:S(2)}) %collective-permute-start.30) | collective-permute-done | bytes 71712 | tf_op jit(solution)/shard_map/ppermute | solution.py:28
  95.4 1.3 %collective-permute-done.31.refs_3_ = bf16[5,56,128]{2,1,0:T(8,128)(2,1)S(1)} collective-permute-done((bf16[5,56,128]{2,1,0:T(8,128)(2,1)S(1)}, bf16[5,56,128]{2,1,0:T(8,128)(2,1)S(1)}, u32[]{:S(2)}, u32[]{:S(2)}) %collective-permute-start.31) | collective-permute-done | bytes 71712 | tf_op jit(solution)/shard_map/ppermute | solution.py:28
  96.6 0.8 shard_map.98
  (43 shorter events, 1.5 us)
Async XLA Ops:
  0.6 47.8 %copy-start = (bf16[1,56,2560]{2,1,0:T(8,128)(2,1)S(1)}, bf16[1,56,2560]{2,1,0:T(8,128)(2,1)}, u32[]{:S(2)}) copy-start(bf16[1,56,2560]{2,1,0:T(8,128)(2,1)} %param.9) | copy-start | bytes 860164
  0.6 1.0 %copy-start.1 = (bf16[1,56,2560]{2,1,0:T(8,128)(2,1)S(1)}, bf16[1,56,2560]{2,1,0:T(8,128)(2,1)}, u32[]{:S(2)}) copy-start(bf16[1,56,2560]{2,1,0:T(8,128)(2,1)} %param.7) | copy-start | bytes 860164
  1.6 1.0 copy-start.2
  2.7 10.2 %collective-permute-start.1 = (bf16[15,56,128]{2,1,0:T(8,128)(2,1)S(1)}, bf16[15,56,128]{2,1,0:T(8,128)(2,1)S(1)}, u32[]{:S(2)}, u32[]{:S(2)}) collective-permute-start(bf16[15,56,128]{2,1,0:T(8,128)(2,1)S(1)} %get-tuple-element.39), channel_id=1, source_target_pairs={{0,16},{1,17},{16,0},{17,1},{2,18},{3,19},{18,2},{19,3},{4,20},{5,... | collective-permute-start | bytes 645128 | tf_op jit(solution)/shard_map/ppermute | solution.py:28
  4.1 6.3 %collective-permute-start = (bf16[5,56,128]{2,1,0:T(8,128)(2,1)S(1)}, bf16[5,56,128]{2,1,0:T(8,128)(2,1)S(1)}, u32[]{:S(2)}, u32[]{:S(2)}) collective-permute-start(bf16[5,56,128]{2,1,0:T(8,128)(2,1)S(1)} %get-tuple-element.38), channel_id=1, source_target_pairs={{0,1},{1,16},{16,17},{17,0},{2,3},{3,18},{18,19},{19,2},{4,5},{5,2... | collective-permute-start | bytes 215048 | tf_op jit(solution)/shard_map/ppermute | solution.py:28
  6.2 6.7 %collective-permute-start.2 = (bf16[5,56,128]{2,1,0:T(8,128)(2,1)S(1)}, bf16[5,56,128]{2,1,0:T(8,128)(2,1)S(1)}, u32[]{:S(2)}, u32[]{:S(2)}) collective-permute-start(bf16[5,56,128]{2,1,0:T(8,128)(2,1)S(1)} %get-tuple-element.40), channel_id=1, source_target_pairs={{0,17},{1,0},{16,1},{17,16},{2,19},{3,2},{18,3},{19,18},{4,21},{5,... | collective-permute-start | bytes 215048 | tf_op jit(solution)/shard_map/ppermute | solution.py:28
  13.0 9.2 %collective-permute-start.6 = (bf16[672,128]{1,0:T(8,128)(2,1)S(1)}, bf16[672,128]{1,0:T(8,128)(2,1)S(1)}, u32[]{:S(2)}, u32[]{:S(2)}) collective-permute-start(bf16[672,128]{1,0:T(8,128)(2,1)S(1)} %get-tuple-element.42.refs_0_.refs_4_), channel_id=1, source_target_pairs={{0,64},{32,96},{64,0},{96,32},{1,65},{33,97},{65,1},{97,33},{2,66}... | collective-permute-start | bytes 516104 | tf_op jit(solution)/shard_map/ppermute | solution.py:28
  17.0 7.9 %collective-permute-start.7 = (bf16[672,128]{1,0:T(8,128)(2,1)S(1)}, bf16[672,128]{1,0:T(8,128)(2,1)S(1)}, u32[]{:S(2)}, u32[]{:S(2)}) collective-permute-start(bf16[672,128]{1,0:T(8,128)(2,1)S(1)} %get-tuple-element.42.refs_0_.refs_4_), channel_id=1, source_target_pairs={{0,32},{32,64},{64,96},{96,0},{1,33},{33,65},{65,97},{97,1},{2,34}... | collective-permute-start | bytes 516104 | tf_op jit(solution)/shard_map/ppermute | solution.py:28
  18.0 7.7 %collective-permute-start.8 = (bf16[672,128]{1,0:T(8,128)(2,1)S(1)}, bf16[672,128]{1,0:T(8,128)(2,1)S(1)}, u32[]{:S(2)}, u32[]{:S(2)}) collective-permute-start(bf16[672,128]{1,0:T(8,128)(2,1)S(1)} %get-tuple-element.42.refs_0_.refs_4_), channel_id=1, source_target_pairs={{0,96},{32,0},{64,32},{96,64},{1,97},{33,1},{65,33},{97,65},{2,98}... | collective-permute-start | bytes 516104 | tf_op jit(solution)/shard_map/ppermute | solution.py:28
  25.7 32.3 %collective-permute-start.9 = (bf16[2688,128]{1,0:T(8,128)(2,1)S(1)}, bf16[2688,128]{1,0:T(8,128)(2,1)S(1)}, u32[]{:S(2)}, u32[]{:S(2)}) collective-permute-start(bf16[2688,128]{1,0:T(8,128)(2,1)S(1)} %shard_map.88), channel_id=1, source_target_pairs={{0,2},{2,0},{1,3},{3,1},{4,6},{6,4},{5,7},{7,5},{8,10},{10,8},{9,1... | collective-permute-start | bytes 2064392 | tf_op jit(solution)/shard_map/ppermute | solution.py:28
  25.8 7.6 %collective-permute-start.16 = (bf16[448,128]{1,0:T(8,128)(2,1)S(1)}, bf16[448,128]{1,0:T(8,128)(2,1)S(1)}, u32[]{:S(2)}, u32[]{:S(2)}) collective-permute-start(bf16[448,128]{1,0:T(8,128)(2,1)S(1)} %get-tuple-element.48.refs_0_.refs_4_), channel_id=1, source_target_pairs={{0,8},{4,12},{8,0},{12,4},{1,9},{5,13},{9,1},{13,5},{2,10},{6,14},... | collective-permute-start | bytes 344072 | tf_op jit(solution)/shard_map/ppermute | solution.py:28
  28.9 6.7 %collective-permute-start.17 = (bf16[448,128]{1,0:T(8,128)(2,1)S(1)}, bf16[448,128]{1,0:T(8,128)(2,1)S(1)}, u32[]{:S(2)}, u32[]{:S(2)}) collective-permute-start(bf16[448,128]{1,0:T(8,128)(2,1)S(1)} %get-tuple-element.48.refs_0_.refs_4_), channel_id=1, source_target_pairs={{0,4},{4,8},{8,12},{12,0},{1,5},{5,9},{9,13},{13,1},{2,6},{6,10},{... | collective-permute-start | bytes 344072 | tf_op jit(solution)/shard_map/ppermute | solution.py:28
  29.5 6.1 %collective-permute-start.18 = (bf16[448,128]{1,0:T(8,128)(2,1)S(1)}, bf16[448,128]{1,0:T(8,128)(2,1)S(1)}, u32[]{:S(2)}, u32[]{:S(2)}) collective-permute-start(bf16[448,128]{1,0:T(8,128)(2,1)S(1)} %get-tuple-element.48.refs_0_.refs_4_), channel_id=1, source_target_pairs={{0,12},{4,0},{8,4},{12,8},{1,13},{5,1},{9,5},{13,9},{2,14},{6,2},{... | collective-permute-start | bytes 344072 | tf_op jit(solution)/shard_map/ppermute | solution.py:28
  35.6 12.9 %collective-permute-start.19 = (bf16[1792,128]{1,0:T(8,128)(2,1)S(1)}, bf16[1792,128]{1,0:T(8,128)(2,1)S(1)}, u32[]{:S(2)}, u32[]{:S(2)}) collective-permute-start(bf16[1792,128]{1,0:T(8,128)(2,1)S(1)} %shard_map.90), channel_id=1, source_target_pairs={{0,2},{2,0},{1,3},{3,1},{4,6},{6,4},{5,7},{7,5},{8,10},{10,8},{9,1... | collective-permute-start | bytes 1376264 | tf_op jit(solution)/shard_map/ppermute | solution.py:28
  35.7 7.6 %collective-permute-start.13 = (bf16[448,128]{1,0:T(8,128)(2,1)S(1)}, bf16[448,128]{1,0:T(8,128)(2,1)S(1)}, u32[]{:S(2)}, u32[]{:S(2)}) collective-permute-start(bf16[448,128]{1,0:T(8,128)(2,1)S(1)} %get-tuple-element.47.refs_0_), channel_id=1, source_target_pairs={{0,64},{32,96},{64,0},{96,32},{1,65},{33,97},{65,1},{97,33},{2,66}... | collective-permute-start | bytes 344072 | tf_op jit(solution)/shard_map/ppermute | solution.py:28
  37.9 7.4 %collective-permute-start.14 = (bf16[448,128]{1,0:T(8,128)(2,1)S(1)}, bf16[448,128]{1,0:T(8,128)(2,1)S(1)}, u32[]{:S(2)}, u32[]{:S(2)}) collective-permute-start(bf16[448,128]{1,0:T(8,128)(2,1)S(1)} %get-tuple-element.47.refs_0_), channel_id=1, source_target_pairs={{0,32},{32,64},{64,96},{96,0},{1,33},{33,65},{65,97},{97,1},{2,34}... | collective-permute-start | bytes 344072 | tf_op jit(solution)/shard_map/ppermute | solution.py:28
  39.3 7.7 %collective-permute-start.15 = (bf16[448,128]{1,0:T(8,128)(2,1)S(1)}, bf16[448,128]{1,0:T(8,128)(2,1)S(1)}, u32[]{:S(2)}, u32[]{:S(2)}) collective-permute-start(bf16[448,128]{1,0:T(8,128)(2,1)S(1)} %get-tuple-element.47.refs_0_), channel_id=1, source_target_pairs={{0,96},{32,0},{64,32},{96,64},{1,97},{33,1},{65,33},{97,65},{2,98}... | collective-permute-start | bytes 344072 | tf_op jit(solution)/shard_map/ppermute | solution.py:28
  43.3 9.9 %collective-permute-start.3 = (bf16[672,128]{1,0:T(8,128)(2,1)S(1)}, bf16[672,128]{1,0:T(8,128)(2,1)S(1)}, u32[]{:S(2)}, u32[]{:S(2)}) collective-permute-start(bf16[672,128]{1,0:T(8,128)(2,1)S(1)} %get-tuple-element.41.refs_0_), channel_id=1, source_target_pairs={{0,8},{4,12},{8,0},{12,4},{1,9},{5,13},{9,1},{13,5},{2,10},{6,14},... | collective-permute-start | bytes 516104 | tf_op jit(solution)/shard_map/ppermute | solution.py:28
  45.2 9.3 %collective-permute-start.4 = (bf16[672,128]{1,0:T(8,128)(2,1)S(1)}, bf16[672,128]{1,0:T(8,128)(2,1)S(1)}, u32[]{:S(2)}, u32[]{:S(2)}) collective-permute-start(bf16[672,128]{1,0:T(8,128)(2,1)S(1)} %get-tuple-element.41.refs_0_), channel_id=1, source_target_pairs={{0,4},{4,8},{8,12},{12,0},{1,5},{5,9},{9,13},{13,1},{2,6},{6,10},{... | collective-permute-start | bytes 516104 | tf_op jit(solution)/shard_map/ppermute | solution.py:28
  47.0 8.9 %collective-permute-start.5 = (bf16[672,128]{1,0:T(8,128)(2,1)S(1)}, bf16[672,128]{1,0:T(8,128)(2,1)S(1)}, u32[]{:S(2)}, u32[]{:S(2)}) collective-permute-start(bf16[672,128]{1,0:T(8,128)(2,1)S(1)} %get-tuple-element.41.refs_0_), channel_id=1, source_target_pairs={{0,12},{4,0},{8,4},{12,8},{1,13},{5,1},{9,5},{13,9},{2,14},{6,2},{... | collective-permute-start | bytes 516104 | tf_op jit(solution)/shard_map/ppermute | solution.py:28
  48.5 16.9 %collective-permute-start.23 = (bf16[5,56,128]{2,1,0:T(8,128)(2,1)S(1)}, bf16[5,56,128]{2,1,0:T(8,128)(2,1)S(1)}, u32[]{:S(2)}, u32[]{:S(2)}) collective-permute-start(bf16[5,56,128]{2,1,0:T(8,128)(2,1)S(1)} %get-tuple-element.54), channel_id=1, source_target_pairs={{0,1},{1,16},{16,17},{17,0},{2,3},{3,18},{18,19},{19,2},{4,5},{5,2... | collective-permute-start | bytes 215048 | tf_op jit(solution)/shard_map/ppermute | solution.py:28
  53.2 14.5 %copy-start.5 = (bf16[2560]{0:T(1024)(128)(2,1)S(1)}, bf16[2560]{0:T(1024)(128)(2,1)}, u32[]{:S(2)}) copy-start(bf16[2560]{0:T(1024)(128)(2,1)} %param.10) | copy-start | bytes 15364
  53.2 16.7 %copy-start.3 = (s32[2,512]{1,0:T(2,128)S(1)}, s32[2,512]{1,0:T(2,128)}, u32[]{:S(2)}) copy-start(s32[2,512]{1,0:T(2,128)} %ids_ref.1) | copy-start | bytes 12292
  53.2 16.7 %copy-start.4 = (s32[512]{0:T(512)S(1)}, s32[512]{0:T(512)}, u32[]{:S(2)}) copy-start(s32[512]{0:T(512)} %param.13) | copy-start | bytes 6148
  53.2 14.4 %collective-permute-start.24 = (bf16[5,56,128]{2,1,0:T(8,128)(2,1)S(1)}, bf16[5,56,128]{2,1,0:T(8,128)(2,1)S(1)}, u32[]{:S(2)}, u32[]{:S(2)}) collective-permute-start(bf16[5,56,128]{2,1,0:T(8,128)(2,1)S(1)} %get-tuple-element.55), channel_id=1, source_target_pairs={{0,16},{1,17},{16,0},{17,1},{2,18},{3,19},{18,2},{19,3},{4,20},{5,... | collective-permute-start | bytes 215048 | tf_op jit(solution)/shard_map/ppermute | solution.py:28
  54.5 13.2 %collective-permute-start.25 = (bf16[5,56,128]{2,1,0:T(8,128)(2,1)S(1)}, bf16[5,56,128]{2,1,0:T(8,128)(2,1)S(1)}, u32[]{:S(2)}, u32[]{:S(2)}) collective-permute-start(bf16[5,56,128]{2,1,0:T(8,128)(2,1)S(1)} %get-tuple-element.56), channel_id=1, source_target_pairs={{0,17},{1,0},{16,1},{17,16},{2,19},{3,2},{18,3},{19,18},{4,21},{5,... | collective-permute-start | bytes 215048 | tf_op jit(solution)/shard_map/ppermute | solution.py:28
  55.9 13.4 %collective-permute-start.20 = (bf16[480,128]{1,0:T(8,128)(2,1)S(1)}, bf16[480,128]{1,0:T(8,128)(2,1)S(1)}, u32[]{:S(2)}, u32[]{:S(2)}) collective-permute-start(bf16[480,128]{1,0:T(8,128)(2,1)S(1)} %get-tuple-element.50), channel_id=1, source_target_pairs={{0,64},{32,96},{64,0},{96,32},{1,65},{33,97},{65,1},{97,33},{2,66}... | collective-permute-start | bytes 368648 | tf_op jit(solution)/shard_map/ppermute | solution.py:28
  64.3 11.2 %collective-permute-start.10 = (bf16[704,128]{1,0:T(8,128)(2,1)S(1)}, bf16[704,128]{1,0:T(8,128)(2,1)S(1)}, u32[]{:S(2)}, u32[]{:S(2)}) collective-permute-start(bf16[704,128]{1,0:T(8,128)(2,1)S(1)} %get-tuple-element.44), channel_id=1, source_target_pairs={{0,8},{4,12},{8,0},{12,4},{1,9},{5,13},{9,1},{13,5},{2,10},{6,14},... | collective-permute-start | bytes 540680 | tf_op jit(solution)/shard_map/ppermute | solution.py:28
  65.4 10.0 %collective-permute-start.11 = (bf16[704,128]{1,0:T(8,128)(2,1)S(1)}, bf16[704,128]{1,0:T(8,128)(2,1)S(1)}, u32[]{:S(2)}, u32[]{:S(2)}) collective-permute-start(bf16[704,128]{1,0:T(8,128)(2,1)S(1)} %get-tuple-element.45), channel_id=1, source_target_pairs={{0,12},{4,0},{8,4},{12,8},{1,13},{5,1},{9,5},{13,9},{2,14},{6,2},{... | collective-permute-start | bytes 540680 | tf_op jit(solution)/shard_map/ppermute | solution.py:28
  67.6 7.8 %collective-permute-start.12 = (bf16[704,128]{1,0:T(8,128)(2,1)S(1)}, bf16[704,128]{1,0:T(8,128)(2,1)S(1)}, u32[]{:S(2)}, u32[]{:S(2)}) collective-permute-start(bf16[704,128]{1,0:T(8,128)(2,1)S(1)} %get-tuple-element.46), channel_id=1, source_target_pairs={{0,4},{4,8},{8,12},{12,0},{1,5},{5,9},{9,13},{13,1},{2,6},{6,10},{... | collective-permute-start | bytes 540680 | tf_op jit(solution)/shard_map/ppermute | solution.py:28
  67.7 5.1 %collective-permute-start.21 = (bf16[480,128]{1,0:T(8,128)(2,1)S(1)}, bf16[480,128]{1,0:T(8,128)(2,1)S(1)}, u32[]{:S(2)}, u32[]{:S(2)}) collective-permute-start(bf16[480,128]{1,0:T(8,128)(2,1)S(1)} %get-tuple-element.51), channel_id=1, source_target_pairs={{0,96},{32,0},{64,32},{96,64},{1,97},{33,1},{65,33},{97,65},{2,98}... | collective-permute-start | bytes 368648 | tf_op jit(solution)/shard_map/ppermute | solution.py:28
  69.4 6.1 %collective-permute-start.22 = (bf16[480,128]{1,0:T(8,128)(2,1)S(1)}, bf16[480,128]{1,0:T(8,128)(2,1)S(1)}, u32[]{:S(2)}, u32[]{:S(2)}) collective-permute-start(bf16[480,128]{1,0:T(8,128)(2,1)S(1)} %get-tuple-element.52), channel_id=1, source_target_pairs={{0,32},{32,64},{64,96},{96,0},{1,33},{33,65},{65,97},{97,1},{2,34}... | collective-permute-start | bytes 368648 | tf_op jit(solution)/shard_map/ppermute | solution.py:28
  77.0 7.0 %collective-permute-start.26 = (bf16[6,56,128]{2,1,0:T(8,128)(2,1)S(1)}, bf16[6,56,128]{2,1,0:T(8,128)(2,1)S(1)}, u32[]{:S(2)}, u32[]{:S(2)}) collective-permute-start(bf16[6,56,128]{2,1,0:T(8,128)(2,1)S(1)} %get-tuple-element.59), channel_id=1, source_target_pairs={{0,17},{1,0},{16,1},{17,16},{2,19},{3,2},{18,3},{19,18},{4,21},{5,... | collective-permute-start | bytes 258056 | tf_op jit(solution)/shard_map/ppermute | solution.py:28
  78.0 6.1 %collective-permute-start.27 = (bf16[6,56,128]{2,1,0:T(8,128)(2,1)S(1)}, bf16[6,56,128]{2,1,0:T(8,128)(2,1)S(1)}, u32[]{:S(2)}, u32[]{:S(2)}) collective-permute-start(bf16[6,56,128]{2,1,0:T(8,128)(2,1)S(1)} %get-tuple-element.60), channel_id=1, source_target_pairs={{0,16},{1,17},{16,0},{17,1},{2,18},{3,19},{18,2},{19,3},{4,20},{5,... | collective-permute-start | bytes 258056 | tf_op jit(solution)/shard_map/ppermute | solution.py:28
  80.4 4.6 %collective-permute-start.28 = (bf16[6,56,128]{2,1,0:T(8,128)(2,1)S(1)}, bf16[6,56,128]{2,1,0:T(8,128)(2,1)S(1)}, u32[]{:S(2)}, u32[]{:S(2)}) collective-permute-start(bf16[6,56,128]{2,1,0:T(8,128)(2,1)S(1)} %get-tuple-element.61), channel_id=1, source_target_pairs={{0,1},{1,16},{16,17},{17,0},{2,3},{3,18},{18,19},{19,2},{4,5},{5,2... | collective-permute-start | bytes 258056 | tf_op jit(solution)/shard_map/ppermute | solution.py:28
  87.2 6.2 %collective-permute-start.29 = (bf16[5,56,128]{2,1,0:T(8,128)(2,1)S(1)}, bf16[5,56,128]{2,1,0:T(8,128)(2,1)S(1)}, u32[]{:S(2)}, u32[]{:S(2)}) collective-permute-start(bf16[5,56,128]{2,1,0:T(8,128)(2,1)S(1)} %get-tuple-element.67), channel_id=1, source_target_pairs={{0,17},{1,0},{16,1},{17,16},{2,19},{3,2},{18,3},{19,18},{4,21},{5,... | collective-permute-start | bytes 215048 | tf_op jit(solution)/shard_map/ppermute | solution.py:28
  88.8 6.6 %collective-permute-start.30 = (bf16[5,56,128]{2,1,0:T(8,128)(2,1)S(1)}, bf16[5,56,128]{2,1,0:T(8,128)(2,1)S(1)}, u32[]{:S(2)}, u32[]{:S(2)}) collective-permute-start(bf16[5,56,128]{2,1,0:T(8,128)(2,1)S(1)} %get-tuple-element.68), channel_id=1, source_target_pairs={{0,16},{1,17},{16,0},{17,1},{2,18},{3,19},{18,2},{19,3},{4,20},{5,... | collective-permute-start | bytes 215048 | tf_op jit(solution)/shard_map/ppermute | solution.py:28
  92.3 4.3 %collective-permute-start.31 = (bf16[5,56,128]{2,1,0:T(8,128)(2,1)S(1)}, bf16[5,56,128]{2,1,0:T(8,128)(2,1)S(1)}, u32[]{:S(2)}, u32[]{:S(2)}) collective-permute-start(bf16[5,56,128]{2,1,0:T(8,128)(2,1)S(1)} %get-tuple-element.69), channel_id=1, source_target_pairs={{0,1},{1,16},{16,17},{17,0},{2,3},{3,18},{18,19},{19,2},{4,5},{5,2... | collective-permute-start | bytes 215048 | tf_op jit(solution)/shard_map/ppermute | solution.py:28
where the time goes:
time: 99.4 us; the launch traced here: 97.4 us
  starting transfers between devices  49.7 us (50%)
  waiting for transfers between devices  24.7 us (25%)
  Pallas kernels  20.1 us (20%)
  local copies, waits for them, and re-layouts  1.98 us (2%)
    ppermute x32, starting transfers between devices, shift(): lax.ppermute(value, axis, [(i, (i + distance) % size) for i in range(size)])  49.7 us
    ppermute x32, waiting for transfers between devices, shift(): lax.ppermute(value, axis, [(i, (i + distance) % size) for i in range(size)])  24.7 us
    pallas_call x13, Pallas kernels, call(): pl.pallas_call(kernel, out_shape=out_shapes, in_specs=in_specs, out_specs...  20.1 us
  transfers between devices with their start and end apart: 32, of which 12 were waited for; matrix products, arithmetic and copies ran while one was open for 0% of the time, Pallas kernels for 16%

commit v1 on v0

--- a/solution.py
+++ b/solution.py
@@ -88,23 +88,23 @@
             outs[distance][head] = rows_ref[:, pl.ds(lane, HD)]
 
 
-def pack_kernel(kept, own, first, across, last, *outs):
+def pack_kernel(kept, own, first, across, last, along_x, along_z):
     queries = (own, first, across, last)
     for group, (low, count, _, _) in enumerate(GROUPS):
-        rows, keys = outs[2 * group], outs[2 * group + 1]
-        for index in range(count):
-            head = low + index
-            rows[index * ROWS : (index + 1) * ROWS, :] = stacked([query[head] for query in queries])
-            keys[index * ROWS : (index + 1) * ROWS, :] = stacked(
+        rows, keys = (along_x, along_z) if group == 0 else (along_z, along_x)
+        for head in range(low, low + count):
+            rows[head * ROWS : (head + 1) * ROWS, :] = stacked([query[head] for query in queries])
+            keys[head * ROWS : (head + 1) * ROWS, :] = stacked(
                 [kept[2 * head], across[NQ + 2 * head], kept[2 * head + 1], across[NQ + 2 * head + 1]]
             )
 
 
 def repack_kernel(*refs):
-    out = refs[4]
-    size = refs[0].shape[0]
+    from_x, from_z, out = refs[:4], refs[4:8], refs[9]
     for index in range(4):
-        out[index * size : (index + 1) * size, :] = refs[index][...]
+        for (low, count, _, _), ref in zip(GROUPS, (from_z[index], from_x[index])):
+            start = 4 * low * ROWS + index * count * ROWS
+            out[start : start + count * ROWS, :] = ref[low * ROWS : (low + count) * ROWS, :]
 
 
 def join_rows_kernel(plane_ref, *refs):
@@ -116,11 +116,12 @@
             out[:, pl.ds(lane, HD)] = pieces[distance][head]
 
 
-def attend_kernel(count, *refs):
+def attend_kernel(low, count, *refs):
     rows_of, keys_of, swapped = refs[:4], refs[4:8], refs[8]
     outs, (keys, values, stats) = refs[9:13], refs[13:]
     size = count * ROWS
-    pieces = [(ref, 0) for ref in keys_of] + [(swapped, index * size) for index in range(4)]
+    pieces = [(ref, low * ROWS) for ref in keys_of]
+    pieces += [(swapped, 4 * low * ROWS + index * size) for index in range(4)]
     lanes = lax.broadcasted_iota(jnp.int32, (ROWS, HD), 1)
     stats[...] = jnp.zeros_like(stats)
 
@@ -132,7 +133,7 @@
                 pl.ds(pl.multiple_of(start + KEYS, 16), KEYS), :
             ]
         for index in range(4):
-            start = pl.multiple_of(head * ROWS, 16)
+            start = pl.multiple_of(low * ROWS + head * ROWS, 16)
             scores = dot_t(rows_of[index][pl.ds(start, ROWS), :], keys[...])
             peak = jnp.max(scores, axis=1, keepdims=True)
             weights = jnp.exp2(scores * (SCALE * LOG2E) - peak * (SCALE * LOG2E))
@@ -157,9 +158,9 @@
 
 
 def attend(group, rows, keys, swapped):
-    _, count, _, _ = GROUPS[group]
+    low, count, _, _ = GROUPS[group]
     return call(
-        functools.partial(attend_kernel, count),
+        functools.partial(attend_kernel, low, count),
         [shaped((count * ROWS + STAT, HD))] * 4,
         [],
         [*rows, *keys, swapped],
@@ -175,8 +176,8 @@
 
 def combine_kernel(*refs):
     partials = (refs[:4], refs[4:8])
-    residuals, attended = refs[8:12], refs[13:17]
-    middle_ref, turn_ref = refs[17:]
+    residuals, attended = refs[8:12], refs[12:16]
+    middle_ref, turn_ref = refs[16:]
     turn_ref[...] = jnp.zeros_like(turn_ref)
     squares = jnp.zeros((ROWS, HD), F32)
     for group, (low, count, _, _) in enumerate(GROUPS):
@@ -229,7 +230,7 @@
 
 
 def prompt_kernel(
-    info_ref, ids_ref, align_ref, gain_ref, text_ref, after_ref, mixed_ref, own_ref, copy_ref, scale_ref, sem
+    info_ref, ids_ref, align_ref, gain_ref, text_ref, mixed_ref, own_ref, copy_ref, scale_ref, sem
 ):
     start = pl.multiple_of(info_ref[0] * (NQ * HD), HD)
     copy = pltpu.make_async_copy(text_ref.at[:, :, :, pl.ds(start, NQ * HD)], copy_ref, sem)
@@ -246,7 +247,7 @@
     mixed_ref[...] = jnp.dot(selection, copy_ref[1, 1], preferred_element_type=F32).astype(BF)
 
 
-def prompts(info, prompt_ids, word_align, gain, text_kv, after):
+def prompts(info, prompt_ids, word_align, gain, text_kv):
     return call(
         prompt_kernel,
         [
@@ -257,7 +258,7 @@
         ],
         [info],
         [prompt_ids, word_align.reshape(1, TXT), gain.reshape(1, -1)],
-        kept=[(text_kv, pltpu.HBM), (after, pl.ANY)],
+        kept=[(text_kv, pltpu.HBM)],
         scratch=[pltpu.SemaphoreType.DMA],
         flops=2 * TXT * TXT * NQ * HD,
         limit=47,
@@ -342,25 +343,23 @@
     last = shift(last, PLANE, 3, 4)
     residuals = call(split_rows_kernel, [shaped(piece)] * 4, [where], [residual_in[0]])
     residuals = [p if d == 0 else shift(p, PLANE, d, 4) for d, p in enumerate(residuals)]
-    buffers = [shaped((count * ROWS, HD)) for _, count, _, _ in GROUPS for _ in range(2)]
-    packed = call(pack_kernel, buffers, [], [kept, mine, first, over, last])
-    partials, groups = [], []
-    for group, (_, count, row_axis, key_axis) in enumerate(GROUPS):
-        rows, keys = packed[2 * group], packed[2 * group + 1]
-        keys = [keys] + [shift(keys, key_axis, d, 4) for d in (2, 1, 3)]
-        rows = [rows] + [shift(rows, row_axis, d, 4) for d in (2, 1, 3)]
-        held = call(repack_kernel, [shaped((4 * count * ROWS, HD))], [], keys)[0]
-        groups.append((rows, keys, shift(held, "c", 1, 2)))
+    buffer = shaped((NQ * ROWS, HD))
+    along_x, along_z = call(pack_kernel, [buffer] * 2, [], [kept, mine, first, over, last])
+    from_x = [along_x] + [shift(along_x, "x", d, 4) for d in (2, 1, 3)]
+    from_z = [along_z] + [shift(along_z, "z", d, 4) for d in (2, 1, 3)]
+    mixed, own, text, gain = prompts(info, prompt_ids, word_align, cross_gain, text_kv)
+    held = call(repack_kernel, [shaped((4 * NQ * ROWS, HD))], [], [*from_x, *from_z], kept=[(own, pl.ANY)])[0]
+    swapped = shift(held, "c", 1, 2)
+    groups = ((from_x, from_z, swapped), (from_z, from_x, swapped))
+    partials = []
     for group, (_, _, row_axis, _) in enumerate(GROUPS):
         outs = attend(group, *groups[group])
         partials += [outs[0]] + [shift(outs[i], row_axis, -d, 4) for i, d in ((1, 2), (2, 1), (3, 3))]
-    mixed, own, text, gain = prompts(info, prompt_ids, word_align, cross_gain, text_kv, outs[0])
     combined = call(
         combine_kernel,
         [shaped((NQ + 1, TOK, HD))] * 4 + [shaped((NQ, 4, TOK, HD), F32)],
         [],
         [*partials, *residuals],
-        kept=[(own, pl.ANY)],
         scratch=[pltpu.VMEM((HD, 2 * HD), F32)],
     )
     middle = combined[4]

time: 99.4 us -> 86.9 us (0.87)
  the two profiles are of different devices: /device:TPU:24 before, /device:TPU:0 now
where the time goes in v1:
time: 86.9 us; the launch traced here: 86.6 us
  starting transfers between devices  39.5 us (45%)
  waiting for transfers between devices  22.2 us (26%)
  Pallas kernels  20 us (23%)
  local copies, waits for them, and re-layouts  3.98 us (5%)
    ppermute x25, starting transfers between devices, shift(): lax.ppermute(value, axis, [(i, (i + distance) % size) for i in range(size)])  39.5 us
    ppermute x25, waiting for transfers between devices, shift(): lax.ppermute(value, axis, [(i, (i + distance) % size) for i in range(size)])  22.2 us
    pallas_call x12, Pallas kernels, call(): pl.pallas_call(kernel, out_shape=out_shapes, in_specs=in_specs, out_specs...  20 us
    unnamed x10, local copies, waits for them, and re-layouts  3.28 us
  transfers between devices with their start and end apart: 25, of which 14 were waited for; matrix products, arithmetic and copies ran while one was open for 1% of the time, Pallas kernels for 18%

profile of v1, /device:TPU:0, one launch (start us, length us, event | category | flops | bytes accessed | tf_op | source)
XLA Modules:
  0.0 86.6 jit_solution(14884340764564558694)
XLA Ops:
  0.6 0.9 %copy-done.1 = bf16[1,56,2560]{2,1,0:T(8,128)(2,1)S(1)} copy-done((bf16[1,56,2560]{2,1,0:T(8,128)(2,1)S(1)}, bf16[1,56,2560]{2,1,0:T(8,128)(2,1)}, u32[]{:S(2)}) %copy-start.1) | copy-done | bytes 286744
  1.6 1.0 %copy-done.2 = bf16[2,56,1280]{2,1,0:T(8,128)(2,1)S(1)} copy-done((bf16[2,56,1280]{2,1,0:T(8,128)(2,1)S(1)}, bf16[2,56,1280]{2,1,0:T(8,128)(2,1)}, u32[]{:S(2)}) %copy-start.2) | copy-done | bytes 286744
  2.7 3.4 %collective-permute-start.1 = (bf16[15,56,128]{2,1,0:T(8,128)(2,1)S(1)}, bf16[15,56,128]{2,1,0:T(8,128)(2,1)S(1)}, u32[]{:S(2)}, u32[]{:S(2)}) collective-permute-start(bf16[15,56,128]{2,1,0:T(8,128)(2,1)S(1)} %get-tuple-element.37), channel_id=1, source_target_pairs={{0,16},{1,17},{16,0},{17,1},{2,18},{3,19},{18,2},{19,3},{4,20},{5,... | collective-permute-start | bytes 645128 | tf_op jit(solution)/shard_map/ppermute | solution.py:28
  6.1 0.7 collective-permute-start
  6.7 2.6 %collective-permute-start.2 = (bf16[5,56,128]{2,1,0:T(8,128)(2,1)S(1)}, bf16[5,56,128]{2,1,0:T(8,128)(2,1)S(1)}, u32[]{:S(2)}, u32[]{:S(2)}) collective-permute-start(bf16[5,56,128]{2,1,0:T(8,128)(2,1)S(1)} %get-tuple-element.38), channel_id=1, source_target_pairs={{0,17},{1,0},{16,1},{17,16},{2,19},{3,2},{18,3},{19,18},{4,21},{5,... | collective-permute-start | bytes 215048 | tf_op jit(solution)/shard_map/ppermute | solution.py:28
  9.3 3.6 %collective-permute-done.first = bf16[5,56,128]{2,1,0:T(8,128)(2,1)S(1)} collective-permute-done((bf16[5,56,128]{2,1,0:T(8,128)(2,1)S(1)}, bf16[5,56,128]{2,1,0:T(8,128)(2,1)S(1)}, u32[]{:S(2)}, u32[]{:S(2)}) %collective-permute-start) | collective-permute-done | bytes 71712 | tf_op jit(solution)/shard_map/ppermute | solution.py:28
  12.9 0.4 collective-permute-done.2.last
  13.4 3.1 %collective-permute-start.3 = (bf16[1120,128]{1,0:T(8,128)(2,1)S(1)}, bf16[1120,128]{1,0:T(8,128)(2,1)S(1)}, u32[]{:S(2)}, u32[]{:S(2)}) collective-permute-start(bf16[1120,128]{1,0:T(8,128)(2,1)S(1)} %get-tuple-element.39.refs_0_.refs_4_), channel_id=1, source_target_pairs={{0,8},{4,12},{8,0},{12,4},{1,9},{5,13},{9,1},{13,5},{2,10},{6,14},... | collective-permute-start | bytes 860168 | tf_op jit(solution)/shard_map/ppermute | solution.py:28
  16.5 0.6 collective-permute-start.4
  17.1 2.6 %collective-permute-start.5 = (bf16[1120,128]{1,0:T(8,128)(2,1)S(1)}, bf16[1120,128]{1,0:T(8,128)(2,1)S(1)}, u32[]{:S(2)}, u32[]{:S(2)}) collective-permute-start(bf16[1120,128]{1,0:T(8,128)(2,1)S(1)} %get-tuple-element.39.refs_0_.refs_4_), channel_id=1, source_target_pairs={{0,12},{4,0},{8,4},{12,8},{1,13},{5,1},{9,5},{13,9},{2,14},{6,2},{... | collective-permute-start | bytes 860168 | tf_op jit(solution)/shard_map/ppermute | solution.py:28
  19.7 3.9 %collective-permute-start.6 = (bf16[1120,128]{1,0:T(8,128)(2,1)S(1)}, bf16[1120,128]{1,0:T(8,128)(2,1)S(1)}, u32[]{:S(2)}, u32[]{:S(2)}) collective-permute-start(bf16[1120,128]{1,0:T(8,128)(2,1)S(1)} %get-tuple-element.40.refs_4_.refs_0_), channel_id=1, source_target_pairs={{0,64},{32,96},{64,0},{96,32},{1,65},{33,97},{65,1},{97,33},{2,66}... | collective-permute-start | bytes 860168 | tf_op jit(solution)/shard_map/ppermute | solution.py:28
  23.6 1.0 %collective-permute-start.7 = (bf16[1120,128]{1,0:T(8,128)(2,1)S(1)}, bf16[1120,128]{1,0:T(8,128)(2,1)S(1)}, u32[]{:S(2)}, u32[]{:S(2)}) collective-permute-start(bf16[1120,128]{1,0:T(8,128)(2,1)S(1)} %get-tuple-element.40.refs_4_.refs_0_), channel_id=1, source_target_pairs={{0,32},{32,64},{64,96},{96,0},{1,33},{33,65},{65,97},{97,1},{2,34}... | collective-permute-start | bytes 860168 | tf_op jit(solution)/shard_map/ppermute | solution.py:28
  24.7 4.0 %collective-permute-start.8 = (bf16[1120,128]{1,0:T(8,128)(2,1)S(1)}, bf16[1120,128]{1,0:T(8,128)(2,1)S(1)}, u32[]{:S(2)}, u32[]{:S(2)}) collective-permute-start(bf16[1120,128]{1,0:T(8,128)(2,1)S(1)} %get-tuple-element.40.refs_4_.refs_0_), channel_id=1, source_target_pairs={{0,96},{32,0},{64,32},{96,64},{1,97},{33,1},{65,33},{97,65},{2,98}... | collective-permute-start | bytes 860168 | tf_op jit(solution)/shard_map/ppermute | solution.py:28
  28.8 0.7 reshape.15.gain_ref
  29.6 0.7 copy-done.3
  30.2 0.7 copy-done.4
  30.9 2.9 %shard_map.88 = (bf16[512,640]{1,0:T(8,128)(2,1)S(1)}, f32[8,512]{1,0:T(8,128)S(1)}, bf16[2,2,512,640]{3,2,1,0:T(8,128)(2,1)S(1)}, f32[8,640]{1,0:T(8,128)S(1)}) custom-call(s32[2]{0:T(128)S(1)} %pad_add_fusion.info_ref, s32[2,512]{1,0:T(2,128)S(1)} %copy-done.3, s32[1,512]{1,0:T(1,128)S(1)} %bitcast.9, bf16[1,2560]{1,0:T(2,128)(2,1)S(1)} %reshape.15.gain_ref, ...), custom_call_target="tpu_custom_call" | custom-call | flops 335544320 | bytes 3324928 | tf_op jit(solution)/shard_map/pallas_call | solution.py:48
  33.8 1.6 %collective-permute-done.7.refs_6_.refs_2_ = bf16[1120,128]{1,0:T(8,128)(2,1)S(1)} collective-permute-done((bf16[1120,128]{1,0:T(8,128)(2,1)S(1)}, bf16[1120,128]{1,0:T(8,128)(2,1)S(1)}, u32[]{:S(2)}, u32[]{:S(2)}) %collective-permute-start.7) | collective-permute-done | bytes 286752 | tf_op jit(solution)/shard_map/ppermute | solution.py:28
  35.4 0.7 collective-permute-done.8.refs_7_.refs_3_
  36.4 1.8 %collective-permute-start.16 = (bf16[5,56,128]{2,1,0:T(8,128)(2,1)S(1)}, bf16[5,56,128]{2,1,0:T(8,128)(2,1)S(1)}, u32[]{:S(2)}, u32[]{:S(2)}) collective-permute-start(bf16[5,56,128]{2,1,0:T(8,128)(2,1)S(1)} %get-tuple-element.51), channel_id=1, source_target_pairs={{0,1},{1,16},{16,17},{17,0},{2,3},{3,18},{18,19},{19,2},{4,5},{5,2... | collective-permute-start | bytes 215048 | tf_op jit(solution)/shard_map/ppermute | solution.py:28
  38.3 2.6 %collective-permute-start.17 = (bf16[5,56,128]{2,1,0:T(8,128)(2,1)S(1)}, bf16[5,56,128]{2,1,0:T(8,128)(2,1)S(1)}, u32[]{:S(2)}, u32[]{:S(2)}) collective-permute-start(bf16[5,56,128]{2,1,0:T(8,128)(2,1)S(1)} %get-tuple-element.52), channel_id=1, source_target_pairs={{0,16},{1,17},{16,0},{17,1},{2,18},{3,19},{18,2},{19,3},{4,20},{5,... | collective-permute-start | bytes 215048 | tf_op jit(solution)/shard_map/ppermute | solution.py:28
  40.9 0.2 collective-permute-start.18
  41.0 4.2 %shard_map.91 = (bf16[480,128]{1,0:T(8,128)(2,1)S(1)}, bf16[480,128]{1,0:T(8,128)(2,1)S(1)}, bf16[480,128]{1,0:T(8,128)(2,1)S(1)}, bf16[480,128]{1,0:T(8,128)(2,1)S(1)}) custom-call(bf16[1120,128]{1,0:T(8,128)(2,1)S(1)} %get-tuple-element.40.refs_4_.refs_0_, bf16[1120,128]{1,0:T(8,128)(2,1)S(1)} %collective-permute-done.6.refs_5_.refs_1_, ...), custom_call_target="tpu_custom_call" | custom-call | flops 822083584 | bytes 3932160 | tf_op jit(solution)/shard_map/pallas_call | solution.py:48
  45.3 2.1 %collective-permute-start.13 = (bf16[480,128]{1,0:T(8,128)(2,1)S(1)}, bf16[480,128]{1,0:T(8,128)(2,1)S(1)}, u32[]{:S(2)}, u32[]{:S(2)}) collective-permute-start(bf16[480,128]{1,0:T(8,128)(2,1)S(1)} %get-tuple-element.47), channel_id=1, source_target_pairs={{0,64},{32,96},{64,0},{96,32},{1,65},{33,97},{65,1},{97,33},{2,66}... | collective-permute-start | bytes 368648 | tf_op jit(solution)/shard_map/ppermute | solution.py:28
  47.4 6.3 %shard_map.90 = (bf16[704,128]{1,0:T(8,128)(2,1)S(1)}, bf16[704,128]{1,0:T(8,128)(2,1)S(1)}, bf16[704,128]{1,0:T(8,128)(2,1)S(1)}, bf16[704,128]{1,0:T(8,128)(2,1)S(1)}) custom-call(bf16[1120,128]{1,0:T(8,128)(2,1)S(1)} %get-tuple-element.39.refs_0_.refs_4_, bf16[1120,128]{1,0:T(8,128)(2,1)S(1)} %collective-permute-done.3.refs_1_.refs_5_, ...), custom_call_target="tpu_custom_call" | custom-call | flops 1233125376 | bytes 4161536 | tf_op jit(solution)/shard_map/pallas_call | solution.py:48
  53.7 0.3 collective-permute-start.10
  54.0 1.8 %collective-permute-start.11 = (bf16[704,128]{1,0:T(8,128)(2,1)S(1)}, bf16[704,128]{1,0:T(8,128)(2,1)S(1)}, u32[]{:S(2)}, u32[]{:S(2)}) collective-permute-start(bf16[704,128]{1,0:T(8,128)(2,1)S(1)} %get-tuple-element.44), channel_id=1, source_target_pairs={{0,12},{4,0},{8,4},{12,8},{1,13},{5,1},{9,5},{13,9},{2,14},{6,2},{... | collective-permute-start | bytes 540680 | tf_op jit(solution)/shard_map/ppermute | solution.py:28
  55.8 0.2 collective-permute-start.12
  56.0 1.5 %collective-permute-start.14 = (bf16[480,128]{1,0:T(8,128)(2,1)S(1)}, bf16[480,128]{1,0:T(8,128)(2,1)S(1)}, u32[]{:S(2)}, u32[]{:S(2)}) collective-permute-start(bf16[480,128]{1,0:T(8,128)(2,1)S(1)} %get-tuple-element.48), channel_id=1, source_target_pairs={{0,96},{32,0},{64,32},{96,64},{1,97},{33,1},{65,33},{97,65},{2,98}... | collective-permute-start | bytes 368648 | tf_op jit(solution)/shard_map/ppermute | solution.py:28
  57.5 1.0 %collective-permute-start.15 = (bf16[480,128]{1,0:T(8,128)(2,1)S(1)}, bf16[480,128]{1,0:T(8,128)(2,1)S(1)}, u32[]{:S(2)}, u32[]{:S(2)}) collective-permute-start(bf16[480,128]{1,0:T(8,128)(2,1)S(1)} %get-tuple-element.49), channel_id=1, source_target_pairs={{0,32},{32,64},{64,96},{96,0},{1,33},{33,65},{65,97},{97,1},{2,34}... | collective-permute-start | bytes 368648 | tf_op jit(solution)/shard_map/ppermute | solution.py:28
  58.5 2.6 %collective-permute-done.14.refs_6_ = bf16[480,128]{1,0:T(8,128)(2,1)S(1)} collective-permute-done((bf16[480,128]{1,0:T(8,128)(2,1)S(1)}, bf16[480,128]{1,0:T(8,128)(2,1)S(1)}, u32[]{:S(2)}, u32[]{:S(2)}) %collective-permute-start.14) | collective-permute-done | bytes 122912 | tf_op jit(solution)/shard_map/ppermute | solution.py:28
  61.1 2.5 %collective-permute-done.15.refs_7_ = bf16[480,128]{1,0:T(8,128)(2,1)S(1)} collective-permute-done((bf16[480,128]{1,0:T(8,128)(2,1)S(1)}, bf16[480,128]{1,0:T(8,128)(2,1)S(1)}, u32[]{:S(2)}, u32[]{:S(2)}) %collective-permute-start.15) | collective-permute-done | bytes 122912 | tf_op jit(solution)/shard_map/ppermute | solution.py:28
  63.6 1.6 %collective-permute-done.12.refs_3_ = bf16[704,128]{1,0:T(8,128)(2,1)S(1)} collective-permute-done((bf16[704,128]{1,0:T(8,128)(2,1)S(1)}, bf16[704,128]{1,0:T(8,128)(2,1)S(1)}, u32[]{:S(2)}, u32[]{:S(2)}) %collective-permute-start.12) | collective-permute-done | bytes 180256 | tf_op jit(solution)/shard_map/ppermute | solution.py:28
  65.2 1.6 %shard_map.93 = (bf16[6,56,128]{2,1,0:T(8,128)(2,1)S(1)}, bf16[6,56,128]{2,1,0:T(8,128)(2,1)S(1)}, bf16[6,56,128]{2,1,0:T(8,128)(2,1)S(1)}, bf16[6,56,128]{2,1,0:T(8,128)(2,1)S(1)}, f32[5,4,56,128]{3,2,1,0:T(8,128)S(1)}) custom-call(bf16[704,128]{1,0:T(8,128)(2,1)S(1)} %get-tuple-element.42.refs_0_, bf16[704,128]{1,0:T(8,128)(2,1)S(1)} %collective-permute-done.10.refs_1_, ...), custom_call_target="tpu_custom_call" | custom-call | bytes 2416640 | tf_op jit(solution)/shard_map/pallas_call | solution.py:48
  66.7 1.3 %collective-permute-start.19 = (bf16[6,56,128]{2,1,0:T(8,128)(2,1)S(1)}, bf16[6,56,128]{2,1,0:T(8,128)(2,1)S(1)}, u32[]{:S(2)}, u32[]{:S(2)}) collective-permute-start(bf16[6,56,128]{2,1,0:T(8,128)(2,1)S(1)} %get-tuple-element.55), channel_id=1, source_target_pairs={{0,17},{1,0},{16,1},{17,16},{2,19},{3,2},{18,3},{19,18},{4,21},{5,... | collective-permute-start | bytes 258056 | tf_op jit(solution)/shard_map/ppermute | solution.py:28
  68.0 2.4 %collective-permute-start.20 = (bf16[6,56,128]{2,1,0:T(8,128)(2,1)S(1)}, bf16[6,56,128]{2,1,0:T(8,128)(2,1)S(1)}, u32[]{:S(2)}, u32[]{:S(2)}) collective-permute-start(bf16[6,56,128]{2,1,0:T(8,128)(2,1)S(1)} %get-tuple-element.56), channel_id=1, source_target_pairs={{0,16},{1,17},{16,0},{17,1},{2,18},{3,19},{18,2},{19,3},{4,20},{5,... | collective-permute-start | bytes 258056 | tf_op jit(solution)/shard_map/ppermute | solution.py:28
  70.5 1.0 %shard_map.95.scores_ref = f32[2,5,112,512]{3,2,1,0:T(8,128)S(1)} custom-call(s32[2]{0:T(128)S(1)} %pad_add_fusion.info_ref, f32[5,4,56,128]{3,2,1,0:T(8,128)S(1)} %get-tuple-element.58.middle_ref, f32[8,640]{1,0:T(8,128)S(1)} %get-tuple-element.59.gain_ref, bf16[2,2,512,640]{3,2,1,0:T(8,128)(2,1)S(1)} %get-tuple-element.60.text_ref), custom_call_target="tpu_custom_call" | custom-call | flops 146800640 | bytes 5509120 | tf_op jit(solution)/shard_map/pallas_call | solution.py:48
  71.5 0.5 collective-permute-done.19.refs_1_.s1
  72.0 2.8 %collective-permute-done.20.refs_2_.s2 = bf16[6,56,128]{2,1,0:T(8,128)(2,1)S(1)} collective-permute-done((bf16[6,56,128]{2,1,0:T(8,128)(2,1)S(1)}, bf16[6,56,128]{2,1,0:T(8,128)(2,1)S(1)}, u32[]{:S(2)}, u32[]{:S(2)}) %collective-permute-start.20) | collective-permute-done | bytes 86048 | tf_op jit(solution)/shard_map/ppermute | solution.py:28
  74.7 1.4 %collective-permute-done.21.refs_3_.s3 = bf16[6,56,128]{2,1,0:T(8,128)(2,1)S(1)} collective-permute-done((bf16[6,56,128]{2,1,0:T(8,128)(2,1)S(1)}, bf16[6,56,128]{2,1,0:T(8,128)(2,1)S(1)}, u32[]{:S(2)}, u32[]{:S(2)}) %collective-permute-start.21) | collective-permute-done | bytes 86048 | tf_op jit(solution)/shard_map/ppermute | solution.py:28
  76.2 2.1 %shard_map.96 = (bf16[5,56,128]{2,1,0:T(8,128)(2,1)S(1)}, bf16[5,56,128]{2,1,0:T(8,128)(2,1)S(1)}, bf16[5,56,128]{2,1,0:T(8,128)(2,1)S(1)}, bf16[5,56,128]{2,1,0:T(8,128)(2,1)S(1)}) custom-call(s32[2]{0:T(128)S(1)} %pad_add_fusion.info_ref, bf16[6,56,128]{2,1,0:T(8,128)(2,1)S(1)} %get-tuple-element.54.refs_0_.s0, ...), custom_call_target="tpu_custom_call" | custom-call | flops 220200960 | bytes 6791168 | tf_op jit(solution)/shard_map/pallas_call | solution.py:48
  78.4 1.9 %collective-permute-start.23 = (bf16[5,56,128]{2,1,0:T(8,128)(2,1)S(1)}, bf16[5,56,128]{2,1,0:T(8,128)(2,1)S(1)}, u32[]{:S(2)}, u32[]{:S(2)}) collective-permute-start(bf16[5,56,128]{2,1,0:T(8,128)(2,1)S(1)} %get-tuple-element.64), channel_id=1, source_target_pairs={{0,16},{1,17},{16,0},{17,1},{2,18},{3,19},{18,2},{19,3},{4,20},{5,... | collective-permute-start | bytes 215048 | tf_op jit(solution)/shard_map/ppermute | solution.py:28
  80.3 0.3 collective-permute-start.24
  80.6 0.8 shard_map.94
  81.4 1.3 %collective-permute-done.22.refs_1_ = bf16[5,56,128]{2,1,0:T(8,128)(2,1)S(1)} collective-permute-done((bf16[5,56,128]{2,1,0:T(8,128)(2,1)S(1)}, bf16[5,56,128]{2,1,0:T(8,128)(2,1)S(1)}, u32[]{:S(2)}, u32[]{:S(2)}) %collective-permute-start.22) | collective-permute-done | bytes 71712 | tf_op jit(solution)/shard_map/ppermute | solution.py:28
  82.7 2.0 %collective-permute-done.23.refs_2_ = bf16[5,56,128]{2,1,0:T(8,128)(2,1)S(1)} collective-permute-done((bf16[5,56,128]{2,1,0:T(8,128)(2,1)S(1)}, bf16[5,56,128]{2,1,0:T(8,128)(2,1)S(1)}, u32[]{:S(2)}, u32[]{:S(2)}) %collective-permute-start.23) | collective-permute-done | bytes 71712 | tf_op jit(solution)/shard_map/ppermute | solution.py:28
  84.7 1.1 %collective-permute-done.24.refs_3_ = bf16[5,56,128]{2,1,0:T(8,128)(2,1)S(1)} collective-permute-done((bf16[5,56,128]{2,1,0:T(8,128)(2,1)S(1)}, bf16[5,56,128]{2,1,0:T(8,128)(2,1)S(1)}, u32[]{:S(2)}, u32[]{:S(2)}) %collective-permute-start.24) | collective-permute-done | bytes 71712 | tf_op jit(solution)/shard_map/ppermute | solution.py:28
  85.8 0.8 shard_map.97
  (26 shorter events, 0.8 us)
Async XLA Ops:
  0.6 1.0 %copy-start.1 = (bf16[1,56,2560]{2,1,0:T(8,128)(2,1)S(1)}, bf16[1,56,2560]{2,1,0:T(8,128)(2,1)}, u32[]{:S(2)}) copy-start(bf16[1,56,2560]{2,1,0:T(8,128)(2,1)} %param.7) | copy-start | bytes 860164
  1.6 1.0 %copy-start.2 = (bf16[2,56,1280]{2,1,0:T(8,128)(2,1)S(1)}, bf16[2,56,1280]{2,1,0:T(8,128)(2,1)}, u32[]{:S(2)}) copy-start(bf16[2,56,1280]{2,1,0:T(8,128)(2,1)} %kv_ref.1) | copy-start | bytes 860164
  2.7 10.6 %collective-permute-start.1 = (bf16[15,56,128]{2,1,0:T(8,128)(2,1)S(1)}, bf16[15,56,128]{2,1,0:T(8,128)(2,1)S(1)}, u32[]{:S(2)}, u32[]{:S(2)}) collective-permute-start(bf16[15,56,128]{2,1,0:T(8,128)(2,1)S(1)} %get-tuple-element.37), channel_id=1, source_target_pairs={{0,16},{1,17},{16,0},{17,1},{2,18},{3,19},{18,2},{19,3},{4,20},{5,... | collective-permute-start | bytes 645128 | tf_op jit(solution)/shard_map/ppermute | solution.py:28
  6.1 6.8 %collective-permute-start = (bf16[5,56,128]{2,1,0:T(8,128)(2,1)S(1)}, bf16[5,56,128]{2,1,0:T(8,128)(2,1)S(1)}, u32[]{:S(2)}, u32[]{:S(2)}) collective-permute-start(bf16[5,56,128]{2,1,0:T(8,128)(2,1)S(1)} %get-tuple-element.36), channel_id=1, source_target_pairs={{0,1},{1,16},{16,17},{17,0},{2,3},{3,18},{18,19},{19,2},{4,5},{5,2... | collective-permute-start | bytes 215048 | tf_op jit(solution)/shard_map/ppermute | solution.py:28
  6.7 6.5 %collective-permute-start.2 = (bf16[5,56,128]{2,1,0:T(8,128)(2,1)S(1)}, bf16[5,56,128]{2,1,0:T(8,128)(2,1)S(1)}, u32[]{:S(2)}, u32[]{:S(2)}) collective-permute-start(bf16[5,56,128]{2,1,0:T(8,128)(2,1)S(1)} %get-tuple-element.38), channel_id=1, source_target_pairs={{0,17},{1,0},{16,1},{17,16},{2,19},{3,2},{18,3},{19,18},{4,21},{5,... | collective-permute-start | bytes 215048 | tf_op jit(solution)/shard_map/ppermute | solution.py:28
  13.4 11.3 %collective-permute-start.3 = (bf16[1120,128]{1,0:T(8,128)(2,1)S(1)}, bf16[1120,128]{1,0:T(8,128)(2,1)S(1)}, u32[]{:S(2)}, u32[]{:S(2)}) collective-permute-start(bf16[1120,128]{1,0:T(8,128)(2,1)S(1)} %get-tuple-element.39.refs_0_.refs_4_), channel_id=1, source_target_pairs={{0,8},{4,12},{8,0},{12,4},{1,9},{5,13},{9,1},{13,5},{2,10},{6,14},... | collective-permute-start | bytes 860168 | tf_op jit(solution)/shard_map/ppermute | solution.py:28
  16.5 17.3 %collective-permute-start.4 = (bf16[1120,128]{1,0:T(8,128)(2,1)S(1)}, bf16[1120,128]{1,0:T(8,128)(2,1)S(1)}, u32[]{:S(2)}, u32[]{:S(2)}) collective-permute-start(bf16[1120,128]{1,0:T(8,128)(2,1)S(1)} %get-tuple-element.39.refs_0_.refs_4_), channel_id=1, source_target_pairs={{0,4},{4,8},{8,12},{12,0},{1,5},{5,9},{9,13},{13,1},{2,6},{6,10},{... | collective-permute-start | bytes 860168 | tf_op jit(solution)/shard_map/ppermute | solution.py:28
  17.1 16.7 %collective-permute-start.5 = (bf16[1120,128]{1,0:T(8,128)(2,1)S(1)}, bf16[1120,128]{1,0:T(8,128)(2,1)S(1)}, u32[]{:S(2)}, u32[]{:S(2)}) collective-permute-start(bf16[1120,128]{1,0:T(8,128)(2,1)S(1)} %get-tuple-element.39.refs_0_.refs_4_), channel_id=1, source_target_pairs={{0,12},{4,0},{8,4},{12,8},{1,13},{5,1},{9,5},{13,9},{2,14},{6,2},{... | collective-permute-start | bytes 860168 | tf_op jit(solution)/shard_map/ppermute | solution.py:28
  19.7 14.1 %collective-permute-start.6 = (bf16[1120,128]{1,0:T(8,128)(2,1)S(1)}, bf16[1120,128]{1,0:T(8,128)(2,1)S(1)}, u32[]{:S(2)}, u32[]{:S(2)}) collective-permute-start(bf16[1120,128]{1,0:T(8,128)(2,1)S(1)} %get-tuple-element.40.refs_4_.refs_0_), channel_id=1, source_target_pairs={{0,64},{32,96},{64,0},{96,32},{1,65},{33,97},{65,1},{97,33},{2,66}... | collective-permute-start | bytes 860168 | tf_op jit(solution)/shard_map/ppermute | solution.py:28
  23.6 11.8 %collective-permute-start.7 = (bf16[1120,128]{1,0:T(8,128)(2,1)S(1)}, bf16[1120,128]{1,0:T(8,128)(2,1)S(1)}, u32[]{:S(2)}, u32[]{:S(2)}) collective-permute-start(bf16[1120,128]{1,0:T(8,128)(2,1)S(1)} %get-tuple-element.40.refs_4_.refs_0_), channel_id=1, source_target_pairs={{0,32},{32,64},{64,96},{96,0},{1,33},{33,65},{65,97},{97,1},{2,34}... | collective-permute-start | bytes 860168 | tf_op jit(solution)/shard_map/ppermute | solution.py:28
  24.7 11.4 %collective-permute-start.8 = (bf16[1120,128]{1,0:T(8,128)(2,1)S(1)}, bf16[1120,128]{1,0:T(8,128)(2,1)S(1)}, u32[]{:S(2)}, u32[]{:S(2)}) collective-permute-start(bf16[1120,128]{1,0:T(8,128)(2,1)S(1)} %get-tuple-element.40.refs_4_.refs_0_), channel_id=1, source_target_pairs={{0,96},{32,0},{64,32},{96,64},{1,97},{33,1},{65,33},{97,65},{2,98}... | collective-permute-start | bytes 860168 | tf_op jit(solution)/shard_map/ppermute | solution.py:28
  29.6 0.7 copy-start.3
  30.2 0.7 copy-start.4
  33.8 2.5 %copy-start = (bf16[1,56,2560]{2,1,0:T(8,128)(2,1)S(1)}, bf16[1,56,2560]{2,1,0:T(8,128)(2,1)}, u32[]{:S(2)}) copy-start(bf16[1,56,2560]{2,1,0:T(8,128)(2,1)} %param.9) | copy-start | bytes 860164
  36.2 4.8 %collective-permute-start.9 = (bf16[4480,128]{1,0:T(8,128)(2,1)S(1)}, bf16[4480,128]{1,0:T(8,128)(2,1)S(1)}, u32[]{:S(2)}, u32[]{:S(2)}) collective-permute-start(bf16[4480,128]{1,0:T(8,128)(2,1)S(1)} %shard_map.89), channel_id=1, source_target_pairs={{0,2},{2,0},{1,3},{3,1},{4,6},{6,4},{5,7},{7,5},{8,10},{10,8},{9,1... | collective-permute-start | bytes 3440648 | tf_op jit(solution)/shard_map/ppermute | solution.py:28
  36.4 17.5 %collective-permute-start.16 = (bf16[5,56,128]{2,1,0:T(8,128)(2,1)S(1)}, bf16[5,56,128]{2,1,0:T(8,128)(2,1)S(1)}, u32[]{:S(2)}, u32[]{:S(2)}) collective-permute-start(bf16[5,56,128]{2,1,0:T(8,128)(2,1)S(1)} %get-tuple-element.51), channel_id=1, source_target_pairs={{0,1},{1,16},{16,17},{17,0},{2,3},{3,18},{18,19},{19,2},{4,5},{5,2... | collective-permute-start | bytes 215048 | tf_op jit(solution)/shard_map/ppermute | solution.py:28
  38.3 17.5 %collective-permute-start.17 = (bf16[5,56,128]{2,1,0:T(8,128)(2,1)S(1)}, bf16[5,56,128]{2,1,0:T(8,128)(2,1)S(1)}, u32[]{:S(2)}, u32[]{:S(2)}) collective-permute-start(bf16[5,56,128]{2,1,0:T(8,128)(2,1)S(1)} %get-tuple-element.52), channel_id=1, source_target_pairs={{0,16},{1,17},{16,0},{17,1},{2,18},{3,19},{18,2},{19,3},{4,20},{5,... | collective-permute-start | bytes 215048 | tf_op jit(solution)/shard_map/ppermute | solution.py:28
  40.9 15.1 %collective-permute-start.18 = (bf16[5,56,128]{2,1,0:T(8,128)(2,1)S(1)}, bf16[5,56,128]{2,1,0:T(8,128)(2,1)S(1)}, u32[]{:S(2)}, u32[]{:S(2)}) collective-permute-start(bf16[5,56,128]{2,1,0:T(8,128)(2,1)S(1)} %get-tuple-element.53), channel_id=1, source_target_pairs={{0,17},{1,0},{16,1},{17,16},{2,19},{3,2},{18,3},{19,18},{4,21},{5,... | collective-permute-start | bytes 215048 | tf_op jit(solution)/shard_map/ppermute | solution.py:28
  45.3 12.3 %collective-permute-start.13 = (bf16[480,128]{1,0:T(8,128)(2,1)S(1)}, bf16[480,128]{1,0:T(8,128)(2,1)S(1)}, u32[]{:S(2)}, u32[]{:S(2)}) collective-permute-start(bf16[480,128]{1,0:T(8,128)(2,1)S(1)} %get-tuple-element.47), channel_id=1, source_target_pairs={{0,64},{32,96},{64,0},{96,32},{1,65},{33,97},{65,1},{97,33},{2,66}... | collective-permute-start | bytes 368648 | tf_op jit(solution)/shard_map/ppermute | solution.py:28
  53.7 10.0 %collective-permute-start.10 = (bf16[704,128]{1,0:T(8,128)(2,1)S(1)}, bf16[704,128]{1,0:T(8,128)(2,1)S(1)}, u32[]{:S(2)}, u32[]{:S(2)}) collective-permute-start(bf16[704,128]{1,0:T(8,128)(2,1)S(1)} %get-tuple-element.43), channel_id=1, source_target_pairs={{0,8},{4,12},{8,0},{12,4},{1,9},{5,13},{9,1},{13,5},{2,10},{6,14},... | collective-permute-start | bytes 540680 | tf_op jit(solution)/shard_map/ppermute | solution.py:28
  54.0 9.7 %collective-permute-start.11 = (bf16[704,128]{1,0:T(8,128)(2,1)S(1)}, bf16[704,128]{1,0:T(8,128)(2,1)S(1)}, u32[]{:S(2)}, u32[]{:S(2)}) collective-permute-start(bf16[704,128]{1,0:T(8,128)(2,1)S(1)} %get-tuple-element.44), channel_id=1, source_target_pairs={{0,12},{4,0},{8,4},{12,8},{1,13},{5,1},{9,5},{13,9},{2,14},{6,2},{... | collective-permute-start | bytes 540680 | tf_op jit(solution)/shard_map/ppermute | solution.py:28
  55.8 9.4 %collective-permute-start.12 = (bf16[704,128]{1,0:T(8,128)(2,1)S(1)}, bf16[704,128]{1,0:T(8,128)(2,1)S(1)}, u32[]{:S(2)}, u32[]{:S(2)}) collective-permute-start(bf16[704,128]{1,0:T(8,128)(2,1)S(1)} %get-tuple-element.45), channel_id=1, source_target_pairs={{0,4},{4,8},{8,12},{12,0},{1,5},{5,9},{9,13},{13,1},{2,6},{6,10},{... | collective-permute-start | bytes 540680 | tf_op jit(solution)/shard_map/ppermute | solution.py:28
  56.0 5.1 %collective-permute-start.14 = (bf16[480,128]{1,0:T(8,128)(2,1)S(1)}, bf16[480,128]{1,0:T(8,128)(2,1)S(1)}, u32[]{:S(2)}, u32[]{:S(2)}) collective-permute-start(bf16[480,128]{1,0:T(8,128)(2,1)S(1)} %get-tuple-element.48), channel_id=1, source_target_pairs={{0,96},{32,0},{64,32},{96,64},{1,97},{33,1},{65,33},{97,65},{2,98}... | collective-permute-start | bytes 368648 | tf_op jit(solution)/shard_map/ppermute | solution.py:28
  57.5 6.1 %collective-permute-start.15 = (bf16[480,128]{1,0:T(8,128)(2,1)S(1)}, bf16[480,128]{1,0:T(8,128)(2,1)S(1)}, u32[]{:S(2)}, u32[]{:S(2)}) collective-permute-start(bf16[480,128]{1,0:T(8,128)(2,1)S(1)} %get-tuple-element.49), channel_id=1, source_target_pairs={{0,32},{32,64},{64,96},{96,0},{1,33},{33,65},{65,97},{97,1},{2,34}... | collective-permute-start | bytes 368648 | tf_op jit(solution)/shard_map/ppermute | solution.py:28
  66.7 5.2 %collective-permute-start.19 = (bf16[6,56,128]{2,1,0:T(8,128)(2,1)S(1)}, bf16[6,56,128]{2,1,0:T(8,128)(2,1)S(1)}, u32[]{:S(2)}, u32[]{:S(2)}) collective-permute-start(bf16[6,56,128]{2,1,0:T(8,128)(2,1)S(1)} %get-tuple-element.55), channel_id=1, source_target_pairs={{0,17},{1,0},{16,1},{17,16},{2,19},{3,2},{18,3},{19,18},{4,21},{5,... | collective-permute-start | bytes 258056 | tf_op jit(solution)/shard_map/ppermute | solution.py:28
  68.0 6.7 %collective-permute-start.20 = (bf16[6,56,128]{2,1,0:T(8,128)(2,1)S(1)}, bf16[6,56,128]{2,1,0:T(8,128)(2,1)S(1)}, u32[]{:S(2)}, u32[]{:S(2)}) collective-permute-start(bf16[6,56,128]{2,1,0:T(8,128)(2,1)S(1)} %get-tuple-element.56), channel_id=1, source_target_pairs={{0,16},{1,17},{16,0},{17,1},{2,18},{3,19},{18,2},{19,3},{4,20},{5,... | collective-permute-start | bytes 258056 | tf_op jit(solution)/shard_map/ppermute | solution.py:28
  70.5 5.7 %collective-permute-start.21 = (bf16[6,56,128]{2,1,0:T(8,128)(2,1)S(1)}, bf16[6,56,128]{2,1,0:T(8,128)(2,1)S(1)}, u32[]{:S(2)}, u32[]{:S(2)}) collective-permute-start(bf16[6,56,128]{2,1,0:T(8,128)(2,1)S(1)} %get-tuple-element.57), channel_id=1, source_target_pairs={{0,1},{1,16},{16,17},{17,0},{2,3},{3,18},{18,19},{19,2},{4,5},{5,2... | collective-permute-start | bytes 258056 | tf_op jit(solution)/shard_map/ppermute | solution.py:28
  78.3 4.4 %collective-permute-start.22 = (bf16[5,56,128]{2,1,0:T(8,128)(2,1)S(1)}, bf16[5,56,128]{2,1,0:T(8,128)(2,1)S(1)}, u32[]{:S(2)}, u32[]{:S(2)}) collective-permute-start(bf16[5,56,128]{2,1,0:T(8,128)(2,1)S(1)} %get-tuple-element.63), channel_id=1, source_target_pairs={{0,17},{1,0},{16,1},{17,16},{2,19},{3,2},{18,3},{19,18},{4,21},{5,... | collective-permute-start | bytes 215048 | tf_op jit(solution)/shard_map/ppermute | solution.py:28
  78.4 6.4 %collective-permute-start.23 = (bf16[5,56,128]{2,1,0:T(8,128)(2,1)S(1)}, bf16[5,56,128]{2,1,0:T(8,128)(2,1)S(1)}, u32[]{:S(2)}, u32[]{:S(2)}) collective-permute-start(bf16[5,56,128]{2,1,0:T(8,128)(2,1)S(1)} %get-tuple-element.64), channel_id=1, source_target_pairs={{0,16},{1,17},{16,0},{17,1},{2,18},{3,19},{18,2},{19,3},{4,20},{5,... | collective-permute-start | bytes 215048 | tf_op jit(solution)/shard_map/ppermute | solution.py:28
  80.3 5.5 %collective-permute-start.24 = (bf16[5,56,128]{2,1,0:T(8,128)(2,1)S(1)}, bf16[5,56,128]{2,1,0:T(8,128)(2,1)S(1)}, u32[]{:S(2)}, u32[]{:S(2)}) collective-permute-start(bf16[5,56,128]{2,1,0:T(8,128)(2,1)S(1)} %get-tuple-element.65), channel_id=1, source_target_pairs={{0,1},{1,16},{16,17},{17,0},{2,3},{3,18},{18,19},{19,2},{4,5},{5,2... | collective-permute-start | bytes 215048 | tf_op jit(solution)/shard_map/ppermute | solution.py:28

commit v2 on v0

--- a/solution.py
+++ b/solution.py
@@ -40,7 +40,7 @@
     return [pl.BlockSpec(memory_space=pltpu.VMEM) for _ in range(count)]
 
 
-def call(kernel, out_shapes, scalars, operands, kept=(), scratch=(), flops=0, exps=0, limit=40):
+def call(kernel, out_shapes, scalars, operands, kept=(), scratch=(), flops=0, exps=0, limit=16):
     in_specs = [pl.BlockSpec(memory_space=pltpu.SMEM)] * len(scalars) + vmem(len(operands))
     in_specs += [pl.BlockSpec(memory_space=space) for _, space in kept]
     moved = sum(math.prod(o.shape) * o.dtype.itemsize for o in operands)
@@ -64,20 +64,71 @@
     return jnp.concatenate([part.astype(F32) for part in parts], axis=0).astype(BF)
 
 
-def split_kernel(plane_ref, rows_ref, kv_ref, kept, first, last, across, own):
+LOW, WIDE, NARROW = GROUPS[1][0], GROUPS[0][1], GROUPS[1][1]
+
+
+def split_kernel(plane_ref, rows_ref, kv_ref, along_x, along_z, first, last, across):
     high = plane_ref[0] // 2
-    outs = (own, first, across, last)
     for distance in range(4):
         plane = lax.rem(plane_ref[0] + distance, 4)
         for head in range(NQ):
             lane = pl.multiple_of((first_head(plane) + head) * HD, HD)
-            outs[distance][head] = rows_ref[:, pl.ds(lane, HD)]
+            rows = rows_ref[:, pl.ds(lane, HD)]
+            if distance == 0 and head < LOW:
+                along_x[head] = rows
+            elif distance == 0:
+                along_z[2 * WIDE + head - LOW] = rows
+            else:
+                (first, across, last)[distance - 1][head] = rows
     for head in range(NQ):
         here = pl.multiple_of((high * NQ + head) * HD, HD)
         there = pl.multiple_of(((1 - high) * NQ + head) * HD, HD)
         for which in range(2):
-            kept[2 * head + which] = kv_ref[which, :, pl.ds(here, HD)]
+            rows = kv_ref[which, :, pl.ds(here, HD)]
+            if head < LOW:
+                along_z[2 * head + which] = rows
+            else:
+                along_x[WIDE + 2 * (head - LOW) + which] = rows
             across[NQ + 2 * head + which] = kv_ref[which, :, pl.ds(there, HD)]
+
+
+def pack_kernel(first, across, last, along_x, along_z):
+    for head in range(NQ):
+        for index, query in enumerate((first, across, last)):
+            if head < LOW:
+                along_x[3 * head + index] = query[head]
+            else:
+                along_z[2 * WIDE + 3 * (head - LOW) + index] = query[head]
+        for which in range(2):
+            rows = across[NQ + 2 * head + which]
+            if head < LOW:
+                along_z[2 * head + which] = rows
+            else:
+                along_x[3 * WIDE + 2 * (head - LOW) + which] = rows
+
+
+def order_kernel(*refs):
+    x1, z1, x2, z2, out, rows = refs[:4], refs[4:8], refs[8:12], refs[12:16], refs[16], refs[17]
+    for head in range(NQ):
+        for which in range(2):
+            for index in range(4):
+                if head < LOW:
+                    unit = 2 * head + which
+                    parts = [z1[index][unit], z2[index][unit]]
+                else:
+                    unit = 2 * (head - LOW) + which
+                    parts = [x1[index][WIDE + unit], x2[index][3 * WIDE + unit]]
+                out[2 * head + which, index * KEYS : (index + 1) * KEYS, :] = stacked(parts)
+
+    for head in range(NQ):
+        for index in range(4):
+            if head < LOW:
+                parts = [x1[index][head]] + [x2[index][3 * head + k] for k in range(3)]
+            else:
+                unit = head - LOW
+                parts = [z1[index][2 * WIDE + unit]]
+                parts += [z2[index][2 * WIDE + 3 * unit + k] for k in range(3)]
+            rows[head, index * ROWS : (index + 1) * ROWS, :] = stacked(parts)
 
 
 def split_rows_kernel(plane_ref, rows_ref, *outs):
@@ -86,25 +137,6 @@
         for head in range(NQ):
             lane = pl.multiple_of((first_head(plane) + head) * HD, HD)
             outs[distance][head] = rows_ref[:, pl.ds(lane, HD)]
-
-
-def pack_kernel(kept, own, first, across, last, *outs):
-    queries = (own, first, across, last)
-    for group, (low, count, _, _) in enumerate(GROUPS):
-        rows, keys = outs[2 * group], outs[2 * group + 1]
-        for index in range(count):
-            head = low + index
-            rows[index * ROWS : (index + 1) * ROWS, :] = stacked([query[head] for query in queries])
-            keys[index * ROWS : (index + 1) * ROWS, :] = stacked(
-                [kept[2 * head], across[NQ + 2 * head], kept[2 * head + 1], across[NQ + 2 * head + 1]]
-            )
-
-
-def repack_kernel(*refs):
-    out = refs[4]
-    size = refs[0].shape[0]
-    for index in range(4):
-        out[index * size : (index + 1) * size, :] = refs[index][...]
 
 
 def join_rows_kernel(plane_ref, *refs):
@@ -116,60 +148,55 @@
             out[:, pl.ds(lane, HD)] = pieces[distance][head]
 
 
-def attend_kernel(count, *refs):
-    rows_of, keys_of, swapped = refs[:4], refs[4:8], refs[8]
-    outs, (keys, values, stats) = refs[9:13], refs[13:]
+def attend_kernel(low, count, queries, held, swapped, *refs):
+    outs, (peaks, totals) = refs[:4], refs[4:]
     size = count * ROWS
-    pieces = [(ref, 0) for ref in keys_of] + [(swapped, index * size) for index in range(4)]
     lanes = lax.broadcasted_iota(jnp.int32, (ROWS, HD), 1)
-    stats[...] = jnp.zeros_like(stats)
-
-    def one_head(head, _):
-        for index, (piece, base) in enumerate(pieces):
-            start = pl.multiple_of(base + head * ROWS, 16)
-            keys[pl.ds(index * KEYS, KEYS), :] = piece[pl.ds(start, KEYS), :]
-            values[pl.ds(index * KEYS, KEYS), :] = piece[
-                pl.ds(pl.multiple_of(start + KEYS, 16), KEYS), :
-            ]
-        for index in range(4):
-            start = pl.multiple_of(head * ROWS, 16)
-            scores = dot_t(rows_of[index][pl.ds(start, ROWS), :], keys[...])
-            peak = jnp.max(scores, axis=1, keepdims=True)
-            weights = jnp.exp2(scores * (SCALE * LOG2E) - peak * (SCALE * LOG2E))
-            total = jnp.sum(weights, axis=1, keepdims=True)
-            summed = jnp.dot(weights.astype(BF), values[...], preferred_element_type=F32)
-            outs[index][pl.ds(pl.multiple_of(head * ROWS, 16), ROWS), :] = (summed / total).astype(BF)
-            level = peak * SCALE + jnp.log(total)
-            coarse = level.astype(BF).astype(F32)
-            middle = (level - coarse).astype(BF).astype(F32)
-            fine = level - coarse - middle
-            old = stats[index, 0:ROWS, :]
-            old = jnp.where(lanes == 3 * head, coarse, old)
-            old = jnp.where(lanes == 3 * head + 1, middle, old)
-            stats[index, 0:ROWS, :] = jnp.where(lanes == 3 * head + 2, fine, old)
-        return 0
-
-    lax.fori_loop(0, count, one_head, 0)
+    peaks[...] = jnp.zeros_like(peaks)
+    totals[...] = jnp.ones_like(totals)
+    tiles = [(head, index) for head in range(count) for index in range(4)]
+
+    def whole(head, which):
+        unit = 2 * (low + head) + which
+        return jnp.concatenate([held[unit], swapped[unit]], axis=0)
+
+    def scores_of(head, index):
+        return dot_t(queries[low + head, index * ROWS : (index + 1) * ROWS, :], whole(head, 0))
+
+    scores = scores_of(*tiles[0])
+    for step, (head, index) in enumerate(tiles):
+        ahead = scores_of(*tiles[step + 1]) if step + 1 < len(tiles) else None
+        peak = jnp.max(scores, axis=1, keepdims=True)
+        weights = jnp.exp2(scores * (SCALE * LOG2E) - peak * (SCALE * LOG2E))
+        total = jnp.sum(weights, axis=1, keepdims=True)
+        summed = jnp.dot(weights.astype(BF), whole(head, 1), preferred_element_type=F32)
+        outs[index][head * ROWS : (head + 1) * ROWS, :] = (summed * (1.0 / total)).astype(BF)
+        peaks[index, 0:ROWS, :] = jnp.where(lanes == head, peak, peaks[index, 0:ROWS, :])
+        totals[index, 0:ROWS, :] = jnp.where(lanes == head, total, totals[index, 0:ROWS, :])
+        scores = ahead
     for index in range(4):
-        turned = stats[index].T
+        level = peaks[index] * SCALE + jnp.log(totals[index])
+        coarse = level.astype(BF).astype(F32)
+        middle = (level - coarse).astype(BF).astype(F32)
+        fine = level - coarse - middle
+        places = lax.broadcasted_iota(jnp.int32, level.shape, 1)
+        parts = jnp.where(places < NQ, coarse, pltpu.roll(middle, NQ, 1))
+        turned = jnp.where(places < 2 * NQ, parts, pltpu.roll(fine, 2 * NQ, 1)).T
         outs[index][size : size + 16, :] = turned[0:16, 0:HD].astype(BF)
         outs[index][size + 16 : size + STAT, :] = turned[0:16, HD : 2 * HD].astype(BF)
 
 
-def attend(group, rows, keys, swapped):
-    _, count, _, _ = GROUPS[group]
+def attend(group, queries, held, swapped):
+    low, count, _, _ = GROUPS[group]
     return call(
-        functools.partial(attend_kernel, count),
+        functools.partial(attend_kernel, low, count),
         [shaped((count * ROWS + STAT, HD))] * 4,
         [],
-        [*rows, *keys, swapped],
-        scratch=[
-            pltpu.VMEM((8 * KEYS, HD), BF),
-            pltpu.VMEM((8 * KEYS, HD), BF),
-            pltpu.VMEM((4, 2 * HD, HD), F32),
-        ],
+        [queries, held, swapped],
+        scratch=[pltpu.VMEM((4, 2 * HD, HD), F32)] * 2,
         flops=4 * count * 4 * ROWS * 8 * KEYS * HD,
         exps=count * 4 * ROWS * 8 * KEYS,
+        limit=32,
     )
 
 
@@ -186,7 +213,7 @@
             turn_ref[0:16, 0:HD] = partial[size : size + 16, :].astype(F32)
             turn_ref[0:16, HD : 2 * HD] = partial[size + 16 : size + STAT, :].astype(F32)
             stat = turn_ref[...].T[0:ROWS, :]
-            levels.append(stat + pltpu.roll(stat, HD - 1, 1) + pltpu.roll(stat, HD - 2, 1))
+            levels.append(stat + pltpu.roll(stat, HD - NQ, 1) + pltpu.roll(stat, HD - 2 * NQ, 1))
         peak = functools.reduce(jnp.maximum, levels)
         shares = [jnp.exp(level - peak) for level in levels]
         inverse = 1.0 / sum(shares)
@@ -195,7 +222,7 @@
             head = low + index
             total = sum(
                 partial[index * ROWS : (index + 1) * ROWS, :].astype(F32)
-                * share[:, 3 * index : 3 * index + 1]
+                * share[:, index : index + 1]
                 for partial, share in zip(partials[group], shares)
             )
             middles = []
@@ -331,28 +358,42 @@
     info = jnp.stack([quarter, plane]).astype(jnp.int32)
     piece = (NQ, TOK, HD)
 
-    kept, first, last, over, mine = call(
+    along_x, along_z, first, last, over = call(
         split_kernel,
-        [shaped((2 * NQ, TOK, HD)), shaped(piece), shaped(piece), shaped((3 * NQ, TOK, HD)), shaped(piece)],
+        [
+            shaped((WIDE + 2 * NARROW, TOK, HD)),
+            shaped((2 * WIDE + NARROW, TOK, HD)),
+            shaped(piece),
+            shaped(piece),
+            shaped((3 * NQ, TOK, HD)),
+        ],
         [where],
         [queries[0], keys_values],
     )
+
+    def gathered(value, axis):
+        return [value] + [shift(value, axis, d, 4) for d in (2, 1, 3)]
+
     over = shift(over, PLANE, 2, 4)
     first = shift(first, PLANE, 1, 4)
     last = shift(last, PLANE, 3, 4)
+    units = gathered(along_x, "x") + gathered(along_z, "z")
+    along_x, along_z = call(
+        pack_kernel,
+        [shaped((3 * WIDE + 2 * NARROW, TOK, HD)), shaped((2 * WIDE + 3 * NARROW, TOK, HD))],
+        [],
+        [first, over, last],
+    )
+    units = units + gathered(along_x, "x") + gathered(along_z, "z")
     residuals = call(split_rows_kernel, [shaped(piece)] * 4, [where], [residual_in[0]])
     residuals = [p if d == 0 else shift(p, PLANE, d, 4) for d, p in enumerate(residuals)]
-    buffers = [shaped((count * ROWS, HD)) for _, count, _, _ in GROUPS for _ in range(2)]
-    packed = call(pack_kernel, buffers, [], [kept, mine, first, over, last])
-    partials, groups = [], []
-    for group, (_, count, row_axis, key_axis) in enumerate(GROUPS):
-        rows, keys = packed[2 * group], packed[2 * group + 1]
-        keys = [keys] + [shift(keys, key_axis, d, 4) for d in (2, 1, 3)]
-        rows = [rows] + [shift(rows, row_axis, d, 4) for d in (2, 1, 3)]
-        held = call(repack_kernel, [shaped((4 * count * ROWS, HD))], [], keys)[0]
-        groups.append((rows, keys, shift(held, "c", 1, 2)))
+    held, rows = call(
+        order_kernel, [shaped((2 * NQ, 4 * KEYS, HD)), shaped((NQ, 4 * ROWS, HD))], [], units
+    )
+    swapped = shift(held, "c", 1, 2)
+    partials = []
     for group, (_, _, row_axis, _) in enumerate(GROUPS):
-        outs = attend(group, *groups[group])
+        outs = attend(group, rows, held, swapped)
         partials += [outs[0]] + [shift(outs[i], row_axis, -d, 4) for i, d in ((1, 2), (2, 1), (3, 3))]
     mixed, own, text, gain = prompts(info, prompt_ids, word_align, cross_gain, text_kv, outs[0])
     combined = call(
@@ -387,6 +428,7 @@
         scratch=[pltpu.VMEM((4, TOK, HD), F32), pltpu.VMEM((4, TOK, HD), F32)],
         flops=2 * 3 * KEYS * TXT * NQ * HD,
         exps=2 * KEYS * NQ * TXT,
+        limit=24,
     )
     results = home(results)
     return (join(attended)[None], join(results)[None])

time: 99.4 us -> 89.3 us (0.90)
  the two profiles are of different devices: /device:TPU:24 before, /device:TPU:6 now
where the time goes in v2:
time: 89.3 us; the launch traced here: 89.2 us
  starting transfers between devices  45.7 us (51%)
  waiting for transfers between devices  23.7 us (27%)
  Pallas kernels  17 us (19%)
  local copies, waits for them, and re-layouts  1.97 us (2%)
    ppermute x31, starting transfers between devices, shift(): lax.ppermute(value, axis, [(i, (i + distance) % size) for i in range(size)])  45.7 us
    ppermute x31, waiting for transfers between devices, shift(): lax.ppermute(value, axis, [(i, (i + distance) % size) for i in range(size)])  23.7 us
    pallas_call x12, Pallas kernels, call(): pl.pallas_call(kernel, out_shape=out_shapes, in_specs=in_specs, out_specs...  17 us
    unnamed x12, local copies, waits for them, and re-layouts  1.97 us
  transfers between devices with their start and end apart: 31, of which 12 were waited for; matrix products, arithmetic and copies ran while one was open for 0% of the time, Pallas kernels for 13%

profile of v2, /device:TPU:6, one launch (start us, length us, event | category | flops | bytes accessed | tf_op | source)
XLA Modules:
  0.0 89.2 jit_solution(6446938217732872966)
XLA Ops:
  0.7 1.0 %copy-done.1 = bf16[1,56,2560]{2,1,0:T(8,128)(2,1)S(1)} copy-done((bf16[1,56,2560]{2,1,0:T(8,128)(2,1)S(1)}, bf16[1,56,2560]{2,1,0:T(8,128)(2,1)}, u32[]{:S(2)}) %copy-start.1) | copy-done | bytes 286744
  1.7 1.0 %copy-done.2 = bf16[2,56,1280]{2,1,0:T(8,128)(2,1)S(1)} copy-done((bf16[2,56,1280]{2,1,0:T(8,128)(2,1)S(1)}, bf16[2,56,1280]{2,1,0:T(8,128)(2,1)}, u32[]{:S(2)}) %copy-start.2) | copy-done | bytes 286744
  2.7 3.3 %collective-permute-start.7 = (bf16[15,56,128]{2,1,0:T(8,128)(2,1)S(1)}, bf16[15,56,128]{2,1,0:T(8,128)(2,1)S(1)}, u32[]{:S(2)}, u32[]{:S(2)}) collective-permute-start(bf16[15,56,128]{2,1,0:T(8,128)(2,1)S(1)} %get-tuple-element.39), channel_id=1, source_target_pairs={{0,16},{1,17},{16,0},{17,1},{2,18},{3,19},{18,2},{19,3},{4,20},{5,... | collective-permute-start | bytes 645128 | tf_op jit(solution)/shard_map/ppermute | solution.py:28
  6.0 0.7 collective-permute-start.6
  6.7 2.6 %collective-permute-start.8 = (bf16[5,56,128]{2,1,0:T(8,128)(2,1)S(1)}, bf16[5,56,128]{2,1,0:T(8,128)(2,1)S(1)}, u32[]{:S(2)}, u32[]{:S(2)}) collective-permute-start(bf16[5,56,128]{2,1,0:T(8,128)(2,1)S(1)} %get-tuple-element.40), channel_id=1, source_target_pairs={{0,17},{1,0},{16,1},{17,16},{2,19},{3,2},{18,3},{19,18},{4,21},{5,... | collective-permute-start | bytes 215048 | tf_op jit(solution)/shard_map/ppermute | solution.py:28
  9.2 0.8 collective-permute-start.2
  10.1 2.4 %collective-permute-start.1 = (bf16[7,56,128]{2,1,0:T(8,128)(2,1)S(1)}, bf16[7,56,128]{2,1,0:T(8,128)(2,1)S(1)}, u32[]{:S(2)}, u32[]{:S(2)}) collective-permute-start(bf16[7,56,128]{2,1,0:T(8,128)(2,1)S(1)} %get-tuple-element.36.refs_0_), channel_id=1, source_target_pairs={{0,4},{4,8},{8,12},{12,0},{1,5},{5,9},{9,13},{13,1},{2,6},{6,10},{... | collective-permute-start | bytes 301064 | tf_op jit(solution)/shard_map/ppermute | solution.py:28
  12.5 0.4 collective-permute-done.6.first
  12.9 0.3 collective-permute-done.8.last
  13.3 4.1 %collective-permute-start.14 = (bf16[12,56,128]{2,1,0:T(8,128)(2,1)S(1)}, bf16[12,56,128]{2,1,0:T(8,128)(2,1)S(1)}, u32[]{:S(2)}, u32[]{:S(2)}) collective-permute-start(bf16[12,56,128]{2,1,0:T(8,128)(2,1)S(1)} %get-tuple-element.42.refs_12_), channel_id=1, source_target_pairs={{0,96},{32,0},{64,32},{96,64},{1,97},{33,1},{65,33},{97,65},{2,98}... | collective-permute-start | bytes 516104 | tf_op jit(solution)/shard_map/ppermute | solution.py:28
  17.4 0.4 collective-permute-start.5
  17.8 1.6 %collective-permute-start.4 = (bf16[8,56,128]{2,1,0:T(8,128)(2,1)S(1)}, bf16[8,56,128]{2,1,0:T(8,128)(2,1)S(1)}, u32[]{:S(2)}, u32[]{:S(2)}) collective-permute-start(bf16[8,56,128]{2,1,0:T(8,128)(2,1)S(1)} %get-tuple-element.37.refs_4_), channel_id=1, source_target_pairs={{0,32},{32,64},{64,96},{96,0},{1,33},{33,65},{65,97},{97,1},{2,34}... | collective-permute-start | bytes 344072 | tf_op jit(solution)/shard_map/ppermute | solution.py:28
  19.4 1.5 %collective-permute-start = (bf16[7,56,128]{2,1,0:T(8,128)(2,1)S(1)}, bf16[7,56,128]{2,1,0:T(8,128)(2,1)S(1)}, u32[]{:S(2)}, u32[]{:S(2)}) collective-permute-start(bf16[7,56,128]{2,1,0:T(8,128)(2,1)S(1)} %get-tuple-element.36.refs_0_), channel_id=1, source_target_pairs={{0,8},{4,12},{8,0},{12,4},{1,9},{5,13},{9,1},{13,5},{2,10},{6,14},... | collective-permute-start | bytes 301064 | tf_op jit(solution)/shard_map/ppermute | solution.py:28
  20.9 4.7 %collective-permute-done.refs_1_ = bf16[7,56,128]{2,1,0:T(8,128)(2,1)S(1)} collective-permute-done((bf16[7,56,128]{2,1,0:T(8,128)(2,1)S(1)}, bf16[7,56,128]{2,1,0:T(8,128)(2,1)S(1)}, u32[]{:S(2)}, u32[]{:S(2)}) %collective-permute-start) | collective-permute-done | bytes 100384 | tf_op jit(solution)/shard_map/ppermute | solution.py:28
  25.6 0.8 collective-permute-start.11
  26.5 2.4 %collective-permute-start.10 = (bf16[13,56,128]{2,1,0:T(8,128)(2,1)S(1)}, bf16[13,56,128]{2,1,0:T(8,128)(2,1)S(1)}, u32[]{:S(2)}, u32[]{:S(2)}) collective-permute-start(bf16[13,56,128]{2,1,0:T(8,128)(2,1)S(1)} %get-tuple-element.41.refs_8_), channel_id=1, source_target_pairs={{0,4},{4,8},{8,12},{12,0},{1,5},{5,9},{9,13},{13,1},{2,6},{6,10},{... | collective-permute-start | bytes 559112 | tf_op jit(solution)/shard_map/ppermute | solution.py:28
  29.1 2.5 %collective-permute-start.13 = (bf16[12,56,128]{2,1,0:T(8,128)(2,1)S(1)}, bf16[12,56,128]{2,1,0:T(8,128)(2,1)S(1)}, u32[]{:S(2)}, u32[]{:S(2)}) collective-permute-start(bf16[12,56,128]{2,1,0:T(8,128)(2,1)S(1)} %get-tuple-element.42.refs_12_), channel_id=1, source_target_pairs={{0,32},{32,64},{64,96},{96,0},{1,33},{33,65},{65,97},{97,1},{2,34}... | collective-permute-start | bytes 516104 | tf_op jit(solution)/shard_map/ppermute | solution.py:28
  31.6 2.0 %collective-permute-start.12 = (bf16[12,56,128]{2,1,0:T(8,128)(2,1)S(1)}, bf16[12,56,128]{2,1,0:T(8,128)(2,1)S(1)}, u32[]{:S(2)}, u32[]{:S(2)}) collective-permute-start(bf16[12,56,128]{2,1,0:T(8,128)(2,1)S(1)} %get-tuple-element.42.refs_12_), channel_id=1, source_target_pairs={{0,64},{32,96},{64,0},{96,32},{1,65},{33,97},{65,1},{97,33},{2,66}... | collective-permute-start | bytes 516104 | tf_op jit(solution)/shard_map/ppermute | solution.py:28
  33.7 3.9 %collective-permute-done.13.refs_14_ = bf16[12,56,128]{2,1,0:T(8,128)(2,1)S(1)} collective-permute-done((bf16[12,56,128]{2,1,0:T(8,128)(2,1)S(1)}, bf16[12,56,128]{2,1,0:T(8,128)(2,1)S(1)}, u32[]{:S(2)}, u32[]{:S(2)}) %collective-permute-start.13) | collective-permute-done | bytes 172064 | tf_op jit(solution)/shard_map/ppermute | solution.py:28
  37.5 2.2 %collective-permute-done.12.refs_13_ = bf16[12,56,128]{2,1,0:T(8,128)(2,1)S(1)} collective-permute-done((bf16[12,56,128]{2,1,0:T(8,128)(2,1)S(1)}, bf16[12,56,128]{2,1,0:T(8,128)(2,1)S(1)}, u32[]{:S(2)}, u32[]{:S(2)}) %collective-permute-start.12) | collective-permute-done | bytes 172064 | tf_op jit(solution)/shard_map/ppermute | solution.py:28
  39.7 0.4 shard_map.88
  40.3 2.1 %collective-permute-start.22 = (bf16[5,56,128]{2,1,0:T(8,128)(2,1)S(1)}, bf16[5,56,128]{2,1,0:T(8,128)(2,1)S(1)}, u32[]{:S(2)}, u32[]{:S(2)}) collective-permute-start(bf16[5,56,128]{2,1,0:T(8,128)(2,1)S(1)} %get-tuple-element.54), channel_id=1, source_target_pairs={{0,1},{1,16},{16,17},{17,0},{2,3},{3,18},{18,19},{19,2},{4,5},{5,2... | collective-permute-start | bytes 215048 | tf_op jit(solution)/shard_map/ppermute | solution.py:28
  42.5 2.5 %collective-permute-start.23 = (bf16[5,56,128]{2,1,0:T(8,128)(2,1)S(1)}, bf16[5,56,128]{2,1,0:T(8,128)(2,1)S(1)}, u32[]{:S(2)}, u32[]{:S(2)}) collective-permute-start(bf16[5,56,128]{2,1,0:T(8,128)(2,1)S(1)} %get-tuple-element.55), channel_id=1, source_target_pairs={{0,16},{1,17},{16,0},{17,1},{2,18},{3,19},{18,2},{19,3},{4,20},{5,... | collective-permute-start | bytes 215048 | tf_op jit(solution)/shard_map/ppermute | solution.py:28
  45.0 0.3 collective-permute-start.24
  45.2 3.0 %shard_map.90 = (bf16[480,128]{1,0:T(8,128)(2,1)S(1)}, bf16[480,128]{1,0:T(8,128)(2,1)S(1)}, bf16[480,128]{1,0:T(8,128)(2,1)S(1)}, bf16[480,128]{1,0:T(8,128)(2,1)S(1)}) custom-call(bf16[5,896,128]{2,1,0:T(8,128)(2,1)S(1)} %get-tuple-element.43.queries, bf16[10,448,128]{2,1,0:T(8,128)(2,1)S(1)} %get-tuple-element.44.held, ...), custom_call_target="tpu_custom_call" | custom-call | flops 822083584 | bytes 3932160 | tf_op jit(solution)/shard_map/pallas_call | solution.py:48
  48.3 1.7 %collective-permute-start.19 = (bf16[480,128]{1,0:T(8,128)(2,1)S(1)}, bf16[480,128]{1,0:T(8,128)(2,1)S(1)}, u32[]{:S(2)}, u32[]{:S(2)}) collective-permute-start(bf16[480,128]{1,0:T(8,128)(2,1)S(1)} %get-tuple-element.50), channel_id=1, source_target_pairs={{0,64},{32,96},{64,0},{96,32},{1,65},{33,97},{65,1},{97,33},{2,66}... | collective-permute-start | bytes 368648 | tf_op jit(solution)/shard_map/ppermute | solution.py:28
  49.9 4.2 %shard_map.89 = (bf16[704,128]{1,0:T(8,128)(2,1)S(1)}, bf16[704,128]{1,0:T(8,128)(2,1)S(1)}, bf16[704,128]{1,0:T(8,128)(2,1)S(1)}, bf16[704,128]{1,0:T(8,128)(2,1)S(1)}) custom-call(bf16[5,896,128]{2,1,0:T(8,128)(2,1)S(1)} %get-tuple-element.43.queries, bf16[10,448,128]{2,1,0:T(8,128)(2,1)S(1)} %get-tuple-element.44.held, ...), custom_call_target="tpu_custom_call" | custom-call | flops 1233125376 | bytes 4161536 | tf_op jit(solution)/shard_map/pallas_call | solution.py:48
  54.1 3.4 %collective-permute-start.16 = (bf16[704,128]{1,0:T(8,128)(2,1)S(1)}, bf16[704,128]{1,0:T(8,128)(2,1)S(1)}, u32[]{:S(2)}, u32[]{:S(2)}) collective-permute-start(bf16[704,128]{1,0:T(8,128)(2,1)S(1)} %get-tuple-element.46), channel_id=1, source_target_pairs={{0,8},{4,12},{8,0},{12,4},{1,9},{5,13},{9,1},{13,5},{2,10},{6,14},... | collective-permute-start | bytes 540680 | tf_op jit(solution)/shard_map/ppermute | solution.py:28
  57.5 3.2 %collective-permute-start.18 = (bf16[704,128]{1,0:T(8,128)(2,1)S(1)}, bf16[704,128]{1,0:T(8,128)(2,1)S(1)}, u32[]{:S(2)}, u32[]{:S(2)}) collective-permute-start(bf16[704,128]{1,0:T(8,128)(2,1)S(1)} %get-tuple-element.48), channel_id=1, source_target_pairs={{0,4},{4,8},{8,12},{12,0},{1,5},{5,9},{9,13},{13,1},{2,6},{6,10},{... | collective-permute-start | bytes 540680 | tf_op jit(solution)/shard_map/ppermute | solution.py:28
  60.8 1.9 %collective-permute-start.20 = (bf16[480,128]{1,0:T(8,128)(2,1)S(1)}, bf16[480,128]{1,0:T(8,128)(2,1)S(1)}, u32[]{:S(2)}, u32[]{:S(2)}) collective-permute-start(bf16[480,128]{1,0:T(8,128)(2,1)S(1)} %get-tuple-element.51), channel_id=1, source_target_pairs={{0,96},{32,0},{64,32},{96,64},{1,97},{33,1},{65,33},{97,65},{2,98}... | collective-permute-start | bytes 368648 | tf_op jit(solution)/shard_map/ppermute | solution.py:28
  62.7 0.2 collective-permute-start.21
  63.0 2.9 %shard_map.92 = (bf16[512,640]{1,0:T(8,128)(2,1)S(1)}, f32[8,512]{1,0:T(8,128)S(1)}, bf16[2,2,512,640]{3,2,1,0:T(8,128)(2,1)S(1)}, f32[8,640]{1,0:T(8,128)S(1)}) custom-call(s32[2]{0:T(128)S(1)} %pad_add_fusion.info_ref, s32[2,512]{1,0:T(2,128)S(1)} %copy-done.3, s32[1,512]{1,0:T(1,128)S(1)} %bitcast.9, bf16[1,2560]{1,0:T(2,128)(2,1)S(1)} %reshape.15.gain_ref, ...), custom_call_target="tpu_custom_call" | custom-call | flops 335544320 | bytes 3324928 | tf_op jit(solution)/shard_map/pallas_call | solution.py:48
  65.8 2.9 %collective-permute-done.21.refs_7_ = bf16[480,128]{1,0:T(8,128)(2,1)S(1)} collective-permute-done((bf16[480,128]{1,0:T(8,128)(2,1)S(1)}, bf16[480,128]{1,0:T(8,128)(2,1)S(1)}, u32[]{:S(2)}, u32[]{:S(2)}) %collective-permute-start.21) | collective-permute-done | bytes 122912 | tf_op jit(solution)/shard_map/ppermute | solution.py:28
  68.8 1.6 %shard_map.93 = (bf16[6,56,128]{2,1,0:T(8,128)(2,1)S(1)}, bf16[6,56,128]{2,1,0:T(8,128)(2,1)S(1)}, bf16[6,56,128]{2,1,0:T(8,128)(2,1)S(1)}, bf16[6,56,128]{2,1,0:T(8,128)(2,1)S(1)}, f32[5,4,56,128]{3,2,1,0:T(8,128)S(1)}) custom-call(bf16[704,128]{1,0:T(8,128)(2,1)S(1)} %get-tuple-element.45.refs_0_, bf16[704,128]{1,0:T(8,128)(2,1)S(1)} %collective-permute-done.16.refs_1_, ...), custom_call_target="tpu_custom_call" | custom-call | bytes 2416640 | tf_op jit(solution)/shard_map/pallas_call | solution.py:48
  70.4 2.5 %collective-permute-start.26 = (bf16[6,56,128]{2,1,0:T(8,128)(2,1)S(1)}, bf16[6,56,128]{2,1,0:T(8,128)(2,1)S(1)}, u32[]{:S(2)}, u32[]{:S(2)}) collective-permute-start(bf16[6,56,128]{2,1,0:T(8,128)(2,1)S(1)} %get-tuple-element.60), channel_id=1, source_target_pairs={{0,16},{1,17},{16,0},{17,1},{2,18},{3,19},{18,2},{19,3},{4,20},{5,... | collective-permute-start | bytes 258056 | tf_op jit(solution)/shard_map/ppermute | solution.py:28
  72.9 1.1 %shard_map.95.scores_ref = f32[2,5,112,512]{3,2,1,0:T(8,128)S(1)} custom-call(s32[2]{0:T(128)S(1)} %pad_add_fusion.info_ref, f32[5,4,56,128]{3,2,1,0:T(8,128)S(1)} %get-tuple-element.62.middle_ref, f32[8,640]{1,0:T(8,128)S(1)} %get-tuple-element.63.gain_ref, bf16[2,2,512,640]{3,2,1,0:T(8,128)(2,1)S(1)} %get-tuple-element.64.text_ref), custom_call_target="tpu_custom_call" | custom-call | flops 146800640 | bytes 5509120 | tf_op jit(solution)/shard_map/pallas_call | solution.py:48
  74.0 0.9 %collective-permute-done.25.refs_1_.s1 = bf16[6,56,128]{2,1,0:T(8,128)(2,1)S(1)} collective-permute-done((bf16[6,56,128]{2,1,0:T(8,128)(2,1)S(1)}, bf16[6,56,128]{2,1,0:T(8,128)(2,1)S(1)}, u32[]{:S(2)}, u32[]{:S(2)}) %collective-permute-start.25) | collective-permute-done | bytes 86048 | tf_op jit(solution)/shard_map/ppermute | solution.py:28
  74.9 1.6 %collective-permute-done.26.refs_2_.s2 = bf16[6,56,128]{2,1,0:T(8,128)(2,1)S(1)} collective-permute-done((bf16[6,56,128]{2,1,0:T(8,128)(2,1)S(1)}, bf16[6,56,128]{2,1,0:T(8,128)(2,1)S(1)}, u32[]{:S(2)}, u32[]{:S(2)}) %collective-permute-start.26) | collective-permute-done | bytes 86048 | tf_op jit(solution)/shard_map/ppermute | solution.py:28
  76.5 2.1 %collective-permute-done.27.refs_3_.s3 = bf16[6,56,128]{2,1,0:T(8,128)(2,1)S(1)} collective-permute-done((bf16[6,56,128]{2,1,0:T(8,128)(2,1)S(1)}, bf16[6,56,128]{2,1,0:T(8,128)(2,1)S(1)}, u32[]{:S(2)}, u32[]{:S(2)}) %collective-permute-start.27) | collective-permute-done | bytes 86048 | tf_op jit(solution)/shard_map/ppermute | solution.py:28
  78.6 2.1 %shard_map.96 = (bf16[5,56,128]{2,1,0:T(8,128)(2,1)S(1)}, bf16[5,56,128]{2,1,0:T(8,128)(2,1)S(1)}, bf16[5,56,128]{2,1,0:T(8,128)(2,1)S(1)}, bf16[5,56,128]{2,1,0:T(8,128)(2,1)S(1)}) custom-call(s32[2]{0:T(128)S(1)} %pad_add_fusion.info_ref, bf16[6,56,128]{2,1,0:T(8,128)(2,1)S(1)} %get-tuple-element.58.refs_0_.s0, ...), custom_call_target="tpu_custom_call" | custom-call | flops 220200960 | bytes 6791168 | tf_op jit(solution)/shard_map/pallas_call | solution.py:48
  80.7 1.0 %collective-permute-start.28 = (bf16[5,56,128]{2,1,0:T(8,128)(2,1)S(1)}, bf16[5,56,128]{2,1,0:T(8,128)(2,1)S(1)}, u32[]{:S(2)}, u32[]{:S(2)}) collective-permute-start(bf16[5,56,128]{2,1,0:T(8,128)(2,1)S(1)} %get-tuple-element.67), channel_id=1, source_target_pairs={{0,17},{1,0},{16,1},{17,16},{2,19},{3,2},{18,3},{19,18},{4,21},{5,... | collective-permute-start | bytes 215048 | tf_op jit(solution)/shard_map/ppermute | solution.py:28
  81.8 0.9 %collective-permute-start.29 = (bf16[5,56,128]{2,1,0:T(8,128)(2,1)S(1)}, bf16[5,56,128]{2,1,0:T(8,128)(2,1)S(1)}, u32[]{:S(2)}, u32[]{:S(2)}) collective-permute-start(bf16[5,56,128]{2,1,0:T(8,128)(2,1)S(1)} %get-tuple-element.68), channel_id=1, source_target_pairs={{0,16},{1,17},{16,0},{17,1},{2,18},{3,19},{18,2},{19,3},{4,20},{5,... | collective-permute-start | bytes 215048 | tf_op jit(solution)/shard_map/ppermute | solution.py:28
  82.7 0.4 collective-permute-start.30
  83.1 0.8 shard_map.94
  83.8 1.3 %collective-permute-done.28.refs_1_ = bf16[5,56,128]{2,1,0:T(8,128)(2,1)S(1)} collective-permute-done((bf16[5,56,128]{2,1,0:T(8,128)(2,1)S(1)}, bf16[5,56,128]{2,1,0:T(8,128)(2,1)S(1)}, u32[]{:S(2)}, u32[]{:S(2)}) %collective-permute-start.28) | collective-permute-done | bytes 71712 | tf_op jit(solution)/shard_map/ppermute | solution.py:28
  85.1 2.5 %collective-permute-done.29.refs_2_ = bf16[5,56,128]{2,1,0:T(8,128)(2,1)S(1)} collective-permute-done((bf16[5,56,128]{2,1,0:T(8,128)(2,1)S(1)}, bf16[5,56,128]{2,1,0:T(8,128)(2,1)S(1)}, u32[]{:S(2)}, u32[]{:S(2)}) %collective-permute-start.29) | collective-permute-done | bytes 71712 | tf_op jit(solution)/shard_map/ppermute | solution.py:28
  87.6 0.8 collective-permute-done.30.refs_3_
  88.4 0.8 shard_map.97
  (40 shorter events, 0.8 us)
Async XLA Ops:
  0.6 39.6 %copy-start = (bf16[1,56,2560]{2,1,0:T(8,128)(2,1)S(1)}, bf16[1,56,2560]{2,1,0:T(8,128)(2,1)}, u32[]{:S(2)}) copy-start(bf16[1,56,2560]{2,1,0:T(8,128)(2,1)} %param.9) | copy-start | bytes 860164
  0.6 1.0 %copy-start.1 = (bf16[1,56,2560]{2,1,0:T(8,128)(2,1)S(1)}, bf16[1,56,2560]{2,1,0:T(8,128)(2,1)}, u32[]{:S(2)}) copy-start(bf16[1,56,2560]{2,1,0:T(8,128)(2,1)} %param.7) | copy-start | bytes 860164
  1.6 1.0 %copy-start.2 = (bf16[2,56,1280]{2,1,0:T(8,128)(2,1)S(1)}, bf16[2,56,1280]{2,1,0:T(8,128)(2,1)}, u32[]{:S(2)}) copy-start(bf16[2,56,1280]{2,1,0:T(8,128)(2,1)} %kv_ref.1) | copy-start | bytes 860164
  2.7 10.5 %collective-permute-start.7 = (bf16[15,56,128]{2,1,0:T(8,128)(2,1)S(1)}, bf16[15,56,128]{2,1,0:T(8,128)(2,1)S(1)}, u32[]{:S(2)}, u32[]{:S(2)}) collective-permute-start(bf16[15,56,128]{2,1,0:T(8,128)(2,1)S(1)} %get-tuple-element.39), channel_id=1, source_target_pairs={{0,16},{1,17},{16,0},{17,1},{2,18},{3,19},{18,2},{19,3},{4,20},{5,... | collective-permute-start | bytes 645128 | tf_op jit(solution)/shard_map/ppermute | solution.py:28
  6.0 6.9 %collective-permute-start.6 = (bf16[5,56,128]{2,1,0:T(8,128)(2,1)S(1)}, bf16[5,56,128]{2,1,0:T(8,128)(2,1)S(1)}, u32[]{:S(2)}, u32[]{:S(2)}) collective-permute-start(bf16[5,56,128]{2,1,0:T(8,128)(2,1)S(1)} %get-tuple-element.38), channel_id=1, source_target_pairs={{0,1},{1,16},{16,17},{17,0},{2,3},{3,18},{18,19},{19,2},{4,5},{5,2... | collective-permute-start | bytes 215048 | tf_op jit(solution)/shard_map/ppermute | solution.py:28
  6.7 6.5 %collective-permute-start.8 = (bf16[5,56,128]{2,1,0:T(8,128)(2,1)S(1)}, bf16[5,56,128]{2,1,0:T(8,128)(2,1)S(1)}, u32[]{:S(2)}, u32[]{:S(2)}) collective-permute-start(bf16[5,56,128]{2,1,0:T(8,128)(2,1)S(1)} %get-tuple-element.40), channel_id=1, source_target_pairs={{0,17},{1,0},{16,1},{17,16},{2,19},{3,2},{18,3},{19,18},{4,21},{5,... | collective-permute-start | bytes 215048 | tf_op jit(solution)/shard_map/ppermute | solution.py:28
  9.2 10.2 %collective-permute-start.2 = (bf16[7,56,128]{2,1,0:T(8,128)(2,1)S(1)}, bf16[7,56,128]{2,1,0:T(8,128)(2,1)S(1)}, u32[]{:S(2)}, u32[]{:S(2)}) collective-permute-start(bf16[7,56,128]{2,1,0:T(8,128)(2,1)S(1)} %get-tuple-element.36.refs_0_), channel_id=1, source_target_pairs={{0,12},{4,0},{8,4},{12,8},{1,13},{5,1},{9,5},{13,9},{2,14},{6,2},{... | collective-permute-start | bytes 301064 | tf_op jit(solution)/shard_map/ppermute | solution.py:28
  10.1 9.3 %collective-permute-start.1 = (bf16[7,56,128]{2,1,0:T(8,128)(2,1)S(1)}, bf16[7,56,128]{2,1,0:T(8,128)(2,1)S(1)}, u32[]{:S(2)}, u32[]{:S(2)}) collective-permute-start(bf16[7,56,128]{2,1,0:T(8,128)(2,1)S(1)} %get-tuple-element.36.refs_0_), channel_id=1, source_target_pairs={{0,4},{4,8},{8,12},{12,0},{1,5},{5,9},{9,13},{13,1},{2,6},{6,10},{... | collective-permute-start | bytes 301064 | tf_op jit(solution)/shard_map/ppermute | solution.py:28
  13.3 18.3 %collective-permute-start.14 = (bf16[12,56,128]{2,1,0:T(8,128)(2,1)S(1)}, bf16[12,56,128]{2,1,0:T(8,128)(2,1)S(1)}, u32[]{:S(2)}, u32[]{:S(2)}) collective-permute-start(bf16[12,56,128]{2,1,0:T(8,128)(2,1)S(1)} %get-tuple-element.42.refs_12_), channel_id=1, source_target_pairs={{0,96},{32,0},{64,32},{96,64},{1,97},{33,1},{65,33},{97,65},{2,98}... | collective-permute-start | bytes 516104 | tf_op jit(solution)/shard_map/ppermute | solution.py:28
  17.4 9.1 %collective-permute-start.5 = (bf16[8,56,128]{2,1,0:T(8,128)(2,1)S(1)}, bf16[8,56,128]{2,1,0:T(8,128)(2,1)S(1)}, u32[]{:S(2)}, u32[]{:S(2)}) collective-permute-start(bf16[8,56,128]{2,1,0:T(8,128)(2,1)S(1)} %get-tuple-element.37.refs_4_), channel_id=1, source_target_pairs={{0,96},{32,0},{64,32},{96,64},{1,97},{33,1},{65,33},{97,65},{2,98}... | collective-permute-start | bytes 344072 | tf_op jit(solution)/shard_map/ppermute | solution.py:28
  17.8 11.1 %collective-permute-start.4 = (bf16[8,56,128]{2,1,0:T(8,128)(2,1)S(1)}, bf16[8,56,128]{2,1,0:T(8,128)(2,1)S(1)}, u32[]{:S(2)}, u32[]{:S(2)}) collective-permute-start(bf16[8,56,128]{2,1,0:T(8,128)(2,1)S(1)} %get-tuple-element.37.refs_4_), channel_id=1, source_target_pairs={{0,32},{32,64},{64,96},{96,0},{1,33},{33,65},{65,97},{97,1},{2,34}... | collective-permute-start | bytes 344072 | tf_op jit(solution)/shard_map/ppermute | solution.py:28
  19.4 9.7 %collective-permute-start.3 = (bf16[8,56,128]{2,1,0:T(8,128)(2,1)S(1)}, bf16[8,56,128]{2,1,0:T(8,128)(2,1)S(1)}, u32[]{:S(2)}, u32[]{:S(2)}) collective-permute-start(bf16[8,56,128]{2,1,0:T(8,128)(2,1)S(1)} %get-tuple-element.37.refs_4_), channel_id=1, source_target_pairs={{0,64},{32,96},{64,0},{96,32},{1,65},{33,97},{65,1},{97,33},{2,66}... | collective-permute-start | bytes 344072 | tf_op jit(solution)/shard_map/ppermute | solution.py:28
  19.4 6.2 %collective-permute-start = (bf16[7,56,128]{2,1,0:T(8,128)(2,1)S(1)}, bf16[7,56,128]{2,1,0:T(8,128)(2,1)S(1)}, u32[]{:S(2)}, u32[]{:S(2)}) collective-permute-start(bf16[7,56,128]{2,1,0:T(8,128)(2,1)S(1)} %get-tuple-element.36.refs_0_), channel_id=1, source_target_pairs={{0,8},{4,12},{8,0},{12,4},{1,9},{5,13},{9,1},{13,5},{2,10},{6,14},... | collective-permute-start | bytes 301064 | tf_op jit(solution)/shard_map/ppermute | solution.py:28
  25.6 14.1 %collective-permute-start.11 = (bf16[13,56,128]{2,1,0:T(8,128)(2,1)S(1)}, bf16[13,56,128]{2,1,0:T(8,128)(2,1)S(1)}, u32[]{:S(2)}, u32[]{:S(2)}) collective-permute-start(bf16[13,56,128]{2,1,0:T(8,128)(2,1)S(1)} %get-tuple-element.41.refs_8_), channel_id=1, source_target_pairs={{0,12},{4,0},{8,4},{12,8},{1,13},{5,1},{9,5},{13,9},{2,14},{6,2},{... | collective-permute-start | bytes 559112 | tf_op jit(solution)/shard_map/ppermute | solution.py:28
  26.5 13.2 %collective-permute-start.10 = (bf16[13,56,128]{2,1,0:T(8,128)(2,1)S(1)}, bf16[13,56,128]{2,1,0:T(8,128)(2,1)S(1)}, u32[]{:S(2)}, u32[]{:S(2)}) collective-permute-start(bf16[13,56,128]{2,1,0:T(8,128)(2,1)S(1)} %get-tuple-element.41.refs_8_), channel_id=1, source_target_pairs={{0,4},{4,8},{8,12},{12,0},{1,5},{5,9},{9,13},{13,1},{2,6},{6,10},{... | collective-permute-start | bytes 559112 | tf_op jit(solution)/shard_map/ppermute | solution.py:28
  28.9 10.8 %collective-permute-start.9 = (bf16[13,56,128]{2,1,0:T(8,128)(2,1)S(1)}, bf16[13,56,128]{2,1,0:T(8,128)(2,1)S(1)}, u32[]{:S(2)}, u32[]{:S(2)}) collective-permute-start(bf16[13,56,128]{2,1,0:T(8,128)(2,1)S(1)} %get-tuple-element.41.refs_8_), channel_id=1, source_target_pairs={{0,8},{4,12},{8,0},{12,4},{1,9},{5,13},{9,1},{13,5},{2,10},{6,14},... | collective-permute-start | bytes 559112 | tf_op jit(solution)/shard_map/ppermute | solution.py:28
  29.1 8.5 %collective-permute-start.13 = (bf16[12,56,128]{2,1,0:T(8,128)(2,1)S(1)}, bf16[12,56,128]{2,1,0:T(8,128)(2,1)S(1)}, u32[]{:S(2)}, u32[]{:S(2)}) collective-permute-start(bf16[12,56,128]{2,1,0:T(8,128)(2,1)S(1)} %get-tuple-element.42.refs_12_), channel_id=1, source_target_pairs={{0,32},{32,64},{64,96},{96,0},{1,33},{33,65},{65,97},{97,1},{2,34}... | collective-permute-start | bytes 516104 | tf_op jit(solution)/shard_map/ppermute | solution.py:28
  31.6 8.1 %collective-permute-start.12 = (bf16[12,56,128]{2,1,0:T(8,128)(2,1)S(1)}, bf16[12,56,128]{2,1,0:T(8,128)(2,1)S(1)}, u32[]{:S(2)}, u32[]{:S(2)}) collective-permute-start(bf16[12,56,128]{2,1,0:T(8,128)(2,1)S(1)} %get-tuple-element.42.refs_12_), channel_id=1, source_target_pairs={{0,64},{32,96},{64,0},{96,32},{1,65},{33,97},{65,1},{97,33},{2,66}... | collective-permute-start | bytes 516104 | tf_op jit(solution)/shard_map/ppermute | solution.py:28
  40.1 5.1 %collective-permute-start.15 = (bf16[10,448,128]{2,1,0:T(8,128)(2,1)S(1)}, bf16[10,448,128]{2,1,0:T(8,128)(2,1)S(1)}, u32[]{:S(2)}, u32[]{:S(2)}) collective-permute-start(bf16[10,448,128]{2,1,0:T(8,128)(2,1)S(1)} %get-tuple-element.44.held), channel_id=1, source_target_pairs={{0,2},{2,0},{1,3},{3,1},{4,6},{6,4},{5,7},{7,5},{8,10},{10,8},{9,1... | collective-permute-start | bytes 3440648 | tf_op jit(solution)/shard_map/ppermute | solution.py:28
  40.3 17.2 %collective-permute-start.22 = (bf16[5,56,128]{2,1,0:T(8,128)(2,1)S(1)}, bf16[5,56,128]{2,1,0:T(8,128)(2,1)S(1)}, u32[]{:S(2)}, u32[]{:S(2)}) collective-permute-start(bf16[5,56,128]{2,1,0:T(8,128)(2,1)S(1)} %get-tuple-element.54), channel_id=1, source_target_pairs={{0,1},{1,16},{16,17},{17,0},{2,3},{3,18},{18,19},{19,2},{4,5},{5,2... | collective-permute-start | bytes 215048 | tf_op jit(solution)/shard_map/ppermute | solution.py:28
  42.5 15.0 %collective-permute-start.23 = (bf16[5,56,128]{2,1,0:T(8,128)(2,1)S(1)}, bf16[5,56,128]{2,1,0:T(8,128)(2,1)S(1)}, u32[]{:S(2)}, u32[]{:S(2)}) collective-permute-start(bf16[5,56,128]{2,1,0:T(8,128)(2,1)S(1)} %get-tuple-element.55), channel_id=1, source_target_pairs={{0,16},{1,17},{16,0},{17,1},{2,18},{3,19},{18,2},{19,3},{4,20},{5,... | collective-permute-start | bytes 215048 | tf_op jit(solution)/shard_map/ppermute | solution.py:28
  45.0 15.8 %collective-permute-start.24 = (bf16[5,56,128]{2,1,0:T(8,128)(2,1)S(1)}, bf16[5,56,128]{2,1,0:T(8,128)(2,1)S(1)}, u32[]{:S(2)}, u32[]{:S(2)}) collective-permute-start(bf16[5,56,128]{2,1,0:T(8,128)(2,1)S(1)} %get-tuple-element.56), channel_id=1, source_target_pairs={{0,17},{1,0},{16,1},{17,16},{2,19},{3,2},{18,3},{19,18},{4,21},{5,... | collective-permute-start | bytes 215048 | tf_op jit(solution)/shard_map/ppermute | solution.py:28
  48.2 12.5 %copy-start.5 = (bf16[2560]{0:T(1024)(128)(2,1)S(1)}, bf16[2560]{0:T(1024)(128)(2,1)}, u32[]{:S(2)}) copy-start(bf16[2560]{0:T(1024)(128)(2,1)} %param.10) | copy-start | bytes 15364
  48.2 14.7 %copy-start.3 = (s32[2,512]{1,0:T(2,128)S(1)}, s32[2,512]{1,0:T(2,128)}, u32[]{:S(2)}) copy-start(s32[2,512]{1,0:T(2,128)} %ids_ref.1) | copy-start | bytes 12292
  48.2 14.7 %copy-start.4 = (s32[512]{0:T(512)S(1)}, s32[512]{0:T(512)}, u32[]{:S(2)}) copy-start(s32[512]{0:T(512)} %param.13) | copy-start | bytes 6148
  48.3 14.4 %collective-permute-start.19 = (bf16[480,128]{1,0:T(8,128)(2,1)S(1)}, bf16[480,128]{1,0:T(8,128)(2,1)S(1)}, u32[]{:S(2)}, u32[]{:S(2)}) collective-permute-start(bf16[480,128]{1,0:T(8,128)(2,1)S(1)} %get-tuple-element.50), channel_id=1, source_target_pairs={{0,64},{32,96},{64,0},{96,32},{1,65},{33,97},{65,1},{97,33},{2,66}... | collective-permute-start | bytes 368648 | tf_op jit(solution)/shard_map/ppermute | solution.py:28
  54.1 14.7 %collective-permute-start.16 = (bf16[704,128]{1,0:T(8,128)(2,1)S(1)}, bf16[704,128]{1,0:T(8,128)(2,1)S(1)}, u32[]{:S(2)}, u32[]{:S(2)}) collective-permute-start(bf16[704,128]{1,0:T(8,128)(2,1)S(1)} %get-tuple-element.46), channel_id=1, source_target_pairs={{0,8},{4,12},{8,0},{12,4},{1,9},{5,13},{9,1},{13,5},{2,10},{6,14},... | collective-permute-start | bytes 540680 | tf_op jit(solution)/shard_map/ppermute | solution.py:28
  57.5 11.2 %collective-permute-start.17 = (bf16[704,128]{1,0:T(8,128)(2,1)S(1)}, bf16[704,128]{1,0:T(8,128)(2,1)S(1)}, u32[]{:S(2)}, u32[]{:S(2)}) collective-permute-start(bf16[704,128]{1,0:T(8,128)(2,1)S(1)} %get-tuple-element.47), channel_id=1, source_target_pairs={{0,12},{4,0},{8,4},{12,8},{1,13},{5,1},{9,5},{13,9},{2,14},{6,2},{... | collective-permute-start | bytes 540680 | tf_op jit(solution)/shard_map/ppermute | solution.py:28
  57.5 11.2 %collective-permute-start.18 = (bf16[704,128]{1,0:T(8,128)(2,1)S(1)}, bf16[704,128]{1,0:T(8,128)(2,1)S(1)}, u32[]{:S(2)}, u32[]{:S(2)}) collective-permute-start(bf16[704,128]{1,0:T(8,128)(2,1)S(1)} %get-tuple-element.48), channel_id=1, source_target_pairs={{0,4},{4,8},{8,12},{12,0},{1,5},{5,9},{9,13},{13,1},{2,6},{6,10},{... | collective-permute-start | bytes 540680 | tf_op jit(solution)/shard_map/ppermute | solution.py:28
  60.8 5.1 %collective-permute-start.20 = (bf16[480,128]{1,0:T(8,128)(2,1)S(1)}, bf16[480,128]{1,0:T(8,128)(2,1)S(1)}, u32[]{:S(2)}, u32[]{:S(2)}) collective-permute-start(bf16[480,128]{1,0:T(8,128)(2,1)S(1)} %get-tuple-element.51), channel_id=1, source_target_pairs={{0,96},{32,0},{64,32},{96,64},{1,97},{33,1},{65,33},{97,65},{2,98}... | collective-permute-start | bytes 368648 | tf_op jit(solution)/shard_map/ppermute | solution.py:28
  62.7 6.1 %collective-permute-start.21 = (bf16[480,128]{1,0:T(8,128)(2,1)S(1)}, bf16[480,128]{1,0:T(8,128)(2,1)S(1)}, u32[]{:S(2)}, u32[]{:S(2)}) collective-permute-start(bf16[480,128]{1,0:T(8,128)(2,1)S(1)} %get-tuple-element.52), channel_id=1, source_target_pairs={{0,32},{32,64},{64,96},{96,0},{1,33},{33,65},{65,97},{97,1},{2,34}... | collective-permute-start | bytes 368648 | tf_op jit(solution)/shard_map/ppermute | solution.py:28
  70.3 4.6 %collective-permute-start.25 = (bf16[6,56,128]{2,1,0:T(8,128)(2,1)S(1)}, bf16[6,56,128]{2,1,0:T(8,128)(2,1)S(1)}, u32[]{:S(2)}, u32[]{:S(2)}) collective-permute-start(bf16[6,56,128]{2,1,0:T(8,128)(2,1)S(1)} %get-tuple-element.59), channel_id=1, source_target_pairs={{0,17},{1,0},{16,1},{17,16},{2,19},{3,2},{18,3},{19,18},{4,21},{5,... | collective-permute-start | bytes 258056 | tf_op jit(solution)/shard_map/ppermute | solution.py:28
  70.4 6.1 %collective-permute-start.26 = (bf16[6,56,128]{2,1,0:T(8,128)(2,1)S(1)}, bf16[6,56,128]{2,1,0:T(8,128)(2,1)S(1)}, u32[]{:S(2)}, u32[]{:S(2)}) collective-permute-start(bf16[6,56,128]{2,1,0:T(8,128)(2,1)S(1)} %get-tuple-element.60), channel_id=1, source_target_pairs={{0,16},{1,17},{16,0},{17,1},{2,18},{3,19},{18,2},{19,3},{4,20},{5,... | collective-permute-start | bytes 258056 | tf_op jit(solution)/shard_map/ppermute | solution.py:28
  72.9 5.7 %collective-permute-start.27 = (bf16[6,56,128]{2,1,0:T(8,128)(2,1)S(1)}, bf16[6,56,128]{2,1,0:T(8,128)(2,1)S(1)}, u32[]{:S(2)}, u32[]{:S(2)}) collective-permute-start(bf16[6,56,128]{2,1,0:T(8,128)(2,1)S(1)} %get-tuple-element.61), channel_id=1, source_target_pairs={{0,1},{1,16},{16,17},{17,0},{2,3},{3,18},{18,19},{19,2},{4,5},{5,2... | collective-permute-start | bytes 258056 | tf_op jit(solution)/shard_map/ppermute | solution.py:28
  80.7 4.4 %collective-permute-start.28 = (bf16[5,56,128]{2,1,0:T(8,128)(2,1)S(1)}, bf16[5,56,128]{2,1,0:T(8,128)(2,1)S(1)}, u32[]{:S(2)}, u32[]{:S(2)}) collective-permute-start(bf16[5,56,128]{2,1,0:T(8,128)(2,1)S(1)} %get-tuple-element.67), channel_id=1, source_target_pairs={{0,17},{1,0},{16,1},{17,16},{2,19},{3,2},{18,3},{19,18},{4,21},{5,... | collective-permute-start | bytes 215048 | tf_op jit(solution)/shard_map/ppermute | solution.py:28
  81.8 5.8 %collective-permute-start.29 = (bf16[5,56,128]{2,1,0:T(8,128)(2,1)S(1)}, bf16[5,56,128]{2,1,0:T(8,128)(2,1)S(1)}, u32[]{:S(2)}, u32[]{:S(2)}) collective-permute-start(bf16[5,56,128]{2,1,0:T(8,128)(2,1)S(1)} %get-tuple-element.68), channel_id=1, source_target_pairs={{0,16},{1,17},{16,0},{17,1},{2,18},{3,19},{18,2},{19,3},{4,20},{5,... | collective-permute-start | bytes 215048 | tf_op jit(solution)/shard_map/ppermute | solution.py:28
  82.7 5.7 %collective-permute-start.30 = (bf16[5,56,128]{2,1,0:T(8,128)(2,1)S(1)}, bf16[5,56,128]{2,1,0:T(8,128)(2,1)S(1)}, u32[]{:S(2)}, u32[]{:S(2)}) collective-permute-start(bf16[5,56,128]{2,1,0:T(8,128)(2,1)S(1)} %get-tuple-element.69), channel_id=1, source_target_pairs={{0,1},{1,16},{16,17},{17,0},{2,3},{3,18},{18,19},{19,2},{4,5},{5,2... | collective-permute-start | bytes 215048 | tf_op jit(solution)/shard_map/ppermute | solution.py:28

commit v3 on v2

--- a/solution.py
+++ b/solution.py
@@ -67,20 +67,29 @@
 LOW, WIDE, NARROW = GROUPS[1][0], GROUPS[0][1], GROUPS[1][1]
 
 
-def split_kernel(plane_ref, rows_ref, kv_ref, along_x, along_z, first, last, across):
-    high = plane_ref[0] // 2
-    for distance in range(4):
+def split_near_kernel(plane_ref, rows_ref, residual_ref, first, last):
+    for out, distance in ((first, 1), (last, 3)):
         plane = lax.rem(plane_ref[0] + distance, 4)
         for head in range(NQ):
             lane = pl.multiple_of((first_head(plane) + head) * HD, HD)
-            rows = rows_ref[:, pl.ds(lane, HD)]
-            if distance == 0 and head < LOW:
-                along_x[head] = rows
-            elif distance == 0:
-                along_z[2 * WIDE + head - LOW] = rows
-            else:
-                (first, across, last)[distance - 1][head] = rows
-    for head in range(NQ):
+            out[head] = rows_ref[:, pl.ds(lane, HD)]
+            out[NQ + head] = residual_ref[:, pl.ds(lane, HD)]
+
+
+def split_kernel(plane_ref, rows_ref, residual_ref, kv_ref, along_x, along_z, across, residual):
+    high = plane_ref[0] // 2
+    opposite = lax.rem(plane_ref[0] + 2, 4)
+    for head in range(NQ):
+        lane = pl.multiple_of((first_head(opposite) + head) * HD, HD)
+        across[head] = rows_ref[:, pl.ds(lane, HD)]
+        across[NQ + head] = residual_ref[:, pl.ds(lane, HD)]
+        lane = pl.multiple_of((first_head(plane_ref[0]) + head) * HD, HD)
+        residual[head] = residual_ref[:, pl.ds(lane, HD)]
+        rows = rows_ref[:, pl.ds(lane, HD)]
+        if head < LOW:
+            along_x[head] = rows
+        else:
+            along_z[2 * WIDE + head - LOW] = rows
         here = pl.multiple_of((high * NQ + head) * HD, HD)
         there = pl.multiple_of(((1 - high) * NQ + head) * HD, HD)
         for which in range(2):
@@ -89,7 +98,7 @@
                 along_z[2 * head + which] = rows
             else:
                 along_x[WIDE + 2 * (head - LOW) + which] = rows
-            across[NQ + 2 * head + which] = kv_ref[which, :, pl.ds(there, HD)]
+            across[2 * NQ + 2 * head + which] = kv_ref[which, :, pl.ds(there, HD)]
 
 
 def pack_kernel(first, across, last, along_x, along_z):
@@ -100,7 +109,7 @@
             else:
                 along_z[2 * WIDE + 3 * (head - LOW) + index] = query[head]
         for which in range(2):
-            rows = across[NQ + 2 * head + which]
+            rows = across[2 * NQ + 2 * head + which]
             if head < LOW:
                 along_z[2 * head + which] = rows
             else:
@@ -129,14 +138,6 @@
                 parts = [z1[index][2 * WIDE + unit]]
                 parts += [z2[index][2 * WIDE + 3 * unit + k] for k in range(3)]
             rows[head, index * ROWS : (index + 1) * ROWS, :] = stacked(parts)
-
-
-def split_rows_kernel(plane_ref, rows_ref, *outs):
-    for distance in range(4):
-        plane = lax.rem(plane_ref[0] + distance, 4)
-        for head in range(NQ):
-            lane = pl.multiple_of((first_head(plane) + head) * HD, HD)
-            outs[distance][head] = rows_ref[:, pl.ds(lane, HD)]
 
 
 def join_rows_kernel(plane_ref, *refs):
@@ -229,7 +230,7 @@
             for block in range(4):
                 part = total[block * TOK : (block + 1) * TOK].astype(BF)
                 attended[block][head] = part
-                middle = residuals[block][head].astype(F32) + part.astype(F32)
+                middle = residuals[block][NQ * min(block, 1) + head].astype(F32) + part.astype(F32)
                 middle_ref[head, block] = middle
                 middles.append(middle)
             rows = jnp.concatenate(middles, axis=0)
@@ -358,25 +359,26 @@
     info = jnp.stack([quarter, plane]).astype(jnp.int32)
     piece = (NQ, TOK, HD)
 
-    along_x, along_z, first, last, over = call(
+    double = shaped((2 * NQ, TOK, HD))
+    first, last = call(split_near_kernel, [double] * 2, [where], [queries[0], residual_in[0]])
+    along_x, along_z, over, residual = call(
         split_kernel,
         [
             shaped((WIDE + 2 * NARROW, TOK, HD)),
             shaped((2 * WIDE + NARROW, TOK, HD)),
+            shaped((4 * NQ, TOK, HD)),
             shaped(piece),
-            shaped(piece),
-            shaped((3 * NQ, TOK, HD)),
         ],
         [where],
-        [queries[0], keys_values],
+        [queries[0], residual_in[0], keys_values],
     )
 
     def gathered(value, axis):
         return [value] + [shift(value, axis, d, 4) for d in (2, 1, 3)]
 
-    over = shift(over, PLANE, 2, 4)
     first = shift(first, PLANE, 1, 4)
     last = shift(last, PLANE, 3, 4)
+    over = shift(over, PLANE, 2, 4)
     units = gathered(along_x, "x") + gathered(along_z, "z")
     along_x, along_z = call(
         pack_kernel,
@@ -385,8 +387,6 @@
         [first, over, last],
     )
     units = units + gathered(along_x, "x") + gathered(along_z, "z")
-    residuals = call(split_rows_kernel, [shaped(piece)] * 4, [where], [residual_in[0]])
-    residuals = [p if d == 0 else shift(p, PLANE, d, 4) for d, p in enumerate(residuals)]
     held, rows = call(
         order_kernel, [shaped((2 * NQ, 4 * KEYS, HD)), shaped((NQ, 4 * ROWS, HD))], [], units
     )
@@ -400,7 +400,7 @@
         combine_kernel,
         [shaped((NQ + 1, TOK, HD))] * 4 + [shaped((NQ, 4, TOK, HD), F32)],
         [],
-        [*partials, *residuals],
+        [*partials, residual, first, over, last],
         kept=[(own, pl.ANY)],
         scratch=[pltpu.VMEM((HD, 2 * HD), F32)],
     )

time: 89.3 us -> 91.8 us (1.028)
  the two profiles are of different devices: /device:TPU:6 before, /device:TPU:24 now
where the time goes in v3:
time: 91.8 us; the launch traced here: 90.2 us
  starting transfers between devices  40 us (44%)
  waiting for transfers between devices  29.5 us (32%)
  Pallas kernels  16.9 us (18%)
  local copies, waits for them, and re-layouts  2.89 us (3%)
    ppermute x28, starting transfers between devices, shift(): lax.ppermute(value, axis, [(i, (i + distance) % size) for i in range(size)])  40 us
    ppermute x28, waiting for transfers between devices, shift(): lax.ppermute(value, axis, [(i, (i + distance) % size) for i in range(size)])  29.5 us
    pallas_call x12, Pallas kernels, call(): pl.pallas_call(kernel, out_shape=out_shapes, in_specs=in_specs, out_specs...  16.9 us
    unnamed x12, local copies, waits for them, and re-layouts  2.88 us
  transfers between devices with their start and end apart: 28, of which 13 were waited for; matrix products, arithmetic and copies ran while one was open for 0% of the time, Pallas kernels for 10%

profile of v3, /device:TPU:24, one launch (start us, length us, event | category | flops | bytes accessed | tf_op | source)
XLA Modules:
  0.0 90.2 jit_solution(4916856262333860743)
XLA Ops:
  0.6 0.9 %copy-done = bf16[1,56,2560]{2,1,0:T(8,128)(2,1)S(1)} copy-done((bf16[1,56,2560]{2,1,0:T(8,128)(2,1)S(1)}, bf16[1,56,2560]{2,1,0:T(8,128)(2,1)}, u32[]{:S(2)}) %copy-start) | copy-done | bytes 286744
  1.6 1.0 %copy-done.1 = bf16[1,56,2560]{2,1,0:T(8,128)(2,1)S(1)} copy-done((bf16[1,56,2560]{2,1,0:T(8,128)(2,1)S(1)}, bf16[1,56,2560]{2,1,0:T(8,128)(2,1)}, u32[]{:S(2)}) %copy-start.1) | copy-done | bytes 286744
  2.6 1.0 %copy-done.2 = bf16[2,56,1280]{2,1,0:T(8,128)(2,1)S(1)} copy-done((bf16[2,56,1280]{2,1,0:T(8,128)(2,1)S(1)}, bf16[2,56,1280]{2,1,0:T(8,128)(2,1)}, u32[]{:S(2)}) %copy-start.2) | copy-done | bytes 286744
  3.5 0.1 shard_map.86
  3.6 1.3 %collective-permute-start.7 = (bf16[20,56,128]{2,1,0:T(8,128)(2,1)S(1)}, bf16[20,56,128]{2,1,0:T(8,128)(2,1)S(1)}, u32[]{:S(2)}, u32[]{:S(2)}) collective-permute-start(bf16[20,56,128]{2,1,0:T(8,128)(2,1)S(1)} %get-tuple-element.36), channel_id=1, source_target_pairs={{0,16},{1,17},{16,0},{17,1},{2,18},{3,19},{18,2},{19,3},{4,20},{5,... | collective-permute-start | bytes 860168 | tf_op jit(solution)/shard_map/ppermute | solution.py:28
  5.0 2.3 %collective-permute-start.6 = (bf16[10,56,128]{2,1,0:T(8,128)(2,1)S(1)}, bf16[10,56,128]{2,1,0:T(8,128)(2,1)S(1)}, u32[]{:S(2)}, u32[]{:S(2)}) collective-permute-start(bf16[10,56,128]{2,1,0:T(8,128)(2,1)S(1)} %get-tuple-element.35), channel_id=1, source_target_pairs={{0,1},{1,16},{16,17},{17,0},{2,3},{3,18},{18,19},{19,2},{4,5},{5,2... | collective-permute-start | bytes 430088 | tf_op jit(solution)/shard_map/ppermute | solution.py:28
  7.3 2.8 %collective-permute-start.2 = (bf16[7,56,128]{2,1,0:T(8,128)(2,1)S(1)}, bf16[7,56,128]{2,1,0:T(8,128)(2,1)S(1)}, u32[]{:S(2)}, u32[]{:S(2)}) collective-permute-start(bf16[7,56,128]{2,1,0:T(8,128)(2,1)S(1)} %get-tuple-element.33.refs_0_), channel_id=1, source_target_pairs={{0,12},{4,0},{8,4},{12,8},{1,13},{5,1},{9,5},{13,9},{2,14},{6,2},{... | collective-permute-start | bytes 301064 | tf_op jit(solution)/shard_map/ppermute | solution.py:28
  10.0 4.4 %collective-permute-done.6.first.refs_9_ = bf16[10,56,128]{2,1,0:T(8,128)(2,1)S(1)} collective-permute-done((bf16[10,56,128]{2,1,0:T(8,128)(2,1)S(1)}, bf16[10,56,128]{2,1,0:T(8,128)(2,1)S(1)}, u32[]{:S(2)}, u32[]{:S(2)}) %collective-permute-start.6) | collective-permute-done | bytes 143392 | tf_op jit(solution)/shard_map/ppermute | solution.py:28
  14.4 2.5 %collective-permute-done.8.last.refs_11_ = bf16[10,56,128]{2,1,0:T(8,128)(2,1)S(1)} collective-permute-done((bf16[10,56,128]{2,1,0:T(8,128)(2,1)S(1)}, bf16[10,56,128]{2,1,0:T(8,128)(2,1)S(1)}, u32[]{:S(2)}, u32[]{:S(2)}) %collective-permute-start.8) | collective-permute-done | bytes 143392 | tf_op jit(solution)/shard_map/ppermute | solution.py:28
  16.9 4.1 %collective-permute-start.14 = (bf16[12,56,128]{2,1,0:T(8,128)(2,1)S(1)}, bf16[12,56,128]{2,1,0:T(8,128)(2,1)S(1)}, u32[]{:S(2)}, u32[]{:S(2)}) collective-permute-start(bf16[12,56,128]{2,1,0:T(8,128)(2,1)S(1)} %get-tuple-element.39.refs_12_), channel_id=1, source_target_pairs={{0,96},{32,0},{64,32},{96,64},{1,97},{33,1},{65,33},{97,65},{2,98}... | collective-permute-start | bytes 516104 | tf_op jit(solution)/shard_map/ppermute | solution.py:28
  21.0 0.4 collective-permute-start.5
  21.4 1.6 %collective-permute-start.4 = (bf16[8,56,128]{2,1,0:T(8,128)(2,1)S(1)}, bf16[8,56,128]{2,1,0:T(8,128)(2,1)S(1)}, u32[]{:S(2)}, u32[]{:S(2)}) collective-permute-start(bf16[8,56,128]{2,1,0:T(8,128)(2,1)S(1)} %get-tuple-element.34.refs_4_), channel_id=1, source_target_pairs={{0,32},{32,64},{64,96},{96,0},{1,33},{33,65},{65,97},{97,1},{2,34}... | collective-permute-start | bytes 344072 | tf_op jit(solution)/shard_map/ppermute | solution.py:28
  23.0 3.1 %collective-permute-start = (bf16[7,56,128]{2,1,0:T(8,128)(2,1)S(1)}, bf16[7,56,128]{2,1,0:T(8,128)(2,1)S(1)}, u32[]{:S(2)}, u32[]{:S(2)}) collective-permute-start(bf16[7,56,128]{2,1,0:T(8,128)(2,1)S(1)} %get-tuple-element.33.refs_0_), channel_id=1, source_target_pairs={{0,8},{4,12},{8,0},{12,4},{1,9},{5,13},{9,1},{13,5},{2,10},{6,14},... | collective-permute-start | bytes 301064 | tf_op jit(solution)/shard_map/ppermute | solution.py:28
  26.1 3.1 %collective-permute-done.refs_1_ = bf16[7,56,128]{2,1,0:T(8,128)(2,1)S(1)} collective-permute-done((bf16[7,56,128]{2,1,0:T(8,128)(2,1)S(1)}, bf16[7,56,128]{2,1,0:T(8,128)(2,1)S(1)}, u32[]{:S(2)}, u32[]{:S(2)}) %collective-permute-start) | collective-permute-done | bytes 100384 | tf_op jit(solution)/shard_map/ppermute | solution.py:28
  29.3 2.8 %collective-permute-start.11 = (bf16[13,56,128]{2,1,0:T(8,128)(2,1)S(1)}, bf16[13,56,128]{2,1,0:T(8,128)(2,1)S(1)}, u32[]{:S(2)}, u32[]{:S(2)}) collective-permute-start(bf16[13,56,128]{2,1,0:T(8,128)(2,1)S(1)} %get-tuple-element.38.refs_8_), channel_id=1, source_target_pairs={{0,12},{4,0},{8,4},{12,8},{1,13},{5,1},{9,5},{13,9},{2,14},{6,2},{... | collective-permute-start | bytes 559112 | tf_op jit(solution)/shard_map/ppermute | solution.py:28
  32.0 2.3 %collective-permute-start.9 = (bf16[13,56,128]{2,1,0:T(8,128)(2,1)S(1)}, bf16[13,56,128]{2,1,0:T(8,128)(2,1)S(1)}, u32[]{:S(2)}, u32[]{:S(2)}) collective-permute-start(bf16[13,56,128]{2,1,0:T(8,128)(2,1)S(1)} %get-tuple-element.38.refs_8_), channel_id=1, source_target_pairs={{0,8},{4,12},{8,0},{12,4},{1,9},{5,13},{9,1},{13,5},{2,10},{6,14},... | collective-permute-start | bytes 559112 | tf_op jit(solution)/shard_map/ppermute | solution.py:28
  34.3 2.4 %collective-permute-start.13 = (bf16[12,56,128]{2,1,0:T(8,128)(2,1)S(1)}, bf16[12,56,128]{2,1,0:T(8,128)(2,1)S(1)}, u32[]{:S(2)}, u32[]{:S(2)}) collective-permute-start(bf16[12,56,128]{2,1,0:T(8,128)(2,1)S(1)} %get-tuple-element.39.refs_12_), channel_id=1, source_target_pairs={{0,32},{32,64},{64,96},{96,0},{1,33},{33,65},{65,97},{97,1},{2,34}... | collective-permute-start | bytes 516104 | tf_op jit(solution)/shard_map/ppermute | solution.py:28
  36.7 2.4 %collective-permute-start.12 = (bf16[12,56,128]{2,1,0:T(8,128)(2,1)S(1)}, bf16[12,56,128]{2,1,0:T(8,128)(2,1)S(1)}, u32[]{:S(2)}, u32[]{:S(2)}) collective-permute-start(bf16[12,56,128]{2,1,0:T(8,128)(2,1)S(1)} %get-tuple-element.39.refs_12_), channel_id=1, source_target_pairs={{0,64},{32,96},{64,0},{96,32},{1,65},{33,97},{65,1},{97,33},{2,66}... | collective-permute-start | bytes 516104 | tf_op jit(solution)/shard_map/ppermute | solution.py:28
  39.1 3.3 %collective-permute-done.13.refs_14_ = bf16[12,56,128]{2,1,0:T(8,128)(2,1)S(1)} collective-permute-done((bf16[12,56,128]{2,1,0:T(8,128)(2,1)S(1)}, bf16[12,56,128]{2,1,0:T(8,128)(2,1)S(1)}, u32[]{:S(2)}, u32[]{:S(2)}) %collective-permute-start.13) | collective-permute-done | bytes 172064 | tf_op jit(solution)/shard_map/ppermute | solution.py:28
  42.5 3.2 %collective-permute-done.12.refs_13_ = bf16[12,56,128]{2,1,0:T(8,128)(2,1)S(1)} collective-permute-done((bf16[12,56,128]{2,1,0:T(8,128)(2,1)S(1)}, bf16[12,56,128]{2,1,0:T(8,128)(2,1)S(1)}, u32[]{:S(2)}, u32[]{:S(2)}) %collective-permute-start.12) | collective-permute-done | bytes 172064 | tf_op jit(solution)/shard_map/ppermute | solution.py:28
  45.7 0.4 shard_map.89
  46.1 0.1 collective-permute-start.15
  46.2 2.8 %collective-permute-done.15.swapped = bf16[10,448,128]{2,1,0:T(8,128)(2,1)S(1)} collective-permute-done((bf16[10,448,128]{2,1,0:T(8,128)(2,1)S(1)}, bf16[10,448,128]{2,1,0:T(8,128)(2,1)S(1)}, u32[]{:S(2)}, u32[]{:S(2)}) %collective-permute-start.15) | collective-permute-done | bytes 1146912 | tf_op jit(solution)/shard_map/ppermute | solution.py:28
  49.0 3.0 %shard_map.91 = (bf16[480,128]{1,0:T(8,128)(2,1)S(1)}, bf16[480,128]{1,0:T(8,128)(2,1)S(1)}, bf16[480,128]{1,0:T(8,128)(2,1)S(1)}, bf16[480,128]{1,0:T(8,128)(2,1)S(1)}) custom-call(bf16[5,896,128]{2,1,0:T(8,128)(2,1)S(1)} %get-tuple-element.40.queries, bf16[10,448,128]{2,1,0:T(8,128)(2,1)S(1)} %get-tuple-element.41.held, ...), custom_call_target="tpu_custom_call" | custom-call | flops 822083584 | bytes 3932160 | tf_op jit(solution)/shard_map/pallas_call | solution.py:48
  52.0 1.7 %collective-permute-start.19 = (bf16[480,128]{1,0:T(8,128)(2,1)S(1)}, bf16[480,128]{1,0:T(8,128)(2,1)S(1)}, u32[]{:S(2)}, u32[]{:S(2)}) collective-permute-start(bf16[480,128]{1,0:T(8,128)(2,1)S(1)} %get-tuple-element.47), channel_id=1, source_target_pairs={{0,64},{32,96},{64,0},{96,32},{1,65},{33,97},{65,1},{97,33},{2,66}... | collective-permute-start | bytes 368648 | tf_op jit(solution)/shard_map/ppermute | solution.py:28
  53.6 4.1 %shard_map.90 = (bf16[704,128]{1,0:T(8,128)(2,1)S(1)}, bf16[704,128]{1,0:T(8,128)(2,1)S(1)}, bf16[704,128]{1,0:T(8,128)(2,1)S(1)}, bf16[704,128]{1,0:T(8,128)(2,1)S(1)}) custom-call(bf16[5,896,128]{2,1,0:T(8,128)(2,1)S(1)} %get-tuple-element.40.queries, bf16[10,448,128]{2,1,0:T(8,128)(2,1)S(1)} %get-tuple-element.41.held, ...), custom_call_target="tpu_custom_call" | custom-call | flops 1233125376 | bytes 4161536 | tf_op jit(solution)/shard_map/pallas_call | solution.py:48
  57.8 0.8 collective-permute-start.16
  58.6 2.1 %collective-permute-start.17 = (bf16[704,128]{1,0:T(8,128)(2,1)S(1)}, bf16[704,128]{1,0:T(8,128)(2,1)S(1)}, u32[]{:S(2)}, u32[]{:S(2)}) collective-permute-start(bf16[704,128]{1,0:T(8,128)(2,1)S(1)} %get-tuple-element.44), channel_id=1, source_target_pairs={{0,12},{4,0},{8,4},{12,8},{1,13},{5,1},{9,5},{13,9},{2,14},{6,2},{... | collective-permute-start | bytes 540680 | tf_op jit(solution)/shard_map/ppermute | solution.py:28
  60.7 1.9 %collective-permute-start.20 = (bf16[480,128]{1,0:T(8,128)(2,1)S(1)}, bf16[480,128]{1,0:T(8,128)(2,1)S(1)}, u32[]{:S(2)}, u32[]{:S(2)}) collective-permute-start(bf16[480,128]{1,0:T(8,128)(2,1)S(1)} %get-tuple-element.48), channel_id=1, source_target_pairs={{0,96},{32,0},{64,32},{96,64},{1,97},{33,1},{65,33},{97,65},{2,98}... | collective-permute-start | bytes 368648 | tf_op jit(solution)/shard_map/ppermute | solution.py:28
  62.6 0.2 collective-permute-start.21
  62.8 0.1 pad_add_fusion.info_ref
  62.9 2.9 %shard_map.92 = (bf16[512,640]{1,0:T(8,128)(2,1)S(1)}, f32[8,512]{1,0:T(8,128)S(1)}, bf16[2,2,512,640]{3,2,1,0:T(8,128)(2,1)S(1)}, f32[8,640]{1,0:T(8,128)S(1)}) custom-call(s32[2]{0:T(128)S(1)} %pad_add_fusion.info_ref, s32[2,512]{1,0:T(2,128)S(1)} %copy-done.3, s32[1,512]{1,0:T(1,128)S(1)} %bitcast.11, bf16[1,2560]{1,0:T(2,128)(2,1)S(1)} %reshape.15.gain_ref, ...), custom_call_target="tpu_custom_call" | custom-call | flops 335544320 | bytes 3324928 | tf_op jit(solution)/shard_map/pallas_call | solution.py:48
  65.8 2.9 %collective-permute-done.21.refs_7_ = bf16[480,128]{1,0:T(8,128)(2,1)S(1)} collective-permute-done((bf16[480,128]{1,0:T(8,128)(2,1)S(1)}, bf16[480,128]{1,0:T(8,128)(2,1)S(1)}, u32[]{:S(2)}, u32[]{:S(2)}) %collective-permute-start.21) | collective-permute-done | bytes 122912 | tf_op jit(solution)/shard_map/ppermute | solution.py:28
  68.7 0.8 collective-permute-done.18.refs_3_
  69.5 1.6 %shard_map.93 = (bf16[6,56,128]{2,1,0:T(8,128)(2,1)S(1)}, bf16[6,56,128]{2,1,0:T(8,128)(2,1)S(1)}, bf16[6,56,128]{2,1,0:T(8,128)(2,1)S(1)}, bf16[6,56,128]{2,1,0:T(8,128)(2,1)S(1)}, f32[5,4,56,128]{3,2,1,0:T(8,128)S(1)}) custom-call(bf16[704,128]{1,0:T(8,128)(2,1)S(1)} %get-tuple-element.42.refs_0_, bf16[704,128]{1,0:T(8,128)(2,1)S(1)} %collective-permute-done.16.refs_1_, ...), custom_call_target="tpu_custom_call" | custom-call | bytes 2775040 | tf_op jit(solution)/shard_map/pallas_call | solution.py:48
  71.2 1.4 %collective-permute-start.23 = (bf16[6,56,128]{2,1,0:T(8,128)(2,1)S(1)}, bf16[6,56,128]{2,1,0:T(8,128)(2,1)S(1)}, u32[]{:S(2)}, u32[]{:S(2)}) collective-permute-start(bf16[6,56,128]{2,1,0:T(8,128)(2,1)S(1)} %get-tuple-element.54), channel_id=1, source_target_pairs={{0,16},{1,17},{16,0},{17,1},{2,18},{3,19},{18,2},{19,3},{4,20},{5,... | collective-permute-start | bytes 258056 | tf_op jit(solution)/shard_map/ppermute | solution.py:28
  72.6 2.3 %collective-permute-start.24 = (bf16[6,56,128]{2,1,0:T(8,128)(2,1)S(1)}, bf16[6,56,128]{2,1,0:T(8,128)(2,1)S(1)}, u32[]{:S(2)}, u32[]{:S(2)}) collective-permute-start(bf16[6,56,128]{2,1,0:T(8,128)(2,1)S(1)} %get-tuple-element.55), channel_id=1, source_target_pairs={{0,1},{1,16},{16,17},{17,0},{2,3},{3,18},{18,19},{19,2},{4,5},{5,2... | collective-permute-start | bytes 258056 | tf_op jit(solution)/shard_map/ppermute | solution.py:28
  74.9 1.1 %shard_map.95.scores_ref = f32[2,5,112,512]{3,2,1,0:T(8,128)S(1)} custom-call(s32[2]{0:T(128)S(1)} %pad_add_fusion.info_ref, f32[5,4,56,128]{3,2,1,0:T(8,128)S(1)} %get-tuple-element.56.middle_ref, f32[8,640]{1,0:T(8,128)S(1)} %get-tuple-element.57.gain_ref, bf16[2,2,512,640]{3,2,1,0:T(8,128)(2,1)S(1)} %get-tuple-element.58.text_ref), custom_call_target="tpu_custom_call" | custom-call | flops 146800640 | bytes 5509120 | tf_op jit(solution)/shard_map/pallas_call | solution.py:48
  75.9 2.4 %collective-permute-done.22.refs_1_.s1 = bf16[6,56,128]{2,1,0:T(8,128)(2,1)S(1)} collective-permute-done((bf16[6,56,128]{2,1,0:T(8,128)(2,1)S(1)}, bf16[6,56,128]{2,1,0:T(8,128)(2,1)S(1)}, u32[]{:S(2)}, u32[]{:S(2)}) %collective-permute-start.22) | collective-permute-done | bytes 86048 | tf_op jit(solution)/shard_map/ppermute | solution.py:28
  78.3 0.6 collective-permute-done.24.refs_3_.s3
  78.9 2.1 %shard_map.96 = (bf16[5,56,128]{2,1,0:T(8,128)(2,1)S(1)}, bf16[5,56,128]{2,1,0:T(8,128)(2,1)S(1)}, bf16[5,56,128]{2,1,0:T(8,128)(2,1)S(1)}, bf16[5,56,128]{2,1,0:T(8,128)(2,1)S(1)}) custom-call(s32[2]{0:T(128)S(1)} %pad_add_fusion.info_ref, bf16[6,56,128]{2,1,0:T(8,128)(2,1)S(1)} %get-tuple-element.52.refs_0_.s0, ...), custom_call_target="tpu_custom_call" | custom-call | flops 220200960 | bytes 6791168 | tf_op jit(solution)/shard_map/pallas_call | solution.py:48
  81.0 1.0 %collective-permute-start.25 = (bf16[5,56,128]{2,1,0:T(8,128)(2,1)S(1)}, bf16[5,56,128]{2,1,0:T(8,128)(2,1)S(1)}, u32[]{:S(2)}, u32[]{:S(2)}) collective-permute-start(bf16[5,56,128]{2,1,0:T(8,128)(2,1)S(1)} %get-tuple-element.61), channel_id=1, source_target_pairs={{0,17},{1,0},{16,1},{17,16},{2,19},{3,2},{18,3},{19,18},{4,21},{5,... | collective-permute-start | bytes 215048 | tf_op jit(solution)/shard_map/ppermute | solution.py:28
  81.9 3.1 %collective-permute-start.26 = (bf16[5,56,128]{2,1,0:T(8,128)(2,1)S(1)}, bf16[5,56,128]{2,1,0:T(8,128)(2,1)S(1)}, u32[]{:S(2)}, u32[]{:S(2)}) collective-permute-start(bf16[5,56,128]{2,1,0:T(8,128)(2,1)S(1)} %get-tuple-element.62), channel_id=1, source_target_pairs={{0,16},{1,17},{16,0},{17,1},{2,18},{3,19},{18,2},{19,3},{4,20},{5,... | collective-permute-start | bytes 215048 | tf_op jit(solution)/shard_map/ppermute | solution.py:28
  85.0 0.8 shard_map.94
  85.8 0.8 collective-permute-done.25.refs_1_
  86.6 1.5 %collective-permute-done.26.refs_2_ = bf16[5,56,128]{2,1,0:T(8,128)(2,1)S(1)} collective-permute-done((bf16[5,56,128]{2,1,0:T(8,128)(2,1)S(1)}, bf16[5,56,128]{2,1,0:T(8,128)(2,1)S(1)}, u32[]{:S(2)}, u32[]{:S(2)}) %collective-permute-start.26) | collective-permute-done | bytes 71712 | tf_op jit(solution)/shard_map/ppermute | solution.py:28
  88.1 1.3 %collective-permute-done.27.refs_3_ = bf16[5,56,128]{2,1,0:T(8,128)(2,1)S(1)} collective-permute-done((bf16[5,56,128]{2,1,0:T(8,128)(2,1)S(1)}, bf16[5,56,128]{2,1,0:T(8,128)(2,1)S(1)}, u32[]{:S(2)}, u32[]{:S(2)}) %collective-permute-start.27) | collective-permute-done | bytes 71712 | tf_op jit(solution)/shard_map/ppermute | solution.py:28
  89.4 0.8 shard_map.97
  (34 shorter events, 0.2 us)
Async XLA Ops:
  0.6 1.0 %copy-start = (bf16[1,56,2560]{2,1,0:T(8,128)(2,1)S(1)}, bf16[1,56,2560]{2,1,0:T(8,128)(2,1)}, u32[]{:S(2)}) copy-start(bf16[1,56,2560]{2,1,0:T(8,128)(2,1)} %param.7) | copy-start | bytes 860164
  1.6 1.0 %copy-start.1 = (bf16[1,56,2560]{2,1,0:T(8,128)(2,1)S(1)}, bf16[1,56,2560]{2,1,0:T(8,128)(2,1)}, u32[]{:S(2)}) copy-start(bf16[1,56,2560]{2,1,0:T(8,128)(2,1)} %param.9) | copy-start | bytes 860164
  2.6 1.0 %copy-start.2 = (bf16[2,56,1280]{2,1,0:T(8,128)(2,1)S(1)}, bf16[2,56,1280]{2,1,0:T(8,128)(2,1)}, u32[]{:S(2)}) copy-start(bf16[2,56,1280]{2,1,0:T(8,128)(2,1)} %kv_ref.1) | copy-start | bytes 860164
  3.6 13.2 %collective-permute-start.7 = (bf16[20,56,128]{2,1,0:T(8,128)(2,1)S(1)}, bf16[20,56,128]{2,1,0:T(8,128)(2,1)S(1)}, u32[]{:S(2)}, u32[]{:S(2)}) collective-permute-start(bf16[20,56,128]{2,1,0:T(8,128)(2,1)S(1)} %get-tuple-element.36), channel_id=1, source_target_pairs={{0,16},{1,17},{16,0},{17,1},{2,18},{3,19},{18,2},{19,3},{4,20},{5,... | collective-permute-start | bytes 860168 | tf_op jit(solution)/shard_map/ppermute | solution.py:28
  5.0 9.4 %collective-permute-start.6 = (bf16[10,56,128]{2,1,0:T(8,128)(2,1)S(1)}, bf16[10,56,128]{2,1,0:T(8,128)(2,1)S(1)}, u32[]{:S(2)}, u32[]{:S(2)}) collective-permute-start(bf16[10,56,128]{2,1,0:T(8,128)(2,1)S(1)} %get-tuple-element.35), channel_id=1, source_target_pairs={{0,1},{1,16},{16,17},{17,0},{2,3},{3,18},{18,19},{19,2},{4,5},{5,2... | collective-permute-start | bytes 430088 | tf_op jit(solution)/shard_map/ppermute | solution.py:28
  7.3 9.6 %collective-permute-start.8 = (bf16[10,56,128]{2,1,0:T(8,128)(2,1)S(1)}, bf16[10,56,128]{2,1,0:T(8,128)(2,1)S(1)}, u32[]{:S(2)}, u32[]{:S(2)}) collective-permute-start(bf16[10,56,128]{2,1,0:T(8,128)(2,1)S(1)} %get-tuple-element.37), channel_id=1, source_target_pairs={{0,17},{1,0},{16,1},{17,16},{2,19},{3,2},{18,3},{19,18},{4,21},{5,... | collective-permute-start | bytes 430088 | tf_op jit(solution)/shard_map/ppermute | solution.py:28
  7.3 15.8 %collective-permute-start.2 = (bf16[7,56,128]{2,1,0:T(8,128)(2,1)S(1)}, bf16[7,56,128]{2,1,0:T(8,128)(2,1)S(1)}, u32[]{:S(2)}, u32[]{:S(2)}) collective-permute-start(bf16[7,56,128]{2,1,0:T(8,128)(2,1)S(1)} %get-tuple-element.33.refs_0_), channel_id=1, source_target_pairs={{0,12},{4,0},{8,4},{12,8},{1,13},{5,1},{9,5},{13,9},{2,14},{6,2},{... | collective-permute-start | bytes 301064 | tf_op jit(solution)/shard_map/ppermute | solution.py:28
  10.0 13.0 %collective-permute-start.1 = (bf16[7,56,128]{2,1,0:T(8,128)(2,1)S(1)}, bf16[7,56,128]{2,1,0:T(8,128)(2,1)S(1)}, u32[]{:S(2)}, u32[]{:S(2)}) collective-permute-start(bf16[7,56,128]{2,1,0:T(8,128)(2,1)S(1)} %get-tuple-element.33.refs_0_), channel_id=1, source_target_pairs={{0,4},{4,8},{8,12},{12,0},{1,5},{5,9},{9,13},{13,1},{2,6},{6,10},{... | collective-permute-start | bytes 301064 | tf_op jit(solution)/shard_map/ppermute | solution.py:28
  16.9 19.8 %collective-permute-start.14 = (bf16[12,56,128]{2,1,0:T(8,128)(2,1)S(1)}, bf16[12,56,128]{2,1,0:T(8,128)(2,1)S(1)}, u32[]{:S(2)}, u32[]{:S(2)}) collective-permute-start(bf16[12,56,128]{2,1,0:T(8,128)(2,1)S(1)} %get-tuple-element.39.refs_12_), channel_id=1, source_target_pairs={{0,96},{32,0},{64,32},{96,64},{1,97},{33,1},{65,33},{97,65},{2,98}... | collective-permute-start | bytes 516104 | tf_op jit(solution)/shard_map/ppermute | solution.py:28
  21.0 11.0 %collective-permute-start.5 = (bf16[8,56,128]{2,1,0:T(8,128)(2,1)S(1)}, bf16[8,56,128]{2,1,0:T(8,128)(2,1)S(1)}, u32[]{:S(2)}, u32[]{:S(2)}) collective-permute-start(bf16[8,56,128]{2,1,0:T(8,128)(2,1)S(1)} %get-tuple-element.34.refs_4_), channel_id=1, source_target_pairs={{0,96},{32,0},{64,32},{96,64},{1,97},{33,1},{65,33},{97,65},{2,98}... | collective-permute-start | bytes 344072 | tf_op jit(solution)/shard_map/ppermute | solution.py:28
  21.4 10.6 %collective-permute-start.4 = (bf16[8,56,128]{2,1,0:T(8,128)(2,1)S(1)}, bf16[8,56,128]{2,1,0:T(8,128)(2,1)S(1)}, u32[]{:S(2)}, u32[]{:S(2)}) collective-permute-start(bf16[8,56,128]{2,1,0:T(8,128)(2,1)S(1)} %get-tuple-element.34.refs_4_), channel_id=1, source_target_pairs={{0,32},{32,64},{64,96},{96,0},{1,33},{33,65},{65,97},{97,1},{2,34}... | collective-permute-start | bytes 344072 | tf_op jit(solution)/shard_map/ppermute | solution.py:28
  23.0 11.3 %collective-permute-start.3 = (bf16[8,56,128]{2,1,0:T(8,128)(2,1)S(1)}, bf16[8,56,128]{2,1,0:T(8,128)(2,1)S(1)}, u32[]{:S(2)}, u32[]{:S(2)}) collective-permute-start(bf16[8,56,128]{2,1,0:T(8,128)(2,1)S(1)} %get-tuple-element.34.refs_4_), channel_id=1, source_target_pairs={{0,64},{32,96},{64,0},{96,32},{1,65},{33,97},{65,1},{97,33},{2,66}... | collective-permute-start | bytes 344072 | tf_op jit(solution)/shard_map/ppermute | solution.py:28
  23.0 6.2 %collective-permute-start = (bf16[7,56,128]{2,1,0:T(8,128)(2,1)S(1)}, bf16[7,56,128]{2,1,0:T(8,128)(2,1)S(1)}, u32[]{:S(2)}, u32[]{:S(2)}) collective-permute-start(bf16[7,56,128]{2,1,0:T(8,128)(2,1)S(1)} %get-tuple-element.33.refs_0_), channel_id=1, source_target_pairs={{0,8},{4,12},{8,0},{12,4},{1,9},{5,13},{9,1},{13,5},{2,10},{6,14},... | collective-permute-start | bytes 301064 | tf_op jit(solution)/shard_map/ppermute | solution.py:28
  29.3 16.4 %collective-permute-start.11 = (bf16[13,56,128]{2,1,0:T(8,128)(2,1)S(1)}, bf16[13,56,128]{2,1,0:T(8,128)(2,1)S(1)}, u32[]{:S(2)}, u32[]{:S(2)}) collective-permute-start(bf16[13,56,128]{2,1,0:T(8,128)(2,1)S(1)} %get-tuple-element.38.refs_8_), channel_id=1, source_target_pairs={{0,12},{4,0},{8,4},{12,8},{1,13},{5,1},{9,5},{13,9},{2,14},{6,2},{... | collective-permute-start | bytes 559112 | tf_op jit(solution)/shard_map/ppermute | solution.py:28
  32.0 13.6 %collective-permute-start.10 = (bf16[13,56,128]{2,1,0:T(8,128)(2,1)S(1)}, bf16[13,56,128]{2,1,0:T(8,128)(2,1)S(1)}, u32[]{:S(2)}, u32[]{:S(2)}) collective-permute-start(bf16[13,56,128]{2,1,0:T(8,128)(2,1)S(1)} %get-tuple-element.38.refs_8_), channel_id=1, source_target_pairs={{0,4},{4,8},{8,12},{12,0},{1,5},{5,9},{9,13},{13,1},{2,6},{6,10},{... | collective-permute-start | bytes 559112 | tf_op jit(solution)/shard_map/ppermute | solution.py:28
  32.0 13.6 %collective-permute-start.9 = (bf16[13,56,128]{2,1,0:T(8,128)(2,1)S(1)}, bf16[13,56,128]{2,1,0:T(8,128)(2,1)S(1)}, u32[]{:S(2)}, u32[]{:S(2)}) collective-permute-start(bf16[13,56,128]{2,1,0:T(8,128)(2,1)S(1)} %get-tuple-element.38.refs_8_), channel_id=1, source_target_pairs={{0,8},{4,12},{8,0},{12,4},{1,9},{5,13},{9,1},{13,5},{2,10},{6,14},... | collective-permute-start | bytes 559112 | tf_op jit(solution)/shard_map/ppermute | solution.py:28
  34.3 8.1 %collective-permute-start.13 = (bf16[12,56,128]{2,1,0:T(8,128)(2,1)S(1)}, bf16[12,56,128]{2,1,0:T(8,128)(2,1)S(1)}, u32[]{:S(2)}, u32[]{:S(2)}) collective-permute-start(bf16[12,56,128]{2,1,0:T(8,128)(2,1)S(1)} %get-tuple-element.39.refs_12_), channel_id=1, source_target_pairs={{0,32},{32,64},{64,96},{96,0},{1,33},{33,65},{65,97},{97,1},{2,34}... | collective-permute-start | bytes 516104 | tf_op jit(solution)/shard_map/ppermute | solution.py:28
  36.7 8.9 %collective-permute-start.12 = (bf16[12,56,128]{2,1,0:T(8,128)(2,1)S(1)}, bf16[12,56,128]{2,1,0:T(8,128)(2,1)S(1)}, u32[]{:S(2)}, u32[]{:S(2)}) collective-permute-start(bf16[12,56,128]{2,1,0:T(8,128)(2,1)S(1)} %get-tuple-element.39.refs_12_), channel_id=1, source_target_pairs={{0,64},{32,96},{64,0},{96,32},{1,65},{33,97},{65,1},{97,33},{2,66}... | collective-permute-start | bytes 516104 | tf_op jit(solution)/shard_map/ppermute | solution.py:28
  46.1 2.9 %collective-permute-start.15 = (bf16[10,448,128]{2,1,0:T(8,128)(2,1)S(1)}, bf16[10,448,128]{2,1,0:T(8,128)(2,1)S(1)}, u32[]{:S(2)}, u32[]{:S(2)}) collective-permute-start(bf16[10,448,128]{2,1,0:T(8,128)(2,1)S(1)} %get-tuple-element.41.held), channel_id=1, source_target_pairs={{0,2},{2,0},{1,3},{3,1},{4,6},{6,4},{5,7},{7,5},{8,10},{10,8},{9,1... | collective-permute-start | bytes 3440648 | tf_op jit(solution)/shard_map/ppermute | solution.py:28
  51.9 8.8 %copy-start.5 = (bf16[2560]{0:T(1024)(128)(2,1)S(1)}, bf16[2560]{0:T(1024)(128)(2,1)}, u32[]{:S(2)}) copy-start(bf16[2560]{0:T(1024)(128)(2,1)} %param.10) | copy-start | bytes 15364
  52.0 10.9 %copy-start.3 = (s32[2,512]{1,0:T(2,128)S(1)}, s32[2,512]{1,0:T(2,128)}, u32[]{:S(2)}) copy-start(s32[2,512]{1,0:T(2,128)} %ids_ref.1) | copy-start | bytes 12292
  52.0 10.9 %copy-start.4 = (s32[512]{0:T(512)S(1)}, s32[512]{0:T(512)}, u32[]{:S(2)}) copy-start(s32[512]{0:T(512)} %param.13) | copy-start | bytes 6148
  52.0 10.7 %collective-permute-start.19 = (bf16[480,128]{1,0:T(8,128)(2,1)S(1)}, bf16[480,128]{1,0:T(8,128)(2,1)S(1)}, u32[]{:S(2)}, u32[]{:S(2)}) collective-permute-start(bf16[480,128]{1,0:T(8,128)(2,1)S(1)} %get-tuple-element.47), channel_id=1, source_target_pairs={{0,64},{32,96},{64,0},{96,32},{1,65},{33,97},{65,1},{97,33},{2,66}... | collective-permute-start | bytes 368648 | tf_op jit(solution)/shard_map/ppermute | solution.py:28
  57.8 11.0 %collective-permute-start.16 = (bf16[704,128]{1,0:T(8,128)(2,1)S(1)}, bf16[704,128]{1,0:T(8,128)(2,1)S(1)}, u32[]{:S(2)}, u32[]{:S(2)}) collective-permute-start(bf16[704,128]{1,0:T(8,128)(2,1)S(1)} %get-tuple-element.43), channel_id=1, source_target_pairs={{0,8},{4,12},{8,0},{12,4},{1,9},{5,13},{9,1},{13,5},{2,10},{6,14},... | collective-permute-start | bytes 540680 | tf_op jit(solution)/shard_map/ppermute | solution.py:28
  58.6 10.1 %collective-permute-start.17 = (bf16[704,128]{1,0:T(8,128)(2,1)S(1)}, bf16[704,128]{1,0:T(8,128)(2,1)S(1)}, u32[]{:S(2)}, u32[]{:S(2)}) collective-permute-start(bf16[704,128]{1,0:T(8,128)(2,1)S(1)} %get-tuple-element.44), channel_id=1, source_target_pairs={{0,12},{4,0},{8,4},{12,8},{1,13},{5,1},{9,5},{13,9},{2,14},{6,2},{... | collective-permute-start | bytes 540680 | tf_op jit(solution)/shard_map/ppermute | solution.py:28
  60.7 8.8 %collective-permute-start.18 = (bf16[704,128]{1,0:T(8,128)(2,1)S(1)}, bf16[704,128]{1,0:T(8,128)(2,1)S(1)}, u32[]{:S(2)}, u32[]{:S(2)}) collective-permute-start(bf16[704,128]{1,0:T(8,128)(2,1)S(1)} %get-tuple-element.45), channel_id=1, source_target_pairs={{0,4},{4,8},{8,12},{12,0},{1,5},{5,9},{9,13},{13,1},{2,6},{6,10},{... | collective-permute-start | bytes 540680 | tf_op jit(solution)/shard_map/ppermute | solution.py:28
  60.7 5.1 %collective-permute-start.20 = (bf16[480,128]{1,0:T(8,128)(2,1)S(1)}, bf16[480,128]{1,0:T(8,128)(2,1)S(1)}, u32[]{:S(2)}, u32[]{:S(2)}) collective-permute-start(bf16[480,128]{1,0:T(8,128)(2,1)S(1)} %get-tuple-element.48), channel_id=1, source_target_pairs={{0,96},{32,0},{64,32},{96,64},{1,97},{33,1},{65,33},{97,65},{2,98}... | collective-permute-start | bytes 368648 | tf_op jit(solution)/shard_map/ppermute | solution.py:28
  62.6 6.1 %collective-permute-start.21 = (bf16[480,128]{1,0:T(8,128)(2,1)S(1)}, bf16[480,128]{1,0:T(8,128)(2,1)S(1)}, u32[]{:S(2)}, u32[]{:S(2)}) collective-permute-start(bf16[480,128]{1,0:T(8,128)(2,1)S(1)} %get-tuple-element.49), channel_id=1, source_target_pairs={{0,32},{32,64},{64,96},{96,0},{1,33},{33,65},{65,97},{97,1},{2,34}... | collective-permute-start | bytes 368648 | tf_op jit(solution)/shard_map/ppermute | solution.py:28
  71.1 7.2 %collective-permute-start.22 = (bf16[6,56,128]{2,1,0:T(8,128)(2,1)S(1)}, bf16[6,56,128]{2,1,0:T(8,128)(2,1)S(1)}, u32[]{:S(2)}, u32[]{:S(2)}) collective-permute-start(bf16[6,56,128]{2,1,0:T(8,128)(2,1)S(1)} %get-tuple-element.53), channel_id=1, source_target_pairs={{0,17},{1,0},{16,1},{17,16},{2,19},{3,2},{18,3},{19,18},{4,21},{5,... | collective-permute-start | bytes 258056 | tf_op jit(solution)/shard_map/ppermute | solution.py:28
  71.2 7.1 %collective-permute-start.23 = (bf16[6,56,128]{2,1,0:T(8,128)(2,1)S(1)}, bf16[6,56,128]{2,1,0:T(8,128)(2,1)S(1)}, u32[]{:S(2)}, u32[]{:S(2)}) collective-permute-start(bf16[6,56,128]{2,1,0:T(8,128)(2,1)S(1)} %get-tuple-element.54), channel_id=1, source_target_pairs={{0,16},{1,17},{16,0},{17,1},{2,18},{3,19},{18,2},{19,3},{4,20},{5,... | collective-permute-start | bytes 258056 | tf_op jit(solution)/shard_map/ppermute | solution.py:28
  72.6 6.3 %collective-permute-start.24 = (bf16[6,56,128]{2,1,0:T(8,128)(2,1)S(1)}, bf16[6,56,128]{2,1,0:T(8,128)(2,1)S(1)}, u32[]{:S(2)}, u32[]{:S(2)}) collective-permute-start(bf16[6,56,128]{2,1,0:T(8,128)(2,1)S(1)} %get-tuple-element.55), channel_id=1, source_target_pairs={{0,1},{1,16},{16,17},{17,0},{2,3},{3,18},{18,19},{19,2},{4,5},{5,2... | collective-permute-start | bytes 258056 | tf_op jit(solution)/shard_map/ppermute | solution.py:28
  81.0 5.6 %collective-permute-start.25 = (bf16[5,56,128]{2,1,0:T(8,128)(2,1)S(1)}, bf16[5,56,128]{2,1,0:T(8,128)(2,1)S(1)}, u32[]{:S(2)}, u32[]{:S(2)}) collective-permute-start(bf16[5,56,128]{2,1,0:T(8,128)(2,1)S(1)} %get-tuple-element.61), channel_id=1, source_target_pairs={{0,17},{1,0},{16,1},{17,16},{2,19},{3,2},{18,3},{19,18},{4,21},{5,... | collective-permute-start | bytes 215048 | tf_op jit(solution)/shard_map/ppermute | solution.py:28
  81.9 6.2 %collective-permute-start.26 = (bf16[5,56,128]{2,1,0:T(8,128)(2,1)S(1)}, bf16[5,56,128]{2,1,0:T(8,128)(2,1)S(1)}, u32[]{:S(2)}, u32[]{:S(2)}) collective-permute-start(bf16[5,56,128]{2,1,0:T(8,128)(2,1)S(1)} %get-tuple-element.62), channel_id=1, source_target_pairs={{0,16},{1,17},{16,0},{17,1},{2,18},{3,19},{18,2},{19,3},{4,20},{5,... | collective-permute-start | bytes 215048 | tf_op jit(solution)/shard_map/ppermute | solution.py:28
  85.0 4.3 %collective-permute-start.27 = (bf16[5,56,128]{2,1,0:T(8,128)(2,1)S(1)}, bf16[5,56,128]{2,1,0:T(8,128)(2,1)S(1)}, u32[]{:S(2)}, u32[]{:S(2)}) collective-permute-start(bf16[5,56,128]{2,1,0:T(8,128)(2,1)S(1)} %get-tuple-element.63), channel_id=1, source_target_pairs={{0,1},{1,16},{16,17},{17,0},{2,3},{3,18},{18,19},{19,2},{4,5},{5,2... | collective-permute-start | bytes 215048 | tf_op jit(solution)/shard_map/ppermute | solution.py:28
